TPU v7x, 32 devices: a whole 2x2x4 slice. The times are simulated.
32 devices in a mesh: dp: 8 (over z, y), mp: 4 (over x, core).
Axes of the slice: x: 2, y: 2, z: 4, core: 2. Of those that a mesh axis runs over, the one named last changes fastest.
Arguments:
- input_stream: bfloat16 [3, 4096, 768], P(None, 'dp'), may hold values from -6 to 6
- teacher: bfloat16 [3, 4096, 768], P(None, 'dp', 'mp'), may hold values from -6 to 6
- timestep: int32 [24], replicated, may hold values from 0 to 999
- lengths: int32 [24], replicated, may hold values from 1 to 512, 9216 in all
- block_perm: int32 [3, 64], replicated, may hold values from 0 to 63, as said below
- table: bfloat16 [1000, 768], P(None, ('dp', 'mp')), may hold values from -3 to 3
- norm_gains: bfloat16 [2, 768], P(None, ('dp', 'mp')), may hold values from 0.5 to 1.5
- shifts: bfloat16 [4, 768], P(None, ('dp', 'mp')), may hold values from -1.796875 to 1.796875
- w_qkv: bfloat16 [768, 2304], P('dp', 'mp'), may hold values from -0.21875 to 0.21875
- qv_bias: bfloat16 [2, 12, 64], P(None, 'mp', 'dp'), may hold values from -1.796875 to 1.796875
- w_out: bfloat16 [768, 768], P('mp', 'dp'), may hold values from -3.5 to 3.5
- w_in: bfloat16 [768, 3072], P('dp', 'mp'), may hold values from -0.21875 to 0.21875
- in_bias: bfloat16 [24, 128], P('mp', 'dp'), may hold values from -1.796875 to 1.796875
- w_back: bfloat16 [3072, 768], P('mp', 'dp'), may hold values from -0.109375 to 0.109375
Outputs:
- y_out: bfloat16 [3, 4096, 768], P(None, 'dp', 'mp')
- loss: float32 [], replicated
- grad_x: bfloat16 [3, 4096, 768], P(None, 'dp', 'mp')
- grad_table: float32 [1000, 768], P(None, ('dp', 'mp'))
- grad_norm_gains: float32 [2, 768], P(None, ('dp', 'mp'))
- grad_shifts: float32 [4, 768], P(None, ('dp', 'mp'))
- grad_qkv: float32 [768, 2304], P('dp', 'mp')
- grad_qv_bias: float32 [2, 12, 64], P(None, 'mp', 'dp')
- grad_out: float32 [768, 768], P('mp', 'dp')
- grad_in: float32 [768, 3072], P('dp', 'mp')
- grad_in_bias: float32 [24, 128], P('mp', 'dp')
- grad_back: float32 [3072, 768], P('mp', 'dp')
Inputs may be any that keep to these rules, and one draw needn't show every extreme that they name: Each row block_perm[m] is a permutation of the 64 blocks; with loader block b = s * 8 + k lying on device s, each sequence slot d receives exactly one of its 8 blocks from each loader device s. The lengths sum to 9216 and at least one sequence is full.
All inputs are finite; a program needn't handle non-finite values.
Results may differ from a plain program's by a relative error of at most 0.0055.
The roundings to bfloat16 on the way count: a program that leaves them out, or rounds other values in their place, can miss the bound.
Values may be sent and summed in bfloat16 or wider, within the bound.
A program may use at most 128 MiB of HBM per device.

v0:
```python
import functools
import math

import jax
import jax.numpy as jnp
from jax import lax
from jax.sharding import PartitionSpec as P

H = 12
DH = 64


epsilon = 1e-05


def normalize_rows(stream):
    centered = stream - jnp.mean(stream, axis=-1, keepdims=True)
    inverse = lax.rsqrt(jnp.mean(centered * centered, axis=-1, keepdims=True) + epsilon)
    return (centered * inverse, inverse)


def column_part(array, start, width):
    return lax.dynamic_slice_in_dim(array, start, width, array.ndim - 1)


def fetch_weights(w_qkv, w_in, w_out, w_back, qv_bias, in_bias):
    return (
        lax.all_gather(w_qkv, "dp", axis=0, tiled=True),
        lax.all_gather(w_in, "dp", axis=0, tiled=True),
        lax.all_gather(w_out, "dp", axis=1, tiled=True),
        lax.all_gather(w_back, "dp", axis=1, tiled=True),
        lax.all_gather(qv_bias, "dp", axis=2, tiled=True),
        lax.all_gather(in_bias, "dp", axis=1, tiled=True),
    )


def invert_map(targets, size):
    ranks = jnp.arange(size, dtype=jnp.int32)
    return jnp.sum(jnp.where(targets[None, :] == ranks[:, None], ranks[None, :], 0), axis=1)


def masked_scores(queries, keys_all, is_live, score_scale):
    scores = (
        jnp.einsum("qhe,khe->hqk", queries, keys_all, preferred_element_type=jnp.float32)
        * score_scale
    )
    return jnp.where(is_live[None, None, :], scores, -1e30)


def attend_rows(keys_all, values, is_live, score_scale, queries):
    scores = masked_scores(queries, keys_all, is_live, score_scale)
    row_top = jnp.max(scores, axis=-1, keepdims=True)
    exponent = jnp.exp(scores - row_top)
    row_total = jnp.sum(exponent, axis=-1, keepdims=True)
    weights_p = (exponent / row_total).astype(jnp.bfloat16)
    mixed = jnp.einsum("hqk,khe->qhe", weights_p, values, preferred_element_type=jnp.float32)
    return (mixed, (row_top + jnp.log(row_total))[..., 0])


def attend_back(keys_all, values, is_live, score_scale, carry, inputs):
    queries, grad_rows, log_total = inputs
    grad_keys, grad_values = carry
    scores = masked_scores(queries, keys_all, is_live, score_scale)
    probabilities = jnp.exp(scores - log_total[..., None])
    grad_probs = jnp.einsum("qhe,khe->hqk", grad_rows, values, preferred_element_type=jnp.float32)
    row_delta = jnp.sum(probabilities * grad_probs, axis=-1, keepdims=True)
    grad_scores = (probabilities * (grad_probs - row_delta)).astype(jnp.bfloat16)
    grad_queries = (
        jnp.einsum("hqk,khe->qhe", grad_scores, keys_all, preferred_element_type=jnp.float32)
        * score_scale
    )
    grad_keys = (
        grad_keys
        + jnp.einsum("hqk,qhe->khe", grad_scores, queries, preferred_element_type=jnp.float32)
        * score_scale
    )
    grad_values = grad_values + jnp.einsum(
        "hqk,qhe->khe",
        probabilities.astype(jnp.bfloat16),
        grad_rows,
        preferred_element_type=jnp.float32,
    )
    return ((grad_keys, grad_values), grad_queries)


def norm_sums(partial_value, normed, gain_full, mp_count):
    weighted = partial_value * gain_full
    sums = jnp.stack([jnp.sum(weighted, axis=1), jnp.sum(weighted * normed, axis=1)], axis=1)
    return jnp.tile(sums, (1, mp_count))


def norm_input_grad(grad_part, gain_part, normed_part, inverse, sums, width):
    scaled = grad_part * gain_part
    return inverse * (scaled - sums[:, 0:1] / width - normed_part * sums[:, 1:2] / width)


def per_device(
    input_stream,
    teacher,
    timestep,
    lengths,
    block_perm,
    table,
    norm_gains,
    shifts,
    w_qkv,
    qv_bias,
    w_out,
    w_in,
    in_bias,
    w_back,
):
    dp_count = lax.axis_size("dp")
    mp_count = lax.axis_size("mp")
    dp_rank = lax.axis_index("dp")
    mp_rank = lax.axis_index("mp")
    micro_count, seq_len, width = input_stream.shape
    part_width = teacher.shape[2]
    block_rows = seq_len // dp_count
    heads_here = H // mp_count
    score_scale = 1.0 / math.sqrt(DH)
    col_start = mp_rank * part_width
    row_block = min(512, seq_len)
    block_count = seq_len // row_block
    valid_count = jnp.sum(lengths).astype(jnp.float32)
    loss_factor = micro_count * dp_count * seq_len / valid_count
    chosen = jnp.take(table, timestep, axis=0)
    gains_full, shifts_full, table_rows = (
        lax.all_gather(norm_gains, ("dp", "mp"), axis=1, tiled=True),
        lax.all_gather(shifts, ("dp", "mp"), axis=1, tiled=True),
        lax.all_gather(chosen, ("dp", "mp"), axis=1, tiled=True),
    )
    gains_full = gains_full.astype(jnp.float32)
    shifts_full = shifts_full.astype(jnp.float32)
    gain_parts = column_part(gains_full, col_start, part_width)
    acc_qkv = jnp.zeros((width, heads_here * 3 * DH), jnp.float32)
    acc_in = jnp.zeros((width, w_in.shape[1]), jnp.float32)
    acc_out = jnp.zeros((heads_here * DH, width), jnp.float32)
    acc_back = jnp.zeros((w_back.shape[0], width), jnp.float32)
    acc_qv = jnp.zeros((2, heads_here, DH), jnp.float32)
    acc_in_bias = jnp.zeros((w_in.shape[1],), jnp.float32)
    acc_gains = jnp.zeros((2, part_width), jnp.float32)
    acc_shifts = jnp.zeros((4, part_width), jnp.float32)
    loss_part = jnp.zeros((), jnp.float32)
    table_sums = []
    outs_y = []
    outs_grad = []
    for micro_index in range(micro_count):
        forward_set = fetch_weights(w_qkv, w_in, w_out, w_back, qv_bias, in_bias)
        proj_qkv, proj_in, proj_out, proj_back, bias_qv, bias_in = forward_set
        bias_qv = bias_qv.astype(jnp.float32)
        bias_in = bias_in.reshape(-1).astype(jnp.float32)
        block_order = block_perm[micro_index].reshape(dp_count, dp_count)
        source = block_order // dp_count
        local_index = block_order % dp_count
        send_index = jnp.sum(jnp.where(source == dp_rank, local_index, 0), axis=1)
        x_blocks = input_stream[micro_index].reshape(dp_count, block_rows, width)
        t_blocks = teacher[micro_index].reshape(dp_count, block_rows, part_width)
        got_x, got_t = (
            lax.all_to_all(
                jnp.take(x_blocks, send_index, axis=0),
                "dp",
                split_axis=0,
                concat_axis=0,
                tiled=True,
            ),
            lax.all_to_all(
                jnp.take(t_blocks, send_index, axis=0),
                "dp",
                split_axis=0,
                concat_axis=0,
                tiled=True,
            ),
        )
        my_source = lax.dynamic_index_in_dim(source, dp_rank, 0, keepdims=False)
        tokens = jnp.take(got_x, my_source, axis=0).reshape(seq_len, width).astype(jnp.float32)
        target = jnp.take(got_t, my_source, axis=0).reshape(seq_len, part_width).astype(jnp.float32)
        seq_index = micro_index * dp_count + dp_rank
        length = lax.dynamic_index_in_dim(lengths, seq_index, 0, keepdims=False)
        table_row = lax.dynamic_index_in_dim(table_rows, seq_index, 0, keepdims=False).astype(
            jnp.float32
        )
        is_live = jnp.arange(seq_len, dtype=jnp.int32) < length
        stream_in = tokens + table_row[None, :]
        normed1, inverse1 = normalize_rows(stream_in)
        normed_in = (normed1 * gains_full[0] + shifts_full[0]).astype(jnp.bfloat16)
        projected = jnp.dot(normed_in, proj_qkv, preferred_element_type=jnp.float32).reshape(
            seq_len, heads_here, 3, DH
        )
        queries = (projected[:, :, 0] + bias_qv[0]).astype(jnp.bfloat16)
        keys_all = projected[:, :, 1].astype(jnp.bfloat16)
        values = (projected[:, :, 2] + bias_qv[1]).astype(jnp.bfloat16)
        query_blocks = queries.reshape(block_count, row_block, heads_here, DH)
        mixed, log_total = lax.map(
            functools.partial(attend_rows, keys_all, values, is_live, score_scale), query_blocks
        )
        attended = mixed.reshape(seq_len, heads_here * DH).astype(jnp.bfloat16)
        attn_part = jnp.dot(attended, proj_out, preferred_element_type=jnp.float32)
        branch_attn = lax.psum_scatter(
            attn_part, "mp", scatter_dimension=1, tiled=True
        ) + column_part(shifts_full[2], col_start, part_width)
        mid_part = column_part(stream_in, col_start, part_width) + branch_attn
        stream_mid = lax.all_gather(mid_part, "mp", axis=1, tiled=True)
        normed2, inverse2 = normalize_rows(stream_mid)
        normed_mid = (normed2 * gains_full[1] + shifts_full[1]).astype(jnp.bfloat16)
        pre_act = jnp.dot(normed_mid, proj_in, preferred_element_type=jnp.float32) + bias_in
        activation = jax.nn.gelu(pre_act, approximate=True).astype(jnp.bfloat16)
        mlp_part = jnp.dot(activation, proj_back, preferred_element_type=jnp.float32)
        mlp_out = lax.psum_scatter(mlp_part, "mp", scatter_dimension=1, tiled=True) + column_part(
            shifts_full[3], col_start, part_width
        )
        out_part = mid_part + mlp_out
        residual_err = jnp.where(is_live[:, None], out_part - target, 0.0)
        loss_part = loss_part + jnp.sum(residual_err * residual_err)
        grad_y = residual_err * loss_factor
        grad_mlp = grad_y.astype(jnp.bfloat16)
        acc_shifts = acc_shifts.at[3].add(jnp.sum(grad_mlp.astype(jnp.float32), axis=0))
        grad_mlp_full = lax.all_gather(grad_mlp, "mp", axis=1, tiled=True)
        back_set = fetch_weights(w_qkv, w_in, w_out, w_back, qv_bias, in_bias)
        back_qkv, back_in, back_out, back_back = (
            back_set[0],
            back_set[1],
            back_set[2],
            back_set[3],
        )
        acc_back = acc_back + jnp.einsum(
            "tf,td->fd", activation, grad_mlp_full, preferred_element_type=jnp.float32
        )
        grad_act = jnp.einsum(
            "td,fd->tf", grad_mlp_full, back_back, preferred_element_type=jnp.float32
        )
        gelu_value, gelu_pull = jax.vjp(lambda inner: jax.nn.gelu(inner, approximate=True), pre_act)
        grad_pre = gelu_pull(grad_act)[0].astype(jnp.bfloat16)
        acc_in_bias = acc_in_bias + jnp.sum(grad_pre.astype(jnp.float32), axis=0)
        acc_in = acc_in + jnp.einsum(
            "td,tf->df", normed_mid, grad_pre, preferred_element_type=jnp.float32
        )
        partial2 = jnp.einsum("tf,df->td", grad_pre, back_in, preferred_element_type=jnp.float32)
        grad_h2, sums2 = (
            lax.psum_scatter(partial2, "mp", scatter_dimension=1, tiled=True),
            lax.psum_scatter(
                norm_sums(partial2, normed2, gains_full[1], mp_count),
                "mp",
                scatter_dimension=1,
                tiled=True,
            ),
        )
        normed2_part = column_part(normed2, col_start, part_width)
        acc_gains = acc_gains.at[1].add(jnp.sum(grad_h2 * normed2_part, axis=0))
        acc_shifts = acc_shifts.at[1].add(jnp.sum(grad_h2, axis=0))
        grad_mid = grad_y + norm_input_grad(
            grad_h2, gain_parts[1], normed2_part, inverse2, sums2, width
        )
        grad_branch = grad_mid.astype(jnp.bfloat16)
        acc_shifts = acc_shifts.at[2].add(jnp.sum(grad_branch.astype(jnp.float32), axis=0))
        grad_branch_full = lax.all_gather(grad_branch, "mp", axis=1, tiled=True)
        acc_out = acc_out + jnp.einsum(
            "tc,td->cd", attended, grad_branch_full, preferred_element_type=jnp.float32
        )
        grad_att = jnp.einsum(
            "td,cd->tc", grad_branch_full, back_out, preferred_element_type=jnp.float32
        ).astype(jnp.bfloat16)
        grad_blocks = grad_att.reshape(block_count, row_block, heads_here, DH)
        zero_heads = jnp.zeros((seq_len, heads_here, DH), jnp.float32)
        (grad_keys, grad_values), grad_queries = lax.scan(
            functools.partial(attend_back, keys_all, values, is_live, score_scale),
            (zero_heads, zero_heads),
            (query_blocks, grad_blocks, log_total),
        )
        grad_queries = grad_queries.reshape(seq_len, heads_here, DH).astype(jnp.bfloat16)
        grad_keys = grad_keys.astype(jnp.bfloat16)
        grad_values = grad_values.astype(jnp.bfloat16)
        acc_qv = acc_qv + jnp.stack(
            [
                jnp.sum(grad_queries.astype(jnp.float32), axis=0),
                jnp.sum(grad_values.astype(jnp.float32), axis=0),
            ]
        )
        grad_qkv_rows = jnp.stack([grad_queries, grad_keys, grad_values], axis=2).reshape(
            seq_len, heads_here * 3 * DH
        )
        acc_qkv = acc_qkv + jnp.einsum(
            "td,tc->dc", normed_in, grad_qkv_rows, preferred_element_type=jnp.float32
        )
        partial1 = jnp.einsum(
            "tc,dc->td", grad_qkv_rows, back_qkv, preferred_element_type=jnp.float32
        )
        grad_h1, sums1 = (
            lax.psum_scatter(partial1, "mp", scatter_dimension=1, tiled=True),
            lax.psum_scatter(
                norm_sums(partial1, normed1, gains_full[0], mp_count),
                "mp",
                scatter_dimension=1,
                tiled=True,
            ),
        )
        normed1_part = column_part(normed1, col_start, part_width)
        acc_gains = acc_gains.at[0].add(jnp.sum(grad_h1 * normed1_part, axis=0))
        acc_shifts = acc_shifts.at[0].add(jnp.sum(grad_h1, axis=0))
        grad_in_stream = grad_mid + norm_input_grad(
            grad_h1, gain_parts[0], normed1_part, inverse1, sums1, width
        )
        table_sums.append(jnp.sum(grad_in_stream, axis=0))
        back_order = invert_map(my_source, dp_count)
        out_blocks = jnp.take(
            out_part.astype(jnp.bfloat16).reshape(dp_count, block_rows, part_width),
            back_order,
            axis=0,
        )
        grad_send = jnp.take(
            grad_in_stream.astype(jnp.bfloat16).reshape(dp_count, block_rows, part_width),
            back_order,
            axis=0,
        )
        home_out, home_grad = (
            lax.all_to_all(out_blocks, "dp", split_axis=0, concat_axis=0, tiled=True),
            lax.all_to_all(grad_send, "dp", split_axis=0, concat_axis=0, tiled=True),
        )
        home_place = invert_map(send_index, dp_count)
        outs_y.append(jnp.take(home_out, home_place, axis=0).reshape(seq_len, part_width))
        outs_grad.append(jnp.take(home_grad, home_place, axis=0).reshape(seq_len, part_width))
    row_sums = jnp.zeros((micro_count, width), jnp.float32)
    row_sums = lax.dynamic_update_slice_in_dim(row_sums, jnp.stack(table_sums), col_start, 1)
    my_steps = jnp.take(timestep, jnp.arange(micro_count, dtype=jnp.int32) * dp_count + dp_rank)
    step_onehot = (
        jnp.arange(table.shape[0], dtype=jnp.int32)[:, None] == my_steps[None, :]
    ).astype(jnp.float32)
    table_grad = jnp.dot(
        step_onehot, row_sums, precision=lax.Precision.HIGHEST, preferred_element_type=jnp.float32
    )
    gains_grad = lax.dynamic_update_slice_in_dim(
        jnp.zeros((2, width), jnp.float32), acc_gains, col_start, 1
    )
    shifts_grad = lax.dynamic_update_slice_in_dim(
        jnp.zeros((4, width), jnp.float32), acc_shifts, col_start, 1
    )
    loss_row = jnp.full((1, dp_count * mp_count), loss_part, jnp.float32)
    grad_table, grad_norm_gains, grad_shifts, loss_cell = (
        lax.psum_scatter(table_grad, ("dp", "mp"), scatter_dimension=1, tiled=True),
        lax.psum_scatter(gains_grad, ("dp", "mp"), scatter_dimension=1, tiled=True),
        lax.psum_scatter(shifts_grad, ("dp", "mp"), scatter_dimension=1, tiled=True),
        lax.psum_scatter(loss_row, ("dp", "mp"), scatter_dimension=1, tiled=True),
    )
    loss = loss_cell[0, 0] / (valid_count * width)
    grad_qkv, grad_in, grad_out, grad_back, grad_qv_bias, grad_in_bias = (
        lax.psum_scatter(acc_qkv, "dp", scatter_dimension=0, tiled=True),
        lax.psum_scatter(acc_in, "dp", scatter_dimension=0, tiled=True),
        lax.psum_scatter(acc_out, "dp", scatter_dimension=1, tiled=True),
        lax.psum_scatter(acc_back, "dp", scatter_dimension=1, tiled=True),
        lax.psum_scatter(acc_qv, "dp", scatter_dimension=2, tiled=True),
        lax.psum_scatter(acc_in_bias.reshape(-1, 128), "dp", scatter_dimension=1, tiled=True),
    )
    y_out = jnp.stack(outs_y)
    grad_x = jnp.stack(outs_grad)
    return (
        y_out,
        loss,
        grad_x,
        grad_table,
        grad_norm_gains,
        grad_shifts,
        grad_qkv,
        grad_qv_bias,
        grad_out,
        grad_in,
        grad_in_bias,
        grad_back,
    )


def solution(mesh):
    return jax.shard_map(
        per_device,
        mesh=mesh,
        in_specs=(
            P(None, "dp", None),
            P(None, "dp", "mp"),
            P(),
            P(),
            P(),
            P(None, ("dp", "mp")),
            P(None, ("dp", "mp")),
            P(None, ("dp", "mp")),
            P("dp", "mp"),
            P(None, "mp", "dp"),
            P("mp", "dp"),
            P("dp", "mp"),
            P("mp", "dp"),
            P("mp", "dp"),
        ),
        out_specs=(
            P(None, "dp", "mp"),
            P(),
            P(None, "dp", "mp"),
            P(None, ("dp", "mp")),
            P(None, ("dp", "mp")),
            P(None, ("dp", "mp")),
            P("dp", "mp"),
            P(None, "mp", "dp"),
            P("mp", "dp"),
            P("dp", "mp"),
            P("mp", "dp"),
            P("mp", "dp"),
        ),
        check_vma=False,
    )
```

profile of v0, /device:TPU:24, one launch (start us, length us, event | category | flops | bytes accessed | tf_op | source)
XLA Modules:
  0.0 1315.9 jit_solution(14885123782752954395)
XLA Ops:
  11.9 6.1 all-to-all-start.4
  25.0 31.1 %all_gather.40 = bf16[2,3,64]{1,0,2:T(2,128)(2,1)S(1)} all-gather(bf16[2,3,8]{1,0,2:T(2,128)(2,1)S(1)} %copy.239), channel_id=1, replica_groups=mesh['dp'=8,'mp'=4] {'dp'}, dimensions={2}, use_global_device_ids=true | all-gather | bytes 864 | tf_op jit(solution)/shard_map/all_gather | solution.py:32
  56.1 33.7 %all_gather.36 = bf16[24,768]{0,1:T(8,128)(2,1)S(1)} all-gather(bf16[24,24]{0,1:T(8,128)(2,1)S(1)} %copy.232), channel_id=1, replica_groups=mesh['dp'=8,'mp'=4] {'dp','mp'}, dimensions={1}, use_global_device_ids=true | all-gather | bytes 38016 | tf_op jit(solution)/shard_map/all_gather | solution.py:131
  92.5 38.1 %all_gather.39 = bf16[768,576]{1,0:T(8,128)(2,1)S(1)} all-gather(bf16[96,576]{1,0:T(8,128)(2,1)S(1)} %copy-done.88), channel_id=1, replica_groups=mesh['dp'=8,'mp'=4] {'dp'}, dimensions={0}, use_global_device_ids=true | all-gather | bytes 995328 | tf_op jit(solution)/shard_map/all_gather | solution.py:28
  130.6 6.8 all-to-all-start
  137.4 37.3 %all-gather = bf16[32,24,2]{1,2,0:T(2,128)(2,1)} all-gather(bf16[1,24,2]{1,2,0:T(2,128)(2,1)S(1)} %bitcast.521), channel_id=1, replica_groups=mesh['dp'=8,'mp'=4] {'dp','mp'}, dimensions={0}, use_global_device_ids=true | all-gather | bytes 3168 | tf_op jit(solution)/shard_map/all_gather | solution.py:129
  177.6 38.2 %all-gather.1 = bf16[32,24,4]{1,2,0:T(4,128)(2,1)} all-gather(bf16[1,24,4]{1,2,0:T(4,128)(2,1)} %bitcast.520), channel_id=1, replica_groups=mesh['dp'=8,'mp'=4] {'dp','mp'}, dimensions={0}, use_global_device_ids=true | all-gather | bytes 6336 | tf_op jit(solution)/shard_map/all_gather | solution.py:130
  230.6 35.9 %all_gather.41 = bf16[192,768]{0,1:T(8,128)(2,1)S(1)} all-gather(bf16[192,96]{0,1:T(8,128)(2,1)} %copy.243), channel_id=1, replica_groups=mesh['dp'=8,'mp'=4] {'dp'}, dimensions={1}, use_global_device_ids=true | all-gather | bytes 331776 | tf_op jit(solution)/shard_map/all_gather | solution.py:30
  271.3 7.4 all-to-all-start.2
  280.8 9.9 all-to-all-done.2
  342.6 18.9 %reduce-scatter.31.cloned.1.call-done = f32[512,192]{0,1:T(8,128)} async-done(((f32[512,768]{0,1:T(8,128)}), f32[512,192]{0,1:T(8,128)}) %reduce-scatter.31.cloned.1.call-update) | async-done | bytes 393232 | tf_op jit(solution)/shard_map/reduce_scatter | solution.py:199
  361.4 30.6 %reduce-scatter.35.cloned.1.call-done = f32[512,192]{0,1:T(8,128)} async-done(((f32[512,768]{0,1:T(8,128)}), f32[512,192]{0,1:T(8,128)}) %reduce-scatter.35.cloned.1.call-update) | async-done | bytes 393232 | tf_op jit(solution)/shard_map/reduce_scatter | solution.py:199
  397.6 22.5 %all-gather.2 = bf16[8,16,6]{1,2,0:T(8,128)(2,1)S(1)} all-gather(bf16[1,16,6]{1,2,0:T(8,128)(2,1)S(1)} %bitcast.519), channel_id=1, replica_groups=mesh['dp'=8,'mp'=4] {'dp'}, dimensions={0}, use_global_device_ids=true | all-gather | bytes 1728 | tf_op jit(solution)/shard_map/all_gather | solution.py:33
  427.0 29.5 %all-gather.11.cloned.1.call-done = bf16[768,768]{1,0:T(8,128)(2,1)} async-done(((bf16[96,768]{1,0:T(8,128)(2,1)}), bf16[768,768]{1,0:T(8,128)(2,1)}) %all-gather.11.cloned.1.call-update) | async-done | bytes 1179664 | tf_op jit(solution)/shard_map/all_gather | solution.py:29
  460.6 37.8 %all-gather.13.cloned.1.call-done = bf16[768,768]{0,1:T(8,128)(2,1)} async-done(((bf16[768,96]{0,1:T(8,128)(2,1)}), bf16[768,768]{0,1:T(8,128)(2,1)}) %all-gather.13.cloned.1.call-update) | async-done | bytes 1179664 | tf_op jit(solution)/shard_map/all_gather | solution.py:31
  502.5 17.2 %all-gather.17.cloned.1.call-done = f32[512,768]{0,1:T(8,128)} async-done(((f32[512,192]{0,1:T(8,128)}), f32[512,768]{0,1:T(8,128)}) %all-gather.17.cloned.1.call-update) | async-done | bytes 1572880 | tf_op jit(solution)/shard_map/all_gather | solution.py:203
  530.1 11.3 all-gather.9.cloned.1.call-done
  558.6 6.0 all-to-all-start.8
  575.9 6.0 all-to-all-start.7
  588.0 6.7 all-to-all-start.6
  612.7 20.3 %reduce-scatter.29.cloned.1.call-done = f32[512,192]{0,1:T(8,128)} async-done(((f32[512,768]{0,1:T(8,128)}), f32[512,192]{0,1:T(8,128)}) %reduce-scatter.29.cloned.1.call-update) | async-done | bytes 393232 | tf_op jit(solution)/shard_map/reduce_scatter | solution.py:209
  637.2 8.0 all_gather.92
  650.5 9.1 all_gather.94
  659.6 10.6 all_gather.90
  710.2 12.4 all-reduce.13
  730.7 13.2 %all_gather.91 = bf16[512,768]{0,1:T(8,128)(2,1)S(1)} all-gather(bf16[512,192]{0,1:T(8,128)(2,1)S(1)} %get-tuple-element.578), channel_id=1, replica_groups=mesh['dp'=8,'mp'=4] {'mp'}, dimensions={1}, use_global_device_ids=true | all-gather | bytes 983040 | tf_op jit(solution)/shard_map/all_gather | solution.py:256
  746.2 8.8 all_gather.93
  765.6 9.3 all_gather.95
  805.6 7.0 multiply_reduce_fusion.19
  840.6 16.8 %all-reduce.10 = f32[2,3,64]{2,1,0:T(4,128)S(1)} all-reduce(f32[2,3,64]{2,1,0:T(4,128)S(1)} %fusion.107), channel_id=25, replica_groups=mesh['dp'=8,'mp'=4] {'dp'}, use_global_device_ids=true, to_apply=%region_96.99.clone | all-reduce | flops 384 | bytes 3072
  860.3 11.0 all-reduce.12
  871.3 7.0 reduce-scatter.59.cloned.1.call-done
  879.9 28.9 %reduce-scatter.45.cloned.1.call-done = f32[512,192]{0,1:T(8,128)} async-done(((f32[512,768]{0,1:T(8,128)}), f32[512,192]{0,1:T(8,128)}) %reduce-scatter.45.cloned.1.call-update) | async-done | bytes 393232 | tf_op jit(solution)/shard_map/reduce_scatter | solution.py:289
  911.0 28.3 %reduce-scatter.41.cloned.1.call-done = f32[512,192]{0,1:T(8,128)} async-done(((f32[512,768]{0,1:T(8,128)}), f32[512,192]{0,1:T(8,128)}) %reduce-scatter.41.cloned.1.call-update) | async-done | bytes 393232 | tf_op jit(solution)/shard_map/reduce_scatter | solution.py:289
  939.3 30.6 %reduce-scatter.49.cloned.1.call-done = f32[512,192]{0,1:T(8,128)} async-done(((f32[512,768]{0,1:T(8,128)}), f32[512,192]{0,1:T(8,128)}) %reduce-scatter.49.cloned.1.call-update) | async-done | bytes 393232 | tf_op jit(solution)/shard_map/reduce_scatter | solution.py:289
  976.2 6.0 all-to-all-start.10
  982.4 12.8 all-to-all-done.10
  995.2 6.1 all-to-all-start.3
  1003.0 10.7 all-to-all-done.3
  1019.5 6.1 all-to-all-done.9
  1025.6 6.3 all-to-all-start.1
  1037.7 6.3 all-to-all-start.11
  1044.1 10.9 all-to-all-done.11
  1055.0 6.0 all-to-all-start.5
  1061.5 39.6 %all-reduce.11 = (f32[1,32]{1,0:T(1,128)S(1)}, f32[2,768]{1,0:T(2,128)S(1)}, f32[4,768]{1,0:T(4,128)S(1)}) all-reduce(f32[1,32]{1,0:T(1,128)S(1)} %broadcast_in_dim.294, f32[2,768]{1,0:T(2,128)S(1)} %dynamic_update_slice.30, f32[4,768]{1,0:T(4,128)S(1)} %dynamic_update_slice.31), channel_id=8, replica_groups=mesh['dp'=8,'mp'=4] {'dp','mp'}, use_global_device_ids=true, to_apply=%region_36.39.clone | all-reduce | flops 4640 | bytes 37120
  1110.0 19.7 %reduce-scatter.55.cloned.1.call-done = f32[96,768]{1,0:T(8,128)} async-done(((f32[768,768]{1,0:T(8,128)}), f32[96,768]{1,0:T(8,128)}) %reduce-scatter.55.cloned.1.call-update) | async-done | bytes 294928 | tf_op jit(solution)/shard_map/reduce_scatter | solution.py:347
  1129.6 70.9 %reduce-scatter.53.cloned.1.call-done = f32[96,576]{1,0:T(8,128)} async-done(((f32[768,576]{1,0:T(8,128)}), f32[96,576]{1,0:T(8,128)}) %reduce-scatter.53.cloned.1.call-update) | async-done | bytes 221200 | tf_op jit(solution)/shard_map/reduce_scatter | solution.py:346
  1200.6 107.5 %reduce-scatter.51.cloned.1.call-done = f32[1000,24]{0,1:T(8,128)} async-done(((f32[1000,768]{0,1:T(8,128)}), f32[1000,24]{0,1:T(8,128)}) %reduce-scatter.51.cloned.1.call-update) | async-done | bytes 96016 | tf_op jit(solution)/shard_map/reduce_scatter | solution.py:339
  (782 shorter events, 332.6 us)
Async XLA Ops:
  11.9 118.8 %all-to-all-start.4 = ((bf16[8,64,768]{2,1,0:T(8,128)(2,1)}), bf16[8,64,768]{2,1,0:T(8,128)(2,1)S(1)}, u32[]{:S(2)}, u32[]{:S(2)}) async-start(bf16[8,64,768]{2,1,0:T(8,128)(2,1)} %broadcast_select_fusion.1), calls=%async_computation.8 | async-start | bytes 1572864 | tf_op jit(solution)/shard_map/all_to_all | solution.py:160
  18.2 73.3 %copy-start.175 = (s32[8]{0:T(128)}, s32[8]{0:T(128)S(1)}, u32[]{:S(2)}) copy-start(s32[8]{0:T(128)S(1)} %get-tuple-element.567) | copy-start | bytes 100
  18.2 73.3 %copy-start.160 = (pred[8]{0:T(512)(128)(4,1)}, pred[8]{0:T(512)(128)(4,1)S(1)}, u32[]{:S(2)}) copy-start(pred[8]{0:T(512)(128)(4,1)S(1)} %compare_and_fusion.11) | copy-start | bytes 28
  19.3 72.2 %copy-start.140 = (s32[1024]{0:T(1024)}, s32[1024]{0:T(1024)S(1)}, u32[]{:S(2)}) copy-start(s32[1024]{0:T(1024)S(1)} %pad_clamp_fusion.13) | copy-start | bytes 12292
  20.4 71.1 %copy-start.181 = (s32[8]{0:T(128)}, s32[8]{0:T(128)S(1)}, u32[]{:S(2)}) copy-start(s32[8]{0:T(128)S(1)} %get-tuple-element.520) | copy-start | bytes 100
  21.0 70.5 %copy-start.179 = (s32[8]{0:T(128)}, s32[8]{0:T(128)S(1)}, u32[]{:S(2)}) copy-start(s32[8]{0:T(128)S(1)} %get-tuple-element.518) | copy-start | bytes 100
  25.0 67.5 %copy-start.88 = (bf16[96,576]{1,0:T(8,128)(2,1)S(1)}, bf16[96,576]{1,0:T(8,128)(2,1)}, u32[]{:S(2)}) copy-start(bf16[96,576]{1,0:T(8,128)(2,1)} %param.62) | copy-start | bytes 331780
  130.6 95.3 %copy-start.5 = (bf16[768,576]{1,0:T(8,128)(2,1)}, bf16[768,576]{1,0:T(8,128)(2,1)S(1)}, u32[]{:S(2)}) copy-start(bf16[768,576]{1,0:T(8,128)(2,1)S(1)} %all_gather.39) | copy-start | bytes 2654212
  130.6 140.7 %all-to-all-start = ((bf16[8,64,768]{2,1,0:T(8,128)(2,1)}), bf16[8,64,768]{2,1,0:T(8,128)(2,1)S(1)}, u32[]{:S(2)}, u32[]{:S(2)}) async-start(bf16[8,64,768]{2,1,0:T(8,128)(2,1)} %broadcast_select_fusion.5), calls=%async_computation | async-start | bytes 1572864 | tf_op jit(solution)/shard_map/all_to_all | solution.py:160
  228.6 62.2 %copy-start.141 = (s32[1024]{0:T(1024)}, s32[1024]{0:T(1024)S(1)}, u32[]{:S(2)}) copy-start(s32[1024]{0:T(1024)S(1)} %pad_clamp_fusion.7) | copy-start | bytes 12292
  230.6 62.8 %copy-start.105 = (f32[768]{0:T(1024)}, f32[768]{0:T(1024)S(1)}, u32[]{:S(2)}) copy-start(f32[768]{0:T(1024)S(1)} %get-tuple-element.461) | copy-start | bytes 9220
  271.3 19.5 %all-to-all-start.2 = ((bf16[8,64,768]{2,1,0:T(8,128)(2,1)}), bf16[8,64,768]{2,1,0:T(8,128)(2,1)}, u32[]{:S(2)}, u32[]{:S(2)}) async-start(bf16[8,64,768]{2,1,0:T(8,128)(2,1)} %broadcast_select_fusion.3), calls=%async_computation.4 | async-start | bytes 1572864 | tf_op jit(solution)/shard_map/all_to_all | solution.py:160
  278.7 63.9 %reduce-scatter.27.cloned.1.call-start = ((), (), s32[]{:S(2)}) async-start(), calls=%async_computation.30 | async-start | bytes 1966080 | tf_op jit(solution)/shard_map/reduce_scatter | solution.py:199
  301.1 60.3 %reduce-scatter.31.cloned.1.call-start = ((), (), s32[]{:S(2)}) async-start(), calls=%async_computation.35 | async-start | bytes 1966080 | tf_op jit(solution)/shard_map/reduce_scatter | solution.py:199
  309.9 82.1 %reduce-scatter.35.cloned.1.call-start = ((), (), s32[]{:S(2)}) async-start(), calls=%async_computation.38 | async-start | bytes 1966080 | tf_op jit(solution)/shard_map/reduce_scatter | solution.py:199
  318.3 103.9 %all-gather.15.cloned.1.call-start = ((), (), s32[]{:S(2)}) async-start(), calls=%async_computation.36 | async-start | bytes 1966080 | tf_op jit(solution)/shard_map/all_gather | solution.py:203
  394.9 61.7 %all-gather.11.cloned.1.call-start = ((), (), s32[]{:S(2)}) async-start(), calls=%async_computation.32 | async-start | bytes 1327104 | tf_op jit(solution)/shard_map/all_gather | solution.py:29
  395.4 103.0 %all-gather.13.cloned.1.call-start = ((), (), s32[]{:S(2)}) async-start(), calls=%async_computation.33 | async-start | bytes 1327104 | tf_op jit(solution)/shard_map/all_gather | solution.py:31
  396.0 123.6 %all-gather.17.cloned.1.call-start = ((), (), s32[]{:S(2)}) async-start(), calls=%async_computation.39 | async-start | bytes 1966080 | tf_op jit(solution)/shard_map/all_gather | solution.py:203
  396.8 144.7 %all-gather.9.cloned.1.call-start = ((), (), s32[]{:S(2)}) async-start(), calls=%async_computation.31 | async-start | bytes 1966080 | tf_op jit(solution)/shard_map/all_gather | solution.py:203
  397.5 215.1 %reduce-scatter.33.cloned.1.call-start = ((), (), s32[]{:S(2)}) async-start(), calls=%async_computation.37 | async-start | bytes 1966080 | tf_op jit(solution)/shard_map/reduce_scatter | solution.py:209
  502.2 110.4 %reduce-scatter.37.cloned.1.call-start = ((), (), s32[]{:S(2)}) async-start(), calls=%async_computation.40 | async-start | bytes 1966080 | tf_op jit(solution)/shard_map/reduce_scatter | solution.py:209
  530.1 102.9 %reduce-scatter.29.cloned.1.call-start = ((), (), s32[]{:S(2)}) async-start(), calls=%async_computation.34 | async-start | bytes 1966080 | tf_op jit(solution)/shard_map/reduce_scatter | solution.py:209
  558.6 17.3 %all-to-all-start.8 = ((bf16[8,64,192]{2,1,0:T(8,128)(2,1)}), bf16[8,64,192]{2,1,0:T(8,128)(2,1)}, u32[]{:S(2)}, u32[]{:S(2)}) async-start(bf16[8,64,192]{2,1,0:T(8,128)(2,1)} %broadcast_select_fusion.7), calls=%async_computation.14 | async-start | bytes 524288 | tf_op jit(solution)/shard_map/all_to_all | solution.py:167
  575.9 12.1 all-to-all-start.7
  588.0 18.4 %all-to-all-start.6 = ((bf16[8,64,192]{2,1,0:T(8,128)(2,1)}), bf16[8,64,192]{2,1,0:T(8,128)(2,1)}, u32[]{:S(2)}, u32[]{:S(2)}) async-start(bf16[8,64,192]{2,1,0:T(8,128)(2,1)} %broadcast_select_fusion.11), calls=%async_computation.12 | async-start | bytes 524288 | tf_op jit(solution)/shard_map/all_to_all | solution.py:167
  594.7 132.2 %reduce-scatter.43.cloned.1.call-start = ((), (), s32[]{:S(2)}) async-start(), calls=%async_computation.43 | async-start | bytes 1966080 | tf_op jit(solution)/shard_map/reduce_scatter | solution.py:240
  650.5 76.4 %reduce-scatter.39.cloned.1.call-start = ((), (), s32[]{:S(2)}) async-start(), calls=%async_computation.41 | async-start | bytes 1966080 | tf_op jit(solution)/shard_map/reduce_scatter | solution.py:240
  684.4 78.1 %reduce-scatter.47.cloned.1.call-start = ((), (), s32[]{:S(2)}) async-start(), calls=%async_computation.45 | async-start | bytes 1966080 | tf_op jit(solution)/shard_map/reduce_scatter | solution.py:240
  684.9 154.2 %reduce-scatter.61.cloned.1.call-start = ((), (), s32[]{:S(2)}) async-start(), calls=%async_computation.52 | async-start | bytes 73728
  726.8 151.5 %reduce-scatter.59.cloned.1.call-start = ((), (), s32[]{:S(2)}) async-start(), calls=%async_computation.51 | async-start | bytes 884736
  781.6 127.2 %reduce-scatter.45.cloned.1.call-start = ((), (), s32[]{:S(2)}) async-start(), calls=%async_computation.44 | async-start | bytes 1966080 | tf_op jit(solution)/shard_map/reduce_scatter | solution.py:289
  793.3 146.0 %reduce-scatter.41.cloned.1.call-start = ((), (), s32[]{:S(2)}) async-start(), calls=%async_computation.42 | async-start | bytes 1966080 | tf_op jit(solution)/shard_map/reduce_scatter | solution.py:289
  812.6 157.3 %reduce-scatter.49.cloned.1.call-start = ((), (), s32[]{:S(2)}) async-start(), calls=%async_computation.46 | async-start | bytes 1966080 | tf_op jit(solution)/shard_map/reduce_scatter | solution.py:289
  813.4 296.6 %reduce-scatter.57.cloned.1.call-start = ((), (), s32[]{:S(2)}) async-start(), calls=%async_computation.50 | async-start | bytes 2654208 | tf_op jit(solution)/shard_map/reduce_scatter | solution.py:349
  820.4 309.3 %reduce-scatter.55.cloned.1.call-start = ((), (), s32[]{:S(2)}) async-start(), calls=%async_computation.49 | async-start | bytes 2654208 | tf_op jit(solution)/shard_map/reduce_scatter | solution.py:347
  827.8 372.8 %reduce-scatter.53.cloned.1.call-start = ((), (), s32[]{:S(2)}) async-start(), calls=%async_computation.48 | async-start | bytes 2211840 | tf_op jit(solution)/shard_map/reduce_scatter | solution.py:346
  836.0 472.0 %reduce-scatter.51.cloned.1.call-start = ((), (), s32[]{:S(2)}) async-start(), calls=%async_computation.47 | async-start | bytes 3244032 | tf_op jit(solution)/shard_map/reduce_scatter | solution.py:339
  837.0 71.8 %copy-start.58 = (f32[512,192]{0,1:T(8,128)S(1)}, f32[512,192]{0,1:T(8,128)}, u32[]{:S(2)}) copy-start(f32[512,192]{0,1:T(8,128)} %get-tuple-element.535) | copy-start | bytes 1179652
  837.0 71.8 %copy-start.130 = (f32[1,192]{1,0:T(1,128)S(1)}, f32[1,192]{1,0:T(1,128)}, u32[]{:S(2)}) copy-start(f32[1,192]{1,0:T(1,128)} %get-tuple-element.572) | copy-start | bytes 2308
  839.1 130.9 %copy-start.57 = (f32[512,192]{0,1:T(8,128)S(1)}, f32[512,192]{0,1:T(8,128)}, u32[]{:S(2)}) copy-start(f32[512,192]{0,1:T(8,128)} %get-tuple-element.579) | copy-start | bytes 1179652
  839.1 130.8 %copy-start.59 = (f32[512,192]{0,1:T(8,128)S(1)}, f32[512,192]{0,1:T(8,128)}, u32[]{:S(2)}) copy-start(f32[512,192]{0,1:T(8,128)} %get-tuple-element.532) | copy-start | bytes 1179652
  976.2 19.0 %all-to-all-start.10 = ((bf16[8,64,192]{2,1,0:T(8,128)(2,1)}), bf16[8,64,192]{2,1,0:T(8,128)(2,1)S(1)}, u32[]{:S(2)}, u32[]{:S(2)}) async-start(bf16[8,64,192]{2,1,0:T(8,128)(2,1)} %get-tuple-element.601), calls=%async_computation.20 | async-start | bytes 524288 | tf_op jit(solution)/shard_map/all_to_all | solution.py:317
  995.2 18.5 %all-to-all-start.3 = ((bf16[8,64,192]{2,1,0:T(8,128)(2,1)}), bf16[8,64,192]{2,1,0:T(8,128)(2,1)S(1)}, u32[]{:S(2)}, u32[]{:S(2)}) async-start(bf16[8,64,192]{2,1,0:T(8,128)(2,1)} %get-tuple-element.602), calls=%async_computation.7 | async-start | bytes 524288 | tf_op jit(solution)/shard_map/all_to_all | solution.py:316
  1013.7 11.9 all-to-all-start.9
  1025.6 12.2 all-to-all-start.1
  1037.7 17.3 %all-to-all-start.11 = ((bf16[8,64,192]{2,1,0:T(8,128)(2,1)}), bf16[8,64,192]{2,1,0:T(8,128)(2,1)S(1)}, u32[]{:S(2)}, u32[]{:S(2)}) async-start(bf16[8,64,192]{2,1,0:T(8,128)(2,1)} %get-tuple-element.605), calls=%async_computation.23 | async-start | bytes 524288 | tf_op jit(solution)/shard_map/all_to_all | solution.py:317
  1055.0 51.5 %all-to-all-start.5 = ((bf16[8,64,192]{2,1,0:T(8,128)(2,1)}), bf16[8,64,192]{2,1,0:T(8,128)(2,1)S(1)}, u32[]{:S(2)}, u32[]{:S(2)}) async-start(bf16[8,64,192]{2,1,0:T(8,128)(2,1)} %get-tuple-element.606), calls=%async_computation.11 | async-start | bytes 524288 | tf_op jit(solution)/shard_map/all_to_all | solution.py:316
  (177 other events, 1161.7 us)
Sparse Core Ops, SparseCore 0:
  301.2 29.5 reduce-scatter.26
  333.4 28.0 reduce-scatter.30
  364.0 28.0 reduce-scatter.34
  395.0 19.6 all-gather.14
  416.7 39.8 all-gather.10
  458.6 39.7 all-gather.12
  500.0 19.6 all-gather.16
  521.8 19.6 all-gather.8
  544.0 27.9 reduce-scatter.32
  574.4 27.9 reduce-scatter.36
  604.9 27.9 reduce-scatter.28
  650.6 28.5 reduce-scatter.42
  684.5 28.3 reduce-scatter.38
  715.3 32.2 reduce-scatter.46
  751.3 61.4 reduce-scatter.60
  816.0 62.2 reduce-scatter.58
  880.7 28.1 reduce-scatter.44
  911.2 28.0 reduce-scatter.40
  941.8 28.0 reduce-scatter.48
  973.8 81.9 reduce-scatter.56
  1059.9 69.6 reduce-scatter.54
  1133.7 66.8 reduce-scatter.52
  1206.6 101.4 reduce-scatter.50
where the time goes:
time: 1330 us; the launch traced here: 1320 us
  waiting for transfers between devices  518 us (39%)
  blocking collectives  376 us (28%)
  local copies, waits for them, and re-layouts  132 us (10%)
  matrix products  96.7 us (7%)
  other arithmetic  94.5 us (7%)
  starting transfers between devices  76.9 us (6%)
  between operations  22.4 us (2%)
    reduce_scatter x1, waiting for transfers between devices, per_device(): lax.psum_scatter(table_grad, ('dp', 'mp'), scatter_dimension=1, tiled=True)  107 us
    reduce_scatter x3, waiting for transfers between devices, per_device(): lax.psum_scatter(partial1, 'mp', scatter_dimension=1, tiled=True)  87.8 us
    unnamed x4, blocking collectives  79.8 us
    reduce_scatter x1, waiting for transfers between devices, per_device(): lax.psum_scatter(acc_qkv, 'dp', scatter_dimension=0, tiled=True)  70.9 us
    reduce_scatter x3, waiting for transfers between devices, per_device(): lax.psum_scatter(attn_part, 'mp', scatter_dimension=1, tiled=True)  49.5 us
    unnamed x399, local copies, waits for them, and re-layouts  44.6 us
    all_gather x1, blocking collectives, per_device(): lax.all_gather(shifts, ('dp', 'mp'), axis=1, tiled=True)  38.2 us
    all_gather x1, blocking collectives, fetch_weights(): lax.all_gather(w_qkv, 'dp', axis=0, tiled=True)  38.1 us
  transfers between devices with their start and end apart: 35, of which 21 were waited for; matrix products, arithmetic and copies ran while one was open for 21% of the time, Pallas kernels for 0%

commit v1 on v0

--- a/solution.py
+++ b/solution.py
@@ -4,6 +4,8 @@
 import jax
 import jax.numpy as jnp
 from jax import lax
+from jax.experimental import pallas as pl
+from jax.experimental.pallas import tpu as pltpu
 from jax.sharding import PartitionSpec as P
 
 H = 12
@@ -368,9 +370,538 @@
     )
 
 
+MESH = pl.DeviceIdType.MESH
+BF = jnp.bfloat16
+F32 = jnp.float32
+VM = pl.BlockSpec(memory_space=pltpu.VMEM)
+DP = 8
+ROWS = 96
+VMEM_LIMIT = 64 * 1024 * 1024 - 65536
+
+
+def place():
+    dp, mp = lax.axis_index("dp"), lax.axis_index("mp")
+    x, c = lax.div(mp, 2), lax.rem(mp, 2)
+    return dp, mp, x, c
+
+
+def remote(src, dst, send_sem, recv_sem, dp, mp):
+    return pltpu.make_async_remote_copy(
+        src_ref=src,
+        dst_ref=dst,
+        send_sem=send_sem,
+        recv_sem=recv_sem,
+        device_id=(dp, mp),
+        device_id_type=MESH,
+    )
+
+
+def landed(dst, recv_sem, spare, dp, mp):
+    remote(dst, dst, spare, recv_sem, dp, mp).wait_recv()
+
+
+def greet_plane(dp, x, c):
+    barrier = pltpu.get_barrier_semaphore()
+    pl.semaphore_signal(barrier, inc=1, device_id=(dp, 2 * x + 1 - c), device_id_type=MESH)
+    for k in range(DP):
+        for xr in range(2):
+            if k or xr:
+                there = (lax.rem(dp + k, DP), 2 * lax.rem(x + xr, 2) + c)
+                pl.semaphore_signal(barrier, inc=1, device_id=there, device_id_type=MESH)
+    pl.semaphore_wait(barrier, 2 * DP)
+
+
+def gather_kernel(
+    xs, ts, wsh, small, tok, tea, w, smalls,
+    s_tok, r_tok, s_tea, r_tea, s_small, r_small, s_w, r_w, s_core, r_core,
+):
+    dp, mp, x, c = place()
+    z, y = lax.div(dp, 2), lax.rem(dp, 2)
+    other = 2 * x + 1 - c
+    mine = x * DP + dp
+    greet_plane(dp, x, c)
+    sent = []
+
+    def go(copy):
+        copy.start()
+        sent.append(copy)
+
+    pltpu.make_async_copy(xs.at[c, x, dp], tok.at[c, dp], r_tok.at[dp]).start()
+
+    @pl.when(y == x)
+    def _():
+        pltpu.make_async_copy(xs.at[c, 2, dp], tok.at[c, 8 + z], r_tok.at[8 + z]).start()
+
+    for k in range(1, DP):
+        d = lax.rem(dp + k, DP)
+        go(remote(xs.at[c, x, d], tok.at[c, dp], s_tok.at[k], r_tok.at[dp], d, mp))
+
+    @pl.when(y == x)
+    def _():
+        for k in range(1, DP):
+            d = lax.rem(dp + k, DP)
+            remote(xs.at[c, 2, d], tok.at[c, 8 + z], s_tok.at[8 + k], r_tok.at[8 + z], d, mp).start()
+
+    pltpu.make_async_copy(small, smalls.at[mp, dp], r_small.at[mine]).start()
+    for k in range(DP):
+        for xr in range(2):
+            if k or xr:
+                d, m = lax.rem(dp + k, DP), 2 * lax.rem(x + xr, 2) + c
+                go(remote(small, smalls.at[mp, dp], s_small.at[2 * k + xr], r_small.at[mine], d, m))
+
+    mx, dy = 2 * (1 - x) + c, 2 * z + 1 - y
+    for p in range(3):
+        pltpu.make_async_copy(wsh.at[p], w.at[p, mine], r_w.at[p, mine]).start()
+        for k in range(1, 4):
+            zz = lax.rem(z + k, 4)
+            go(remote(wsh.at[p], w.at[p, mine], s_w.at[p, k - 1], r_w.at[p, mine], 2 * zz + y, mp))
+        go(remote(wsh.at[p], w.at[p, mine], s_w.at[p, 3], r_w.at[p, mine], dp, mx))
+        go(remote(wsh.at[p], w.at[p, mine], s_w.at[p, 4], r_w.at[p, mine], dy, mp))
+
+    def spread(p):
+        for k in range(1, 4):
+            b = x * DP + 2 * lax.rem(z + k, 4) + y
+            landed(w.at[p, b], r_w.at[p, b], s_w.at[p, 0], dp, mp)
+            go(remote(w.at[p, b], w.at[p, b], s_w.at[p, 3 + 2 * k], r_w.at[p, b], dp, mx))
+            go(remote(w.at[p, b], w.at[p, b], s_w.at[p, 4 + 2 * k], r_w.at[p, b], dy, mp))
+
+    def relay(p):
+        for k in range(4):
+            bx, by = (1 - x) * DP + 2 * k + y, x * DP + 2 * k + 1 - y
+            landed(w.at[p, bx], r_w.at[p, bx], s_w.at[p, 0], dp, mp)
+            landed(w.at[p, by], r_w.at[p, by], s_w.at[p, 0], dp, mp)
+            if k < 2:
+                go(remote(w.at[p, bx], w.at[p, bx], s_w.at[p, 11 + k], r_w.at[p, bx], dy, mp))
+            else:
+                go(remote(w.at[p, by], w.at[p, by], s_w.at[p, 11 + k], r_w.at[p, by], dp, mx))
+
+    spread(0)
+
+    pltpu.make_async_copy(ts.at[x, dp], tea.at[mp, dp], r_tea.at[x, dp]).start()
+    for k in range(DP):
+        d = lax.rem(dp + k, DP)
+        for xr in range(2):
+            if k or xr:
+                xx = lax.rem(x + xr, 2)
+                go(remote(ts.at[xx, d], tea.at[mp, dp], s_tea.at[2 * k + xr], r_tea.at[x, dp], d, 2 * xx + c))
+        if k:
+            go(remote(ts.at[2, d], tea.at[mp, 8 + z], s_tea.at[16 + k], r_tea.at[x, 8 + z], d, 2 * y + c))
+
+    @pl.when(y == x)
+    def _():
+        pltpu.make_async_copy(ts.at[2, dp], tea.at[mp, 8 + z], r_tea.at[x, 8 + z]).start()
+
+    @pl.when(y != x)
+    def _():
+        copy = remote(ts.at[2, dp], tea.at[mp, 8 + z], s_tea.at[16], r_tea.at[x, 8 + z], dp, 2 * y + c)
+        copy.start()
+        copy.wait_send()
+
+    spread(1)
+    relay(0)
+    spread(2)
+
+    for j in range(12):
+        landed(tok.at[c, j], r_tok.at[j], s_tok.at[0], dp, mp)
+    go(remote(tok.at[c], tok.at[c], s_core.at[0], r_core.at[0], dp, other))
+    for j in range(8):
+        for xx in range(2):
+            m = 2 * xx + c
+            landed(smalls.at[m, j], r_small.at[xx * DP + j], s_small.at[0], dp, mp)
+    go(remote(smalls.at[c], smalls.at[c], s_core.at[1], r_core.at[1], dp, other))
+    go(remote(smalls.at[2 + c], smalls.at[2 + c], s_core.at[2], r_core.at[2], dp, other))
+
+    relay(1)
+    relay(2)
+
+    for xx in range(2):
+        for j in range(12):
+            landed(tea.at[2 * xx + c, j], r_tea.at[xx, j], s_tea.at[0], dp, mp)
+    go(remote(tea.at[c], tea.at[c], s_core.at[3], r_core.at[3], dp, other))
+    go(remote(tea.at[2 + c], tea.at[2 + c], s_core.at[4], r_core.at[4], dp, other))
+
+    for p in range(3):
+        landed(w.at[p, mine], r_w.at[p, mine], s_w.at[p, 0], dp, mp)
+        for k in range(4):
+            b = (1 - x) * DP + 2 * k + 1 - y
+            landed(w.at[p, b], r_w.at[p, b], s_w.at[p, 0], dp, mp)
+    o = 1 - c
+    landed(tok.at[o], r_core.at[0], s_core.at[0], dp, mp)
+    landed(smalls.at[o], r_core.at[1], s_core.at[0], dp, mp)
+    landed(smalls.at[2 + o], r_core.at[2], s_core.at[0], dp, mp)
+    landed(tea.at[o], r_core.at[3], s_core.at[0], dp, mp)
+    landed(tea.at[2 + o], r_core.at[4], s_core.at[0], dp, mp)
+    for copy in sent:
+        copy.wait_send()
+
+    @pl.when(y == x)
+    def _():
+        for k in range(1, DP):
+            d = lax.rem(dp + k, DP)
+            remote(xs.at[c, 2, d], tok.at[c, 8 + z], s_tok.at[8 + k], r_tok.at[8 + z], d, mp).wait_send()
+
+
+def gather_all(xs, ts, wsh, small):
+    dma = pltpu.SemaphoreType.DMA
+    return pl.pallas_call(
+        gather_kernel,
+        name="gather_all",
+        out_shape=(
+            jax.ShapeDtypeStruct((2, 12, 64, 384), BF),
+            jax.ShapeDtypeStruct((4, 12, 64, 192), BF),
+            jax.ShapeDtypeStruct((3, 16, ROWS, 768), BF),
+            jax.ShapeDtypeStruct((4, DP, 32, 128), BF),
+        ),
+        in_specs=[VM] * 4,
+        out_specs=(VM,) * 4,
+        scratch_shapes=[
+            dma((16,)), dma((12,)), dma((24,)), dma((2, 12)), dma((16,)), dma((16,)),
+            dma((3, 15)), dma((3, 16)), dma((5,)), dma((5,)),
+        ],
+        compiler_params=pltpu.CompilerParams(
+            collective_id=1, has_side_effects=True, vmem_limit_bytes=VMEM_LIMIT
+        ),
+    )(xs, ts, wsh, small)
+
+
+def swap_kernel(along_x, a, b, send_sem, recv_sem):
+    dp, mp, x, c = place()
+    peer = 2 * (1 - x) + c if along_x else 2 * x + 1 - c
+    barrier = pltpu.get_barrier_semaphore()
+    pl.semaphore_signal(barrier, inc=1, device_id=(dp, peer), device_id_type=MESH)
+    pl.semaphore_wait(barrier, 1)
+    copy = remote(a, b, send_sem, recv_sem, dp, peer)
+    copy.start()
+    copy.wait()
+
+
+def swap(array, along_x, number):
+    return pl.pallas_call(
+        functools.partial(swap_kernel, along_x),
+        name=f"swap_{number}",
+        out_shape=jax.ShapeDtypeStruct(array.shape, array.dtype),
+        in_specs=[VM],
+        out_specs=VM,
+        scratch_shapes=[pltpu.SemaphoreType.DMA(()), pltpu.SemaphoreType.DMA(())],
+        compiler_params=pltpu.CompilerParams(collective_id=number, has_side_effects=True),
+    )(array)
+
+
+def reduce_kernel(
+    g, msg, yg, gs, msgs, back,
+    s1, r1, s2, r2, s3, r3,
+    s_msg, r_msg, s_yg, r_yg, s_a, r_a, s_b, r_b, s_c, r_c,
+):
+    dp, mp, x, c = place()
+    z, y = lax.div(dp, 2), lax.rem(dp, 2)
+    mine = x * DP + dp
+    greet_plane(dp, x, c)
+    sent = []
+
+    def go(copy):
+        copy.start()
+        sent.append(copy)
+
+    mx, dy = 2 * (1 - x) + c, 2 * z + 1 - y
+
+    def first(p):
+        for k in range(4):
+            b = (1 - x) * DP + 2 * k + 1 - y
+            s1[p, k] = g[p, b].astype(BF)
+            there = (dp, mx) if k < 2 else (dy, mp)
+            go(remote(s1.at[p, k], r1.at[p, k], s_a.at[p, k], r_a.at[p, k], *there))
+
+    def second(p):
+        for k in range(4):
+            bx, by = (1 - x) * DP + 2 * k + y, x * DP + 2 * k + 1 - y
+            landed(r1.at[p, k], r_a.at[p, k], s_a.at[p, k], dp, mp)
+            extra = r1[p, k].astype(F32)
+            gx, gy = g[p, bx], g[p, by]
+            if k < 2:
+                gy = gy + extra
+            else:
+                gx = gx + extra
+            s2[p, 0, k] = gx.astype(BF)
+            s2[p, 1, k] = gy.astype(BF)
+            go(remote(s2.at[p, 0, k], r2.at[p, 0, k], s_b.at[p, 0, k], r_b.at[p, 0, k], dp, mx))
+            go(remote(s2.at[p, 1, k], r2.at[p, 1, k], s_b.at[p, 1, k], r_b.at[p, 1, k], dy, mp))
+
+    def third(p):
+        for k in range(1, 5):
+            zz = lax.rem(z + k, 4)
+            b = x * DP + 2 * zz + y
+            for side in range(2):
+                landed(r2.at[p, side, zz], r_b.at[p, side, zz], s_b.at[p, side, 0], dp, mp)
+            total = g[p, b] + r2[p, 0, zz].astype(F32) + r2[p, 1, zz].astype(F32)
+            if k < 4:
+                s3[p, k - 1] = total.astype(BF)
+                go(remote(s3.at[p, k - 1], r3.at[p, k - 1], s_c.at[p, k - 1], r_c.at[p, k - 1], 2 * zz + y, mp))
+            else:
+                gs[p] = total
+
+    def last(p):
+        for k in range(3):
+            landed(r3.at[p, k], r_c.at[p, k], s_c.at[p, k], dp, mp)
+        gs[p] = gs[p] + (r3[p, 0].astype(F32) + r3[p, 1].astype(F32) + r3[p, 2].astype(F32))
+
+    first(2)
+    first(1)
+    pltpu.make_async_copy(msg.at[mine], msgs.at[mine], r_msg.at[mine]).start()
+    for k in range(DP):
+        for xr in range(2):
+            if k or xr:
+                d, xx = lax.rem(dp + k, DP), lax.rem(x + xr, 2)
+                go(remote(msg.at[xx * DP + d], msgs.at[mine], s_msg.at[2 * k + xr], r_msg.at[mine], d, 2 * xx + c))
+    second(2)
+    first(0)
+    second(1)
+    third(2)
+
+    pltpu.make_async_copy(yg.at[:, mp, dp], back.at[:, x, dp], r_yg.at[x, dp]).start()
+    for k in range(DP):
+        s = lax.rem(dp + k, DP)
+        for xr in range(2):
+            if k or xr:
+                m = 2 * lax.rem(x + xr, 2) + c
+                go(remote(yg.at[:, m, s], back.at[:, x, dp], s_yg.at[2 * k + xr], r_yg.at[x, dp], s, m))
+    for k in range(4):
+        j = lax.rem(z + k, 4)
+        for xr in range(2):
+            m = 2 * lax.rem(x + xr, 2) + c
+            if k or xr:
+                go(remote(yg.at[:, m, 8 + j], back.at[:, 2, dp], s_yg.at[16 + 2 * k + xr], r_yg.at[2, dp], 2 * j + x, m))
+
+    @pl.when(y == x)
+    def _():
+        pltpu.make_async_copy(yg.at[:, mp, 8 + z], back.at[:, 2, dp], r_yg.at[2, dp]).start()
+
+    @pl.when(y != x)
+    def _():
+        copy = remote(yg.at[:, mp, 8 + z], back.at[:, 2, dp], s_yg.at[16], r_yg.at[2, dp], 2 * z + x, mp)
+        copy.start()
+        copy.wait_send()
+
+    second(0)
+    third(1)
+    third(0)
+    last(2)
+    last(1)
+    last(0)
+    for j in range(16):
+        landed(msgs.at[j], r_msg.at[j], s_msg.at[0], dp, mp)
+    for m in range(3):
+        for j in range(DP):
+            landed(back.at[:, m, j], r_yg.at[m, j], s_yg.at[0], dp, mp)
+    for copy in sent:
+        copy.wait_send()
+
+
+def reduce_all(g, msg, yg):
+    dma = pltpu.SemaphoreType.DMA
+    block = (ROWS, 768)
+    return pl.pallas_call(
+        reduce_kernel,
+        name="reduce_all",
+        out_shape=(
+            jax.ShapeDtypeStruct((3, ROWS, 768), F32),
+            jax.ShapeDtypeStruct((16, 16, 128), F32),
+            jax.ShapeDtypeStruct((2, 3, DP, 64, 192), BF),
+        ),
+        in_specs=[VM] * 3,
+        out_specs=(VM,) * 3,
+        scratch_shapes=[
+            pltpu.VMEM((3, 4) + block, BF), pltpu.VMEM((3, 4) + block, BF),
+            pltpu.VMEM((3, 2, 4) + block, BF), pltpu.VMEM((3, 2, 4) + block, BF),
+            pltpu.VMEM((3, 3) + block, BF), pltpu.VMEM((3, 3) + block, BF),
+            dma((16,)), dma((16,)), dma((24,)), dma((3, DP)), dma((3, 4)), dma((3, 4)),
+            dma((3, 2, 4)), dma((3, 2, 4)), dma((3, 3)), dma((3, 3)),
+        ],
+        compiler_params=pltpu.CompilerParams(
+            collective_id=2, has_side_effects=True, vmem_limit_bytes=VMEM_LIMIT
+        ),
+    )(g, msg, yg)
+
+
+def dot(a, b, dims):
+    return lax.dot_general(a, b, (dims, ((), ())), preferred_element_type=F32)
+
+
+def per_device_compact(
+    input_stream, teacher, timestep, lengths, block_perm, table, norm_gains, shifts,
+    w_qkv, qv_bias, w_out, w_in, in_bias, w_back,
+):
+    dp, mp, x, c = place()
+    seq_len, width, quarter = input_stream.shape[1], input_stream.shape[2], teacher.shape[2]
+    score_scale = 1.0 / math.sqrt(DH)
+    valid_count = jnp.sum(lengths).astype(F32)
+    loss_factor = 3 * DP * seq_len / valid_count
+
+    order = block_perm.reshape(3, DP, DP)
+    source, local = order // DP, order % DP
+    send_index = jnp.sum(jnp.where(source == dp, local, 0), axis=2)
+    my_source = lax.dynamic_index_in_dim(source, dp, 1, keepdims=False)
+    ranks = jnp.arange(DP, dtype=jnp.int32)
+    where_block = jnp.sum(
+        jnp.where(my_source[:, None, :] == ranks[None, :, None], ranks[None, None, :], 0), axis=2
+    )
+    micro = jnp.arange(3)[:, None]
+    x_blocks = input_stream.reshape(3, DP, 64, 2, 384).transpose(3, 0, 1, 2, 4)[:, micro, send_index]
+    t_blocks = teacher.reshape(3, DP, 64, quarter)[micro, send_index]
+    half_block = lax.dynamic_index_in_dim(where_block[2].reshape(4, 2), x, 1, keepdims=False)
+    their_block = lax.dynamic_index_in_dim(where_block[2].reshape(4, 2), 1 - x, 1, keepdims=False)
+    first_block = lax.dynamic_index_in_dim(where_block, x, 0, keepdims=False)
+    length_a = lax.dynamic_index_in_dim(lengths, x * DP + dp, 0, keepdims=False)
+    length_c = lax.dynamic_index_in_dim(lengths, 2 * DP + dp, 0, keepdims=False)
+    inside = jnp.arange(64, dtype=jnp.int32)
+    live_a = ((first_block[:, None] * 64 + inside[None]) < length_a).reshape(512)
+    live_c = ((half_block[:, None] * 64 + inside[None]) < length_c).reshape(256)
+    live_d = ((their_block[:, None] * 64 + inside[None]) < length_c).reshape(256)
+    live = jnp.concatenate([live_a, live_c])
+    keys_live_c = jnp.concatenate([live_c, live_d])
+
+    wsh = jnp.stack([jnp.concatenate([w_qkv, w_out.T], axis=1), w_in, w_back.T])
+    chosen = jnp.take(table, timestep, axis=0)
+    small = jnp.zeros((32, 128), BF)
+    small = small.at[:30, :24].set(jnp.concatenate([norm_gains, shifts, chosen]))
+    small = small.at[30, :48].set(qv_bias.reshape(48)).at[31, :96].set(in_bias.reshape(96))
+
+    tok, tea, w, smalls = gather_all(x_blocks, t_blocks, wsh, small)
+
+    tokens = tok.transpose(1, 2, 0, 3).reshape(768, width).astype(F32)
+    target = tea.transpose(1, 2, 0, 3).reshape(768, width).astype(F32)
+    w = w.reshape(3, 2, width, 768)
+    vectors = smalls[:, :, :30, :24].transpose(2, 1, 0, 3).reshape(30, width).astype(F32)
+    my_small = jnp.stack(
+        [lax.dynamic_index_in_dim(smalls, 2 * k + c, 0, keepdims=False) for k in range(2)]
+    ).astype(F32)
+    bias_qv = my_small[:, :, 30, :48].reshape(2, DP, 2, 3, 8).transpose(2, 0, 3, 1, 4).reshape(2, 6, DH)
+    bias_in = my_small[:, :, 31, :96].reshape(2, DP, 6, 16).transpose(0, 2, 1, 3).reshape(2 * 768)
+    gains, shift_rows = vectors[0:2], vectors[2:6]
+    row_a = lax.dynamic_index_in_dim(vectors, 6 + x * DP + dp, 0, keepdims=False)
+    row_c = lax.dynamic_index_in_dim(vectors, 6 + 2 * DP + dp, 0, keepdims=False)
+    is_a = jnp.arange(768)[:, None] < 512
+    stream_in = tokens + jnp.where(is_a, row_a[None], row_c[None])
+    normed1, inverse1 = normalize_rows(stream_in)
+    normed_in = (normed1 * gains[0] + shift_rows[0]).astype(BF)
+    proj = w[0].transpose(1, 0, 2)[:, :, :576].reshape(width, 1152)
+    out_t = w[0].transpose(1, 0, 2)[:, :, 576:].reshape(width, 384)
+    in_w = w[1].transpose(1, 0, 2).reshape(width, 1536)
+    back_t = w[2].transpose(1, 0, 2).reshape(width, 1536)
+    projected = dot(normed_in, proj, ((1,), (0,))).reshape(768, 6, 3, DH)
+    queries = (projected[:, :, 0] + bias_qv[0]).astype(BF)
+    keys = projected[:, :, 1].astype(BF)
+    values = (projected[:, :, 2] + bias_qv[1]).astype(BF)
+    kv = jnp.concatenate([keys[512:].reshape(256, 384), values[512:].reshape(256, 384)], axis=1)
+    kv = swap(kv, True, 3)
+    keys_c = jnp.concatenate([keys[512:], kv[:, :384].reshape(256, 6, DH)])
+    values_c = jnp.concatenate([values[512:], kv[:, 384:].reshape(256, 6, DH)])
+    mixed_a, log_a = attend_rows(keys[:512], values[:512], live_a, score_scale, queries[:512])
+    mixed_c, log_c = attend_rows(keys_c, values_c, keys_live_c, score_scale, queries[512:])
+    attended = jnp.concatenate([mixed_a, mixed_c]).reshape(768, 384).astype(BF)
+    part = dot(attended, out_t, ((1,), (1,)))
+    stream_mid = stream_in + (part + swap(part, False, 4) + shift_rows[2])
+    normed2, inverse2 = normalize_rows(stream_mid)
+    normed_mid = (normed2 * gains[1] + shift_rows[1]).astype(BF)
+    pre_act = dot(normed_mid, in_w, ((1,), (0,))) + bias_in
+    gelu = functools.partial(jax.nn.gelu, approximate=True)
+    activation = gelu(pre_act).astype(BF)
+    part = dot(activation, back_t, ((1,), (1,)))
+    out = stream_mid + (part + swap(part, False, 5) + shift_rows[3])
+    residual = jnp.where(live[:, None], out - target, 0.0)
+    loss_part = jnp.sum(residual * residual)
+    grad_y = residual * loss_factor
+    grad_mlp = grad_y.astype(BF)
+    g_shift3 = jnp.sum(grad_mlp.astype(F32), axis=0)
+    g_back = dot(grad_mlp, activation, ((0,), (0,)))
+    grad_act = dot(grad_mlp, back_t, ((1,), (0,)))
+    grad_pre = jax.vjp(gelu, pre_act)[1](grad_act)[0].astype(BF)
+    g_in_bias = jnp.sum(grad_pre.astype(F32), axis=0)
+    g_in = dot(normed_mid, grad_pre, ((0,), (0,)))
+    part = dot(grad_pre, in_w, ((1,), (1,)))
+    grad_h2 = part + swap(part, False, 6)
+    g_gain1, g_shift1 = jnp.sum(grad_h2 * normed2, axis=0), jnp.sum(grad_h2, axis=0)
+    g = grad_h2 * gains[1]
+    grad_mid = grad_y + inverse2 * (
+        g - jnp.mean(g, axis=1, keepdims=True) - normed2 * jnp.mean(g * normed2, axis=1, keepdims=True)
+    )
+    grad_branch = grad_mid.astype(BF)
+    g_shift2 = jnp.sum(grad_branch.astype(F32), axis=0)
+    g_out = dot(grad_branch, attended, ((0,), (0,)))
+    grad_att = dot(grad_branch, out_t, ((1,), (0,))).astype(BF).reshape(768, 6, DH)
+    zero = jnp.zeros((512, 6, DH), F32)
+    (gk_a, gv_a), gq_a = attend_back(
+        keys[:512], values[:512], live_a, score_scale, (zero, zero), (queries[:512], grad_att[:512], log_a)
+    )
+    (gk_c, gv_c), gq_c = attend_back(
+        keys_c, values_c, keys_live_c, score_scale, (zero, zero), (queries[512:], grad_att[512:], log_c)
+    )
+    gkv = jnp.concatenate([gk_c[256:].reshape(256, 384), gv_c[256:].reshape(256, 384)], axis=1)
+    gkv = swap(gkv.astype(BF), True, 7).astype(F32)
+    gk = jnp.concatenate([gk_a, gk_c[:256] + gkv[:, :384].reshape(256, 6, DH)]).astype(BF)
+    gv = jnp.concatenate([gv_a, gv_c[:256] + gkv[:, 384:].reshape(256, 6, DH)]).astype(BF)
+    gq = jnp.concatenate([gq_a, gq_c]).astype(BF)
+    g_qb, g_vb = jnp.sum(gq.astype(F32), axis=0), jnp.sum(gv.astype(F32), axis=0)
+    rows = jnp.stack([gq, gk, gv], axis=2).reshape(768, 1152)
+    g_qkv = dot(normed_in, rows, ((0,), (0,)))
+    part = dot(rows, proj, ((1,), (1,)))
+    grad_h1 = part + swap(part, False, 8)
+    g_gain0, g_shift0 = jnp.sum(grad_h1 * normed1, axis=0), jnp.sum(grad_h1, axis=0)
+    g = grad_h1 * gains[0]
+    grad_in = grad_mid + inverse1 * (
+        g - jnp.mean(g, axis=1, keepdims=True) - normed1 * jnp.mean(g * normed1, axis=1, keepdims=True)
+    )
+    table_a, table_c = jnp.sum(grad_in[:512], axis=0), jnp.sum(grad_in[512:], axis=0)
+
+    sums = jnp.stack(
+        [g_gain0, g_gain1, g_shift0, g_shift1, g_shift2, g_shift3, table_a, table_c]
+    ).reshape(8, DP, 2, 2, 24)
+    sums = lax.dynamic_index_in_dim(sums, c, 3, keepdims=False).transpose(2, 1, 0, 3).reshape(16, 8, 24)
+    msg = jnp.zeros((16, 16, 128), F32)
+    msg = msg.at[:, :8, :24].set(sums).at[:, 8, 0].set(loss_part)
+    qvb = jnp.stack([g_qb, g_vb]).reshape(2, 2, 3, DP, 8).transpose(1, 3, 0, 2, 4).reshape(16, 48)
+    inb = g_in_bias.reshape(2, 6, DP, 16).transpose(0, 2, 1, 3).reshape(16, 96)
+    msg = msg.at[:, 9, :48].set(qvb).at[:, 10, :96].set(inb)
+    grads = jnp.stack(
+        [
+            jnp.concatenate([g_qkv.reshape(width, 2, 576), g_out.reshape(width, 2, 192)], axis=2),
+            g_in.reshape(width, 2, 768),
+            g_back.reshape(width, 2, 768),
+        ]
+    ).transpose(0, 2, 1, 3).reshape(3, 16, ROWS, 768)
+    yg = jnp.stack([out, grad_in]).astype(BF).reshape(2, 12, 64, 4, quarter).transpose(0, 3, 1, 2, 4)
+    gs, msgs, home = reduce_all(grads, msg, yg)
+
+    place_home = jnp.sum(
+        jnp.where(send_index[:, None, :] == ranks[None, :, None], ranks[None, None, :], 0), axis=2
+    )
+    home = home[:, micro, place_home].reshape(2, 3, seq_len, quarter)
+    total = jnp.sum(msgs, axis=0)
+    loss = total[8, 0] / (valid_count * width)
+    rows_a = msgs[:, 6, :24].reshape(16, 24)
+    rows_c = msgs[:DP, 7, :24] + msgs[DP:, 7, :24]
+    seq_rows = jnp.concatenate([rows_a, rows_c])
+    onehot = (jnp.arange(table.shape[0], dtype=jnp.int32)[:, None] == timestep[None, :]).astype(F32)
+    grad_table = jnp.dot(onehot, seq_rows, precision=lax.Precision.HIGHEST, preferred_element_type=F32)
+    return (
+        home[0],
+        loss,
+        home[1],
+        grad_table,
+        total[0:2, :24],
+        total[2:6, :24],
+        gs[0, :, :576],
+        total[9, :48].reshape(2, 3, 8),
+        gs[0, :, 576:].T,
+        gs[1],
+        total[10, :96].reshape(6, 16),
+        gs[2].T,
+    )
+
+
 def solution(mesh):
+    compact = mesh.shape["dp"] == 8 and mesh.shape["mp"] == 4
     return jax.shard_map(
-        per_device,
+        per_device_compact if compact else per_device,
         mesh=mesh,
         in_specs=(
             P(None, "dp", None),

time: 1330 us -> 555 us (0.42)
  waiting for transfers between devices: 518 us -> 0 us
  blocking collectives: 376 us -> 0 us
  Pallas kernels: 0 us -> 282 us
  starting transfers between devices: 76.9 us -> 0 us
  other arithmetic: 94.5 us -> 62.2 us
  matrix products: 96.7 us -> 67.9 us
  between operations: 22.4 us -> 4.99 us
    reduce_scatter x16 -> x0, waiting for transfers between devices: 356 us -> none  [the longest x1 107 us: per_device(): lax.psum_scatter(table_grad, ('dp', 'mp'), scatter_dimension=1, tiled=True)]
    all_gather x13 -> x0, blocking collectives: 296 us -> none  [the longest x1 38.2 us: per_device(): lax.all_gather(shifts, ('dp', 'mp'), axis=1, tiled=True)]
    pallas_call x0 -> x8, Pallas kernels: none -> 282 us  [the longest x1 119 us: reduce_all(): pl.pallas_call(reduce_kernel, name='reduce_all', out_shape=(jax.ShapeDtyp...]
    all_gather x5 -> x0, waiting for transfers between devices: 95.8 us -> none  [the longest x1 37.8 us: fetch_weights(): lax.all_gather(w_back, 'dp', axis=1, tiled=True)]
    unnamed x4 -> x0, blocking collectives: 79.8 us -> none
    all_to_all x12 -> x0, starting transfers between devices: 75.3 us -> none  [the longest x3 20.2 us: per_device(): lax.all_to_all(jnp.take(x_blocks, send_index, axis=0), 'dp', split_axis=0...]
    all_to_all x12 -> x0, waiting for transfers between devices: 55.3 us -> none  [the longest x3 29.8 us: per_device(): lax.all_to_all(grad_send, 'dp', split_axis=0, concat_axis=0, tiled=True)]
    dot_general x37 -> x13, matrix products: 74.4 us -> 45.9 us  [the longest x12 44.9 us: dot(): return lax.dot_general(a, b, (dims, ((), ())), preferred_element_type=F32)]
  transfers between devices with their start and end apart: 35 -> 0, of which waited for: 21 -> 0; matrix products, arithmetic and copies ran while one was open for 21% -> 0% of each run, Pallas kernels for 0% -> 0%
where the time goes in v1:
time: 555 us; the launch traced here: 549 us
  Pallas kernels  282 us (51%)
  local copies, waits for them, and re-layouts  131 us (24%)
  matrix products  67.9 us (12%)
  other arithmetic  62.2 us (11%)
    pallas_call x1, Pallas kernels, reduce_all(): pl.pallas_call(reduce_kernel, name='reduce_all', out_shape=(jax.ShapeDtyp...  119 us
    pallas_call x1, Pallas kernels, gather_all(): pl.pallas_call(gather_kernel, name='gather_all', out_shape=(jax.ShapeDtyp...  110 us
    pallas_call x6, Pallas kernels, swap(): pl.pallas_call(functools.partial(swap_kernel, along_x), name=f'swap_{numb...  54.1 us
    dot_general x12, matrix products, dot(): return lax.dot_general(a, b, (dims, ((), ())), preferred_element_type=F32)  44.9 us
    unnamed x176, local copies, waits for them, and re-layouts  24.6 us
    transpose x1, local copies, waits for them, and re-layouts, per_device_compact(): grads = jnp.stack([jnp.concatenate([g_qkv.reshape(width, 2, 576), g_out.r...  15.1 us
    transpose x1, other arithmetic, per_device_compact(): grads = jnp.stack([jnp.concatenate([g_qkv.reshape(width, 2, 576), g_out.r...  11.8 us
    another operation x4, local copies, waits for them, and re-layouts, per_device_compact(): jnp.stack([out, grad_in]).astype(BF).reshape(2, 12, 64, 4, quarter)  11.4 us

profile of v1, /device:TPU:24, one launch (start us, length us, event | category | flops | bytes accessed | tf_op | source)
XLA Modules:
  0.0 548.5 jit_solution(9302087867334020352)
XLA Ops:
  23.8 2.1 reshape.761
  25.9 2.2 copy.316
  28.1 2.4 gather_fusion
  30.5 3.3 copy.228
  33.9 109.6 %gather_all.1 = (bf16[2,12,64,384]{3,2,1,0:T(8,128)(2,1)}, bf16[4,12,64,192]{3,2,1,0:T(8,128)(2,1)}, bf16[3,16,96,768]{3,2,1,0:T(8,128)(2,1)}, bf16[4,8,32,128]{3,2,1,0:T(8,128)(2,1)}) custom-call(bf16[2,3,8,64,384]{4,3,2,1,0:T(8,128)(2,1)} %bitcast.214, bf16[3,8,64,192]{3,2,1,0:T(8,128)(2,1)} %bitcast.231, bf16[3,96,768]{2,1,0:T(8,128)(2,1)} %pad_maximum_fusion.1.wsh, ...), custom_call_target="tpu_custom_call" | custom-call | tf_op jit(solution)/shard_map/gather_all/pallas_call | solution.py:546
  143.5 5.8 %fusion.101 = (bf16[1,16,96,768]{3,2,1,0:T(8,128)(2,1)}, bf16[1,16,96,768]{3,2,1,0:T(8,128)(2,1)S(1)}, bf16[1,16,96,768]{3,2,1,0:T(8,128)(2,1)}) fusion(bf16[3,16,96,768]{3,2,1,0:T(8,128)(2,1)} %get-tuple-element.105), kind=kLoop, calls=%fused_computation.237 | loop fusion | bytes 14155776 | tf_op jit(solution)/shard_map/slice | solution.py:789
  149.3 4.4 copy.251
  153.8 2.5 copy.249
  171.6 2.5 copy.237
  174.2 2.0 slice.435
  176.2 2.8 slice.424
  179.4 2.0 copy.253
  181.4 3.3 reshape.785
  184.8 4.7 fusion.108
  192.1 10.4 %swap_3.1 = bf16[256,768]{1,0:T(8,128)(2,1)} custom-call(bf16[256,768]{1,0:T(8,128)(2,1)} %pad_maximum_fusion.2.a), custom_call_target="tpu_custom_call" | custom-call | tf_op jit(solution)/shard_map/swap_3/pallas_call | solution.py:579
  207.4 2.4 fusion.110
  214.6 2.2 fusion.41.a
  216.8 7.6 %swap_4.1 = f32[768,768]{1,0:T(8,128)} custom-call(f32[768,768]{1,0:T(8,128)} %fusion.41.a), custom_call_target="tpu_custom_call" | custom-call | tf_op jit(solution)/shard_map/swap_4/pallas_call | solution.py:579
  224.4 3.8 fusion.100
  229.9 5.1 multiply_convert_fusion.1
  236.4 3.4 fusion.111.a
  239.8 7.6 %swap_5.1 = f32[768,768]{1,0:T(8,128)} custom-call(f32[768,768]{1,0:T(8,128)} %fusion.111.a), custom_call_target="tpu_custom_call" | custom-call | tf_op jit(solution)/shard_map/swap_5/pallas_call | solution.py:579
  247.4 4.2 fusion.97
  251.6 2.3 multiply_reduce_fusion.2
  255.1 4.4 stack.94
  259.6 3.1 copy.272
  264.7 6.6 %convert_reduce_fusion = (f32[1536]{0:T(1024)S(1)}, bf16[768,1536]{1,0:T(8,128)(2,1)S(1)}) fusion(f32[768,1536]{1,0:T(8,128)} %get-tuple-element.236, f32[1536]{0:T(1024)S(1)} %add.370, bf16[768,768]{1,0:T(8,128)(2,1)S(1)} %get-tuple-element.193, bf16[768,1536]{0,1:T(8,128)(2,1)S(1)} %bitcast.238), kind=kOutput, calls=%fused_computation.23 | convolution fusion | flops 1839069696 | bytes 10629120 | tf_op jit(solution)/shard_map/dot_general | solution.py:726
  272.8 3.4 fusion.112.a
  277.6 6.1 %fusion.95 = f32[768,1536]{0,1:T(8,128)} fusion(bf16[768,1536]{1,0:T(8,128)(2,1)} %copy-done.77, f32[768,768]{1,0:T(8,128)S(1)} %get-tuple-element.199, f32[768]{0:T(1024)S(1)} %add.367, f32[768]{0:T(1024)S(1)} %mul.250, f32[768]{0:T(1024)S(1)} %add_rsqrt_fusion.1, f32[768]{0:T(1024)S(1)} %broadcast_multiply_fusion.5), kind=kOutput, calls=%fused_computation.232 | convolution fusion | flops 1814888448 | bytes 9449472 | tf_op jit(solution)/shard_map/dot_general | solution.py:726
  283.8 7.7 %swap_6.1 = f32[768,768]{1,0:T(8,128)} custom-call(f32[768,768]{1,0:T(8,128)} %fusion.112.a), custom_call_target="tpu_custom_call" | custom-call | tf_op jit(solution)/shard_map/swap_6/pallas_call | solution.py:579
  291.5 3.8 multiply_reduce_fusion.4
  300.8 4.8 fusion.26
  312.2 6.3 %fusion.114 = f32[768,1536]{0,1:T(8,128)} fusion(bf16[768,768]{1,0:T(8,128)(2,1)} %copy-done.39, bf16[768,1536]{1,0:T(8,128)(2,1)} %copy-done.76), kind=kOutput, calls=%fused_computation.250 | convolution fusion | flops 1811939328 | bytes 8257536 | tf_op jit(solution)/shard_map/dot_general | solution.py:726
  324.2 13.0 %swap_7.1 = bf16[256,768]{1,0:T(8,128)(2,1)} custom-call(bf16[256,768]{1,0:T(8,128)(2,1)} %pad_maximum_fusion.5.a), custom_call_target="tpu_custom_call" | custom-call | tf_op jit(solution)/shard_map/swap_7/pallas_call | solution.py:579
  337.3 1.9 fusion.104
  339.1 2.0 copy.258
  344.0 4.3 multiply_reduce_fusion
  355.9 3.2 fusion.115.a
  359.1 7.8 %swap_8.1 = f32[768,768]{1,0:T(8,128)} custom-call(f32[768,768]{1,0:T(8,128)} %fusion.115.a), custom_call_target="tpu_custom_call" | custom-call | tf_op jit(solution)/shard_map/swap_8/pallas_call | solution.py:579
  367.0 3.5 multiply_reduce_fusion.3
  370.6 2.1 fusion.98
  379.2 3.6 stack.95
  383.1 2.2 maximum_bitcast_fusion.2.yg
  387.2 2.4 maximum_bitcast_fusion.1
  389.6 11.8 %maximum_bitcast_fusion = f32[3,2,768,768]{2,3,1,0:T(8,128)} fusion(f32[1,768,2,768]{1,3,2,0:T(8,128)} %bitcast.224, f32[1,768,2,768]{1,3,2,0:T(8,128)} %bitcast.223, f32[1,768,2,768]{1,3,2,0:T(8,128)} %maximum_bitcast_fusion.1), kind=kLoop, calls=%fused_computation.4 | loop fusion | flops 7077888 | bytes 28311552 | tf_op jit(solution)/shard_map/transpose | solution.py:870
  401.4 15.1 %copy.264 = f32[3,2,768,768]{3,2,1,0:T(8,128)} copy(f32[3,2,768,768]{2,3,1,0:T(8,128)} %maximum_bitcast_fusion) | data formatting | bytes 28311552 | tf_op jit(solution)/shard_map/transpose | solution.py:870
  416.5 118.6 %reduce_all.1 = (f32[3,96,768]{2,1,0:T(8,128)}, f32[16,16,128]{2,1,0:T(8,128)}, bf16[2,3,8,64,192]{4,3,2,1,0:T(8,128)(2,1)}) custom-call(f32[3,16,96,768]{3,2,1,0:T(8,128)} %bitcast.207, f32[16,16,128]{2,1,0:T(8,128)} %scatter.34.msg, bf16[2,4,12,64,192]{4,3,2,1,0:T(8,128)(2,1)} %maximum_bitcast_fusion.2.yg), custom_call_target="tpu_custom_call" | custom-call | tf_op jit(solution)/shard_map/reduce_all/pallas_call | solution.py:702
  535.2 2.2 gather_fusion.3
  (353 shorter events, 104.7 us)
Async XLA Ops:
  10.3 8.1 %copy-start.72 = (pred[512]{0:T(512)(128)(4,1)}, pred[512]{0:T(512)(128)(4,1)S(1)}, u32[]{:S(2)}) copy-start(pred[512]{0:T(512)(128)(4,1)S(1)} %lt.130) | copy-start | bytes 1540
  10.3 13.4 %copy-start.22 = (bf16[3,512,768]{2,1,0:T(8,128)(2,1)S(1)}, bf16[3,512,768]{2,1,0:T(8,128)(2,1)}, u32[]{:S(2)}) copy-start(bf16[3,512,768]{2,1,0:T(8,128)(2,1)} %param.28) | copy-start | bytes 7077892
  153.8 2.5 copy-start.50
  157.8 66.6 %copy-start.54 = (f32[768]{0:T(1024)}, f32[768]{0:T(1024)S(1)}, u32[]{:S(2)}) copy-start(f32[768]{0:T(1024)S(1)} %get-tuple-element.178) | copy-start | bytes 9220
  157.8 66.6 %copy-start.56 = (f32[768]{0:T(1024)}, f32[768]{0:T(1024)S(1)}, u32[]{:S(2)}) copy-start(f32[768]{0:T(1024)S(1)} %get-tuple-element.179) | copy-start | bytes 9220
  169.1 2.5 copy-start.10
  174.2 4.8 copy-start.38
  189.6 17.8 %copy-start.15 = (bf16[768,6,64]{0,2,1:T(8,128)(2,1)}, bf16[768,6,64]{0,2,1:T(8,128)(2,1)S(1)}, u32[]{:S(2)}) copy-start(bf16[768,6,64]{0,2,1:T(8,128)(2,1)S(1)} %get-tuple-element.205) | copy-start | bytes 1769476
  189.7 21.1 %copy-start.20 = (bf16[768,6,64]{0,2,1:T(8,128)(2,1)}, bf16[768,6,64]{0,2,1:T(8,128)(2,1)S(1)}, u32[]{:S(2)}) copy-start(bf16[768,6,64]{0,2,1:T(8,128)(2,1)S(1)} %get-tuple-element.206) | copy-start | bytes 1769476
  189.7 16.5 %copy-start.36 = (bf16[256,6,64]{0,2,1:T(8,128)(2,1)}, bf16[256,6,64]{0,2,1:T(8,128)(2,1)S(1)}, u32[]{:S(2)}) copy-start(bf16[256,6,64]{0,2,1:T(8,128)(2,1)S(1)} %slice.432) | copy-start | bytes 589828
  189.7 14.2 %copy-start.75 = (pred[512]{0:T(512)(128)(4,1)S(1)}, pred[512]{0:T(512)(128)(4,1)}, u32[]{:S(2)}) copy-start(pred[512]{0:T(512)(128)(4,1)} %pad_add_fusion.1) | copy-start | bytes 1540
  191.1 13.5 %copy-start.44 = (bf16[256,6,64]{0,2,1:T(8,128)(2,1)}, bf16[256,6,64]{0,2,1:T(8,128)(2,1)S(1)}, u32[]{:S(2)}) copy-start(bf16[256,6,64]{0,2,1:T(8,128)(2,1)S(1)} %get-tuple-element.207) | copy-start | bytes 589828
  203.7 2.5 copy-start.48
  204.6 2.8 copy-start.1
  209.9 2.6 copy-start
  216.8 7.7 %copy-start.69 = (pred[768]{0:T(1024)(128)(4,1)S(1)}, pred[768]{0:T(1024)(128)(4,1)}, u32[]{:S(2)}) copy-start(pred[768]{0:T(1024)(128)(4,1)} %iota_compare_fusion.6) | copy-start | bytes 2308
  229.9 6.5 %copy-start.25 = (bf16[2,768,768]{1,2,0:T(8,128)(2,1)S(1)}, bf16[2,768,768]{1,2,0:T(8,128)(2,1)}, u32[]{:S(2)}) copy-start(bf16[2,768,768]{1,2,0:T(8,128)(2,1)} %copy.251) | copy-start | bytes 7077892
  247.4 4.2 copy-start.11
  247.4 4.2 copy-start.71
  259.6 3.1 copy-start.7
  263.0 8.3 %copy-start.39 = (bf16[768,768]{1,0:T(8,128)(2,1)}, bf16[768,768]{1,0:T(8,128)(2,1)S(1)}, u32[]{:S(2)}) copy-start(bf16[768,768]{1,0:T(8,128)(2,1)S(1)} %get-tuple-element.193) | copy-start | bytes 3538948
  264.7 8.1 %copy-start.24 = (bf16[2,768,768]{1,2,0:T(8,128)(2,1)S(1)}, bf16[2,768,768]{1,2,0:T(8,128)(2,1)}, u32[]{:S(2)}) copy-start(bf16[2,768,768]{1,2,0:T(8,128)(2,1)} %copy.249) | copy-start | bytes 7077892
  291.5 3.8 copy-start.8
  300.8 6.6 %copy-start.28 = (bf16[256,384]{0,1:T(8,128)(2,1)}, bf16[256,384]{0,1:T(8,128)(2,1)S(1)}, u32[]{:S(2)}) copy-start(bf16[256,384]{0,1:T(8,128)(2,1)S(1)} %slice.441) | copy-start | bytes 589828
  300.8 4.8 copy-start.5
  300.8 4.8 copy-start.27
  312.2 6.3 %copy-start.29 = (bf16[256,384]{0,1:T(8,128)(2,1)S(1)}, bf16[256,384]{0,1:T(8,128)(2,1)}, u32[]{:S(2)}) copy-start(bf16[256,384]{0,1:T(8,128)(2,1)} %copy-done.28) | copy-start | bytes 589828
  312.2 6.3 %copy-start.37 = (bf16[256,6,64]{0,2,1:T(8,128)(2,1)S(1)}, bf16[256,6,64]{0,2,1:T(8,128)(2,1)}, u32[]{:S(2)}) copy-start(bf16[256,6,64]{0,2,1:T(8,128)(2,1)} %copy-done.36) | copy-start | bytes 589828
  312.2 6.3 %copy-start.49 = (bf16[256,384]{0,1:T(8,128)(2,1)S(1)}, bf16[256,384]{0,1:T(8,128)(2,1)}, u32[]{:S(2)}) copy-start(bf16[256,384]{0,1:T(8,128)(2,1)} %copy-done.48) | copy-start | bytes 589828
  312.2 6.3 %copy-start.53 = (f32[6,256]{1,0:T(8,128)S(1)}, f32[6,256]{1,0:T(8,128)}, u32[]{:S(2)}) copy-start(f32[6,256]{1,0:T(8,128)} %log_add_fusion.1) | copy-start | bytes 18436
  320.7 2.8 copy-start.46
  324.2 18.8 %copy-start.19 = (f32[512,6,64]{0,2,1:T(8,128)S(1)}, f32[512,6,64]{0,2,1:T(8,128)}, u32[]{:S(2)}) copy-start(f32[512,6,64]{0,2,1:T(8,128)} %copy-done.18) | copy-start | bytes 2359300
  337.2 6.5 %copy-start.17 = (bf16[6,64,512]{2,1,0:T(8,128)(2,1)S(1)}, bf16[6,64,512]{2,1,0:T(8,128)(2,1)}, u32[]{:S(2)}) copy-start(bf16[6,64,512]{2,1,0:T(8,128)(2,1)} %fusion.26) | copy-start | bytes 1179652
  339.1 4.9 copy-start.21
  343.9 4.4 slice-start
  344.0 4.6 slice-start.1
  359.1 7.8 %copy-start.3 = (f32[96,8,2,384]{3,1,2,0:T(8,128)S(1)}, f32[96,8,2,384]{3,1,2,0:T(8,128)}, u32[]{:S(2)}) copy-start(f32[96,8,2,384]{3,1,2,0:T(8,128)} %copy.291) | copy-start | bytes 7077892
  359.1 7.8 %copy-start.55 = (f32[768]{0:T(1024)S(1)}, f32[768]{0:T(1024)}, u32[]{:S(2)}) copy-start(f32[768]{0:T(1024)} %copy-done.54) | copy-start | bytes 9220
  359.1 7.9 %copy-start.57 = (f32[768]{0:T(1024)S(1)}, f32[768]{0:T(1024)}, u32[]{:S(2)}) copy-start(f32[768]{0:T(1024)} %copy-done.56) | copy-start | bytes 9220
  359.1 7.9 %copy-start.62 = (f32[768]{0:T(1024)S(1)}, f32[768]{0:T(1024)}, u32[]{:S(2)}) copy-start(f32[768]{0:T(1024)} %div.94) | copy-start | bytes 9220
  359.1 7.9 %copy-start.63 = (f32[768]{0:T(1024)S(1)}, f32[768]{0:T(1024)}, u32[]{:S(2)}) copy-start(f32[768]{0:T(1024)} %rsqrt.22) | copy-start | bytes 9220
  359.1 7.9 %copy-start.64 = (f32[768]{0:T(1024)S(1)}, f32[768]{0:T(1024)}, u32[]{:S(2)}) copy-start(f32[768]{0:T(1024)} %mul.292) | copy-start | bytes 9220
  359.1 7.9 %copy-start.70 = (pred[768]{0:T(1024)(128)(4,1)S(1)}, pred[768]{0:T(1024)(128)(4,1)}, u32[]{:S(2)}) copy-start(pred[768]{0:T(1024)(128)(4,1)} %iota_compare_fusion.6) | copy-start | bytes 2308
  367.0 3.6 copy-start.6
  372.7 4.9 copy-start.66
  379.2 3.9 copy-start.12
  537.6 6.1 %copy-start.74 = (s32[24]{0:T(128)S(1)}, s32[24]{0:T(128)}, u32[]{:S(2)}) copy-start(s32[24]{0:T(128)} %param.30) | copy-start | bytes 292
  537.6 7.2 %copy-start.41 = (f32[3,96,768]{2,1,0:T(8,128)S(1)}, f32[3,96,768]{2,1,0:T(8,128)}, u32[]{:S(2)}) copy-start(f32[3,96,768]{2,1,0:T(8,128)} %get-tuple-element.109) | copy-start | bytes 2654212
  (32 other events, 47.4 us)

commit v2 on v1

--- a/solution.py
+++ b/solution.py
@@ -419,6 +419,7 @@
     z, y = lax.div(dp, 2), lax.rem(dp, 2)
     other = 2 * x + 1 - c
     mine = x * DP + dp
+    half = pl.ds(pl.multiple_of(384 * c, 128), 384)
     greet_plane(dp, x, c)
     sent = []
 
@@ -426,21 +427,21 @@
         copy.start()
         sent.append(copy)
 
-    pltpu.make_async_copy(xs.at[c, x, dp], tok.at[c, dp], r_tok.at[dp]).start()
+    pltpu.make_async_copy(xs.at[x, dp, :, half], tok.at[dp, :, half], r_tok.at[dp]).start()
 
     @pl.when(y == x)
     def _():
-        pltpu.make_async_copy(xs.at[c, 2, dp], tok.at[c, 8 + z], r_tok.at[8 + z]).start()
+        pltpu.make_async_copy(xs.at[2, dp, :, half], tok.at[8 + z, :, half], r_tok.at[8 + z]).start()
 
     for k in range(1, DP):
         d = lax.rem(dp + k, DP)
-        go(remote(xs.at[c, x, d], tok.at[c, dp], s_tok.at[k], r_tok.at[dp], d, mp))
+        go(remote(xs.at[x, d, :, half], tok.at[dp, :, half], s_tok.at[k], r_tok.at[dp], d, mp))
 
     @pl.when(y == x)
     def _():
         for k in range(1, DP):
             d = lax.rem(dp + k, DP)
-            remote(xs.at[c, 2, d], tok.at[c, 8 + z], s_tok.at[8 + k], r_tok.at[8 + z], d, mp).start()
+            remote(xs.at[2, d, :, half], tok.at[8 + z, :, half], s_tok.at[8 + k], r_tok.at[8 + z], d, mp).start()
 
     pltpu.make_async_copy(small, smalls.at[mp, dp], r_small.at[mine]).start()
     for k in range(DP):
@@ -502,8 +503,8 @@
     spread(2)
 
     for j in range(12):
-        landed(tok.at[c, j], r_tok.at[j], s_tok.at[0], dp, mp)
-    go(remote(tok.at[c], tok.at[c], s_core.at[0], r_core.at[0], dp, other))
+        landed(tok.at[j, :, half], r_tok.at[j], s_tok.at[0], dp, mp)
+    go(remote(tok.at[:, :, half], tok.at[:, :, half], s_core.at[0], r_core.at[0], dp, other))
     for j in range(8):
         for xx in range(2):
             m = 2 * xx + c
@@ -526,7 +527,7 @@
             b = (1 - x) * DP + 2 * k + 1 - y
             landed(w.at[p, b], r_w.at[p, b], s_w.at[p, 0], dp, mp)
     o = 1 - c
-    landed(tok.at[o], r_core.at[0], s_core.at[0], dp, mp)
+    landed(tok.at[:, :, pl.ds(pl.multiple_of(384 * o, 128), 384)], r_core.at[0], s_core.at[0], dp, mp)
     landed(smalls.at[o], r_core.at[1], s_core.at[0], dp, mp)
     landed(smalls.at[2 + o], r_core.at[2], s_core.at[0], dp, mp)
     landed(tea.at[o], r_core.at[3], s_core.at[0], dp, mp)
@@ -538,7 +539,7 @@
     def _():
         for k in range(1, DP):
             d = lax.rem(dp + k, DP)
-            remote(xs.at[c, 2, d], tok.at[c, 8 + z], s_tok.at[8 + k], r_tok.at[8 + z], d, mp).wait_send()
+            remote(xs.at[2, d, :, half], tok.at[8 + z, :, half], s_tok.at[8 + k], r_tok.at[8 + z], d, mp).wait_send()
 
 
 def gather_all(xs, ts, wsh, small):
@@ -547,7 +548,7 @@
         gather_kernel,
         name="gather_all",
         out_shape=(
-            jax.ShapeDtypeStruct((2, 12, 64, 384), BF),
+            jax.ShapeDtypeStruct((12, 64, 768), BF),
             jax.ShapeDtypeStruct((4, 12, 64, 192), BF),
             jax.ShapeDtypeStruct((3, 16, ROWS, 768), BF),
             jax.ShapeDtypeStruct((4, DP, 32, 128), BF),
@@ -562,29 +563,6 @@
             collective_id=1, has_side_effects=True, vmem_limit_bytes=VMEM_LIMIT
         ),
     )(xs, ts, wsh, small)
-
-
-def swap_kernel(along_x, a, b, send_sem, recv_sem):
-    dp, mp, x, c = place()
-    peer = 2 * (1 - x) + c if along_x else 2 * x + 1 - c
-    barrier = pltpu.get_barrier_semaphore()
-    pl.semaphore_signal(barrier, inc=1, device_id=(dp, peer), device_id_type=MESH)
-    pl.semaphore_wait(barrier, 1)
-    copy = remote(a, b, send_sem, recv_sem, dp, peer)
-    copy.start()
-    copy.wait()
-
-
-def swap(array, along_x, number):
-    return pl.pallas_call(
-        functools.partial(swap_kernel, along_x),
-        name=f"swap_{number}",
-        out_shape=jax.ShapeDtypeStruct(array.shape, array.dtype),
-        in_specs=[VM],
-        out_specs=VM,
-        scratch_shapes=[pltpu.SemaphoreType.DMA(()), pltpu.SemaphoreType.DMA(())],
-        compiler_params=pltpu.CompilerParams(collective_id=number, has_side_effects=True),
-    )(array)
 
 
 def reduce_kernel(
@@ -726,13 +704,345 @@
     return lax.dot_general(a, b, (dims, ((), ())), preferred_element_type=F32)
 
 
+T = 768
+R = 256
+LOG_SCALE = 0.125
+
+
+def nn(a, b):
+    return dot(a, b, ((1,), (0,)))
+
+
+def nt(a, b):
+    return dot(a, b, ((1,), (1,)))
+
+
+def chunk(i):
+    return pl.ds(pl.multiple_of(i * R, R), R)
+
+
+def colsum(a):
+    return jnp.sum(a, axis=0, keepdims=True)
+
+
+def wide(column_tile, width):
+    return jnp.concatenate([column_tile] * (width // 128), axis=1)
+
+
+def gelu_pair(v):
+    k = 0.7978845608028654
+    v2 = v * v
+    t = jnp.tanh(k * (v + 0.044715 * (v2 * v)))
+    half = 0.5 * (1.0 + t)
+    slope = half + 0.5 * v * ((1.0 - t * t) * (k * (1.0 + 0.134145 * v2)))
+    return v * half, slope
+
+
+def norm_back(g, normed, inverse):
+    inner = jnp.mean(g * normed, axis=1, keepdims=True)
+    return inverse * (g - jnp.mean(g, axis=1, keepdims=True) - normed * inner)
+
+
+def step_kernel(
+    tok, tea, w, vec, mask,
+    g, yg, sums,
+    nin, q_s, kv, kvt, o_t, att, n2_s, act, gy, gm, gp, x3, recv, tr, ga, dq, dkv, dkx, dkr, lse,
+    s_core, r_core, s_x, r_x,
+):
+    dp, mp, x, c = place()
+    other, across = 2 * x + 1 - c, 2 * (1 - x) + c
+    barrier = pltpu.get_barrier_semaphore()
+    for m in (other, across):
+        pl.semaphore_signal(barrier, inc=1, device_id=(dp, m), device_id_type=MESH)
+    pl.semaphore_wait(barrier, 2)
+    smid = g.at[0, 0]
+    sums[...] = jnp.zeros(sums.shape, F32)
+
+    def core(k, buffer, i):
+        rows = chunk(i)
+        return remote(
+            buffer.at[rows], recv.at[k % 2, rows], s_core.at[k, i], r_core.at[k, i], dp, other
+        )
+
+    def each(count, body):
+        def run(i, carry):
+            body(i)
+            return carry
+
+        lax.fori_loop(0, count, run, 0)
+
+    def add(row, value):
+        width = value.shape[1]
+        sums[row : row + 1, 0:width] = sums[row : row + 1, 0:width] + value
+
+    def stream(i):
+        return tok[chunk(i)].astype(F32) + jnp.where(i < 2, vec[0:1], vec[1:2])
+
+    def project(i):
+        rows = chunk(i)
+        normed, _ = normalize_rows(stream(i))
+        nb = (normed * vec[2:3] + vec[4:5]).astype(BF)
+        nin[rows] = nb
+        for xi in range(2):
+            pr = (nn(nb, w[0, xi, :, 0:640]) + vec[8 + xi : 9 + xi, 0:640]).astype(BF)
+            for j in range(3):
+                head, a = 3 * xi + j, 192 * j
+                q_s[head, rows] = jnp.concatenate([pr[:, a : a + 64], jnp.zeros((R, 64), BF)], axis=1)
+                kv[head, rows] = pr[:, a + 64 : a + 192]
+
+    project(2)
+    own, theirs = pl.ds(512, 256), pl.ds(768, 256)
+    kv_copy = remote(kv.at[:, own], kv.at[:, theirs], s_x.at[0], r_x.at[0], dp, across)
+    kv_copy.start()
+    each(2, project)
+
+    def turn(part):
+        def body(h):
+            kvt[h, :, part * 512 : part * 512 + 512] = kv[h, part * 512 : part * 512 + 512].T
+
+        each(6, body)
+
+    def attend(h, block):
+        part = block // 2
+        keys, rows = slice(part * 512, part * 512 + 512), slice(block * R, block * R + R)
+        st = nt(kv[h, keys], q_s[h, rows]) * LOG_SCALE + wide(mask[keys], R)
+        top = jnp.max(st, axis=0, keepdims=True)
+        e = jnp.exp(st - top)
+        total = colsum(e)
+        pt = (e * (1.0 / total)).astype(BF)
+        ot = nn(kvt[h, 64:128, keys], pt)
+        xi, j = lax.div(h, 3), lax.rem(h, 3)
+        o_t[xi, pl.ds(pl.multiple_of(64 + 64 * j, 64), 64), rows] = ot.astype(BF)
+        lse[h, :, rows] = top + jnp.log(total)
+
+    o_t[:, 0:64] = jnp.zeros((2, 64, T), BF)
+    turn(0)
+
+    def attend_a(h):
+        attend(h, 0)
+        attend(h, 1)
+
+    each(6, attend_a)
+    kv_copy.wait()
+    turn(1)
+    each(6, lambda h: attend(h, 2))
+
+    def out_project(i):
+        rows = chunk(i)
+        part = None
+        for xi in range(2):
+            a = o_t[xi, :, rows].T
+            att[xi, rows] = a
+            piece = nt(a, w[0, xi, :, 512:768])
+            part = piece if part is None else part + piece
+        smid[rows] = part
+        core(0, smid, i).start()
+
+    each(3, out_project)
+
+    def forward(i):
+        rows = chunk(i)
+        core(0, smid, i).wait()
+        mid = stream(i) + (smid[rows] + recv[0, rows] + vec[6:7])
+        smid[rows] = mid
+        normed, _ = normalize_rows(mid)
+        nb = (normed * vec[3:4] + vec[5:6]).astype(BF)
+        n2_s[rows] = nb
+        part = None
+        for xi in range(2):
+            value, slope = gelu_pair(nn(nb, w[1, xi]) + vec[10 + xi : 11 + xi])
+            a = value.astype(BF)
+            act[xi, rows] = a
+            g[1, xi, rows] = slope
+            piece = nt(a, w[2, xi])
+            part = piece if part is None else part + piece
+        gy[rows] = part
+        core(1, gy, i).start()
+
+    each(3, forward)
+
+    def turn_back(i):
+        rows, blocks = chunk(i), pl.ds(i * 4, 4)
+        core(1, gy, i).wait()
+        out = smid[rows] + (gy[rows] + recv[1, rows] + vec[7:8])
+        out_b = out.astype(BF)
+        for m in range(4):
+            yg[0, m, blocks] = out_b[:, 192 * m : 192 * m + 192].reshape(4, 64, 192)
+        target = jnp.concatenate([tea[m, blocks].reshape(R, 192) for m in range(4)], axis=1)
+        residual = jnp.where(wide(mask[rows], T) == 0.0, out - target.astype(F32), 0.0)
+        add(8, colsum(residual * residual))
+        grad_y = residual * vec[12:13]
+        gy[rows] = grad_y
+        gb = grad_y.astype(BF)
+        gm[rows] = gb
+        add(5, colsum(gb.astype(F32)))
+        part = None
+        for xi in range(2):
+            gpre = (nn(gb, w[2, xi]) * g[1, xi, rows]).astype(BF)
+            gp[xi, rows] = gpre
+            add(11 + xi, colsum(gpre.astype(F32)))
+            piece = nt(gpre, w[1, xi])
+            part = piece if part is None else part + piece
+        x3[rows] = part
+        core(2, x3, i).start()
+
+    each(3, turn_back)
+
+    def turn_rows(source):
+        def body(i):
+            tr[:, chunk(i)] = source[chunk(i)].T
+
+        each(3, body)
+
+    def weight_grad(p, values):
+        def body(i):
+            for xi in range(2):
+                g[p, xi, chunk(i)] = nn(tr[chunk(i)], values[xi])
+
+        each(3, body)
+
+    turn_rows(gm)
+    weight_grad(2, act)
+    turn_rows(n2_s)
+    weight_grad(1, gp)
+
+    def mid_back(i):
+        rows = chunk(i)
+        core(2, x3, i).wait()
+        grad_h = x3[rows] + recv[0, rows]
+        normed, inverse = normalize_rows(smid[rows])
+        add(1, colsum(grad_h * normed))
+        add(3, colsum(grad_h))
+        grad_mid = gy[rows] + norm_back(grad_h * vec[3:4], normed, inverse)
+        gy[rows] = grad_mid
+        gb = grad_mid.astype(BF)
+        gm[rows] = gb
+        add(4, colsum(gb.astype(F32)))
+        for xi in range(2):
+            gatt = nn(gb, w[0, xi, :, 512:768]).astype(BF)
+            for j in range(3):
+                piece = gatt[:, 64 + 64 * j : 128 + 64 * j]
+                ga[3 * xi + j, rows] = jnp.concatenate([jnp.zeros((R, 64), BF), piece], axis=1)
+
+    each(3, mid_back)
+
+    def attend_grad(h, block):
+        part = block // 2
+        keys, rows = slice(part * 512, part * 512 + 512), slice(block * R, block * R + R)
+        kvs, q, go = kv[h, keys], q_s[h, rows], ga[h, rows]
+        st = nt(kvs, q) * LOG_SCALE + wide(mask[keys], R)
+        pt = jnp.exp(st - lse[h, :, rows])
+        dpt = nt(kvs, go)
+        delta = colsum(pt * dpt)
+        dst = (pt * (dpt - delta)).astype(BF)
+        dqt = nn(kvt[h, 0:64, keys], dst) * LOG_SCALE
+        dq[h, rows] = dqt.T.astype(BF)
+        return nn(dst, q) * LOG_SCALE + nn(pt.astype(BF), go)
+
+    def grad_c(h):
+        both = attend_grad(h, 2)
+        dkv[h, 512:768] = both[0:256]
+        dkx[h] = both[256:512].astype(BF)
+
+    def grad_a(h):
+        dkv[h, 0:512] = attend_grad(h, 0) + attend_grad(h, 1)
+
+    each(6, grad_c)
+    dk_copy = remote(dkx, dkr, s_x.at[1], r_x.at[1], dp, across)
+    dk_copy.start()
+    each(6, grad_a)
+    turn_rows(gm)
+
+    def out_grad(i):
+        for xi in range(2):
+            g[0, xi, chunk(i), 512:768] = nn(tr[chunk(i)], att[xi])
+
+    each(3, out_grad)
+    dk_copy.wait()
+
+    def join(h):
+        dkv[h, 512:768] = dkv[h, 512:768] + dkr[h].astype(F32)
+
+    each(6, join)
+
+    def project_back(i):
+        rows = chunk(i)
+        part = None
+        for xi in range(2):
+            pieces = []
+            for j in range(3):
+                pieces += [dq[3 * xi + j, rows], dkv[3 * xi + j, rows].astype(BF)]
+            gr = jnp.concatenate(pieces + [jnp.zeros((R, 64), BF)], axis=1)
+            gp[xi, rows, 0:640] = gr
+            add(9 + xi if xi == 0 else 13, colsum(gr.astype(F32)))
+            piece = nt(gr, w[0, xi, :, 0:640])
+            part = piece if part is None else part + piece
+        x3[rows] = part
+        core(3, x3, i).start()
+
+    each(3, project_back)
+    turn_rows(nin)
+
+    def qkv_grad(i):
+        rows = chunk(i)
+        for xi in range(2):
+            h = nn(tr[rows], gp[xi, :, 0:640])
+            g[0, xi, rows, 0:512] = h[:, 0:512]
+            g[0, xi, rows, 512:640] = g[0, xi, rows, 512:640] + h[:, 512:640]
+
+    each(3, qkv_grad)
+
+    def in_back(i):
+        rows, blocks = chunk(i), pl.ds(i * 4, 4)
+        core(3, x3, i).wait()
+        grad_h = x3[rows] + recv[1, rows]
+        normed, inverse = normalize_rows(stream(i))
+        add(0, colsum(grad_h * normed))
+        add(2, colsum(grad_h))
+        grad_in = gy[rows] + norm_back(grad_h * vec[2:3], normed, inverse)
+        total = colsum(grad_in)
+        add(6, jnp.where(i < 2, total, 0.0))
+        add(7, jnp.where(i < 2, 0.0, total))
+        out_b = grad_in.astype(BF)
+        for m in range(4):
+            yg[1, m, blocks] = out_b[:, 192 * m : 192 * m + 192].reshape(4, 64, 192)
+
+    each(3, in_back)
+
+
+def step(tok, tea, w, vec, mask):
+    dma = pltpu.SemaphoreType.DMA
+    vm = pltpu.VMEM
+    return pl.pallas_call(
+        step_kernel,
+        name="step",
+        out_shape=(
+            jax.ShapeDtypeStruct((3, 2, T, 768), F32),
+            jax.ShapeDtypeStruct((2, 4, 12, 64, 192), BF),
+            jax.ShapeDtypeStruct((16, 768), F32),
+        ),
+        in_specs=[VM] * 5,
+        out_specs=(VM,) * 3,
+        scratch_shapes=[
+            vm((T, 768), BF), vm((6, T, 128), BF), vm((6, 1024, 128), BF), vm((6, 128, 1024), BF),
+            vm((2, R, T), BF), vm((2, T, R), BF), vm((T, 768), BF), vm((2, T, 768), BF),
+            vm((T, 768), F32), vm((T, 768), BF), vm((2, T, 768), BF), vm((T, 768), F32),
+            vm((2, T, 768), F32), vm((768, T), BF), vm((6, T, 128), BF), vm((6, T, 64), BF),
+            vm((6, T, 128), F32), vm((6, R, 128), BF), vm((6, R, 128), BF), vm((6, 1, T), F32),
+            dma((4, 3)), dma((4, 3)), dma((2,)), dma((2,)),
+        ],
+        compiler_params=pltpu.CompilerParams(
+            collective_id=3, has_side_effects=True, vmem_limit_bytes=VMEM_LIMIT
+        ),
+    )(tok, tea, w, vec, mask)
+
+
 def per_device_compact(
     input_stream, teacher, timestep, lengths, block_perm, table, norm_gains, shifts,
     w_qkv, qv_bias, w_out, w_in, in_bias, w_back,
 ):
     dp, mp, x, c = place()
     seq_len, width, quarter = input_stream.shape[1], input_stream.shape[2], teacher.shape[2]
-    score_scale = 1.0 / math.sqrt(DH)
     valid_count = jnp.sum(lengths).astype(F32)
     loss_factor = 3 * DP * seq_len / valid_count
 
@@ -745,7 +1055,7 @@
         jnp.where(my_source[:, None, :] == ranks[None, :, None], ranks[None, None, :], 0), axis=2
     )
     micro = jnp.arange(3)[:, None]
-    x_blocks = input_stream.reshape(3, DP, 64, 2, 384).transpose(3, 0, 1, 2, 4)[:, micro, send_index]
+    x_blocks = input_stream.reshape(3, DP, 64, width)[micro, send_index]
     t_blocks = teacher.reshape(3, DP, 64, quarter)[micro, send_index]
     half_block = lax.dynamic_index_in_dim(where_block[2].reshape(4, 2), x, 1, keepdims=False)
     their_block = lax.dynamic_index_in_dim(where_block[2].reshape(4, 2), 1 - x, 1, keepdims=False)
@@ -756,8 +1066,6 @@
     live_a = ((first_block[:, None] * 64 + inside[None]) < length_a).reshape(512)
     live_c = ((half_block[:, None] * 64 + inside[None]) < length_c).reshape(256)
     live_d = ((their_block[:, None] * 64 + inside[None]) < length_c).reshape(256)
-    live = jnp.concatenate([live_a, live_c])
-    keys_live_c = jnp.concatenate([live_c, live_d])
 
     wsh = jnp.stack([jnp.concatenate([w_qkv, w_out.T], axis=1), w_in, w_back.T])
     chosen = jnp.take(table, timestep, axis=0)
@@ -767,109 +1075,34 @@
 
     tok, tea, w, smalls = gather_all(x_blocks, t_blocks, wsh, small)
 
-    tokens = tok.transpose(1, 2, 0, 3).reshape(768, width).astype(F32)
-    target = tea.transpose(1, 2, 0, 3).reshape(768, width).astype(F32)
-    w = w.reshape(3, 2, width, 768)
     vectors = smalls[:, :, :30, :24].transpose(2, 1, 0, 3).reshape(30, width).astype(F32)
     my_small = jnp.stack(
         [lax.dynamic_index_in_dim(smalls, 2 * k + c, 0, keepdims=False) for k in range(2)]
     ).astype(F32)
-    bias_qv = my_small[:, :, 30, :48].reshape(2, DP, 2, 3, 8).transpose(2, 0, 3, 1, 4).reshape(2, 6, DH)
-    bias_in = my_small[:, :, 31, :96].reshape(2, DP, 6, 16).transpose(0, 2, 1, 3).reshape(2 * 768)
-    gains, shift_rows = vectors[0:2], vectors[2:6]
-    row_a = lax.dynamic_index_in_dim(vectors, 6 + x * DP + dp, 0, keepdims=False)
-    row_c = lax.dynamic_index_in_dim(vectors, 6 + 2 * DP + dp, 0, keepdims=False)
-    is_a = jnp.arange(768)[:, None] < 512
-    stream_in = tokens + jnp.where(is_a, row_a[None], row_c[None])
-    normed1, inverse1 = normalize_rows(stream_in)
-    normed_in = (normed1 * gains[0] + shift_rows[0]).astype(BF)
-    proj = w[0].transpose(1, 0, 2)[:, :, :576].reshape(width, 1152)
-    out_t = w[0].transpose(1, 0, 2)[:, :, 576:].reshape(width, 384)
-    in_w = w[1].transpose(1, 0, 2).reshape(width, 1536)
-    back_t = w[2].transpose(1, 0, 2).reshape(width, 1536)
-    projected = dot(normed_in, proj, ((1,), (0,))).reshape(768, 6, 3, DH)
-    queries = (projected[:, :, 0] + bias_qv[0]).astype(BF)
-    keys = projected[:, :, 1].astype(BF)
-    values = (projected[:, :, 2] + bias_qv[1]).astype(BF)
-    kv = jnp.concatenate([keys[512:].reshape(256, 384), values[512:].reshape(256, 384)], axis=1)
-    kv = swap(kv, True, 3)
-    keys_c = jnp.concatenate([keys[512:], kv[:, :384].reshape(256, 6, DH)])
-    values_c = jnp.concatenate([values[512:], kv[:, 384:].reshape(256, 6, DH)])
-    mixed_a, log_a = attend_rows(keys[:512], values[:512], live_a, score_scale, queries[:512])
-    mixed_c, log_c = attend_rows(keys_c, values_c, keys_live_c, score_scale, queries[512:])
-    attended = jnp.concatenate([mixed_a, mixed_c]).reshape(768, 384).astype(BF)
-    part = dot(attended, out_t, ((1,), (1,)))
-    stream_mid = stream_in + (part + swap(part, False, 4) + shift_rows[2])
-    normed2, inverse2 = normalize_rows(stream_mid)
-    normed_mid = (normed2 * gains[1] + shift_rows[1]).astype(BF)
-    pre_act = dot(normed_mid, in_w, ((1,), (0,))) + bias_in
-    gelu = functools.partial(jax.nn.gelu, approximate=True)
-    activation = gelu(pre_act).astype(BF)
-    part = dot(activation, back_t, ((1,), (1,)))
-    out = stream_mid + (part + swap(part, False, 5) + shift_rows[3])
-    residual = jnp.where(live[:, None], out - target, 0.0)
-    loss_part = jnp.sum(residual * residual)
-    grad_y = residual * loss_factor
-    grad_mlp = grad_y.astype(BF)
-    g_shift3 = jnp.sum(grad_mlp.astype(F32), axis=0)
-    g_back = dot(grad_mlp, activation, ((0,), (0,)))
-    grad_act = dot(grad_mlp, back_t, ((1,), (0,)))
-    grad_pre = jax.vjp(gelu, pre_act)[1](grad_act)[0].astype(BF)
-    g_in_bias = jnp.sum(grad_pre.astype(F32), axis=0)
-    g_in = dot(normed_mid, grad_pre, ((0,), (0,)))
-    part = dot(grad_pre, in_w, ((1,), (1,)))
-    grad_h2 = part + swap(part, False, 6)
-    g_gain1, g_shift1 = jnp.sum(grad_h2 * normed2, axis=0), jnp.sum(grad_h2, axis=0)
-    g = grad_h2 * gains[1]
-    grad_mid = grad_y + inverse2 * (
-        g - jnp.mean(g, axis=1, keepdims=True) - normed2 * jnp.mean(g * normed2, axis=1, keepdims=True)
-    )
-    grad_branch = grad_mid.astype(BF)
-    g_shift2 = jnp.sum(grad_branch.astype(F32), axis=0)
-    g_out = dot(grad_branch, attended, ((0,), (0,)))
-    grad_att = dot(grad_branch, out_t, ((1,), (0,))).astype(BF).reshape(768, 6, DH)
-    zero = jnp.zeros((512, 6, DH), F32)
-    (gk_a, gv_a), gq_a = attend_back(
-        keys[:512], values[:512], live_a, score_scale, (zero, zero), (queries[:512], grad_att[:512], log_a)
-    )
-    (gk_c, gv_c), gq_c = attend_back(
-        keys_c, values_c, keys_live_c, score_scale, (zero, zero), (queries[512:], grad_att[512:], log_c)
-    )
-    gkv = jnp.concatenate([gk_c[256:].reshape(256, 384), gv_c[256:].reshape(256, 384)], axis=1)
-    gkv = swap(gkv.astype(BF), True, 7).astype(F32)
-    gk = jnp.concatenate([gk_a, gk_c[:256] + gkv[:, :384].reshape(256, 6, DH)]).astype(BF)
-    gv = jnp.concatenate([gv_a, gv_c[:256] + gkv[:, 384:].reshape(256, 6, DH)]).astype(BF)
-    gq = jnp.concatenate([gq_a, gq_c]).astype(BF)
-    g_qb, g_vb = jnp.sum(gq.astype(F32), axis=0), jnp.sum(gv.astype(F32), axis=0)
-    rows = jnp.stack([gq, gk, gv], axis=2).reshape(768, 1152)
-    g_qkv = dot(normed_in, rows, ((0,), (0,)))
-    part = dot(rows, proj, ((1,), (1,)))
-    grad_h1 = part + swap(part, False, 8)
-    g_gain0, g_shift0 = jnp.sum(grad_h1 * normed1, axis=0), jnp.sum(grad_h1, axis=0)
-    g = grad_h1 * gains[0]
-    grad_in = grad_mid + inverse1 * (
-        g - jnp.mean(g, axis=1, keepdims=True) - normed1 * jnp.mean(g * normed1, axis=1, keepdims=True)
-    )
-    table_a, table_c = jnp.sum(grad_in[:512], axis=0), jnp.sum(grad_in[512:], axis=0)
-
-    sums = jnp.stack(
-        [g_gain0, g_gain1, g_shift0, g_shift1, g_shift2, g_shift3, table_a, table_c]
-    ).reshape(8, DP, 2, 2, 24)
-    sums = lax.dynamic_index_in_dim(sums, c, 3, keepdims=False).transpose(2, 1, 0, 3).reshape(16, 8, 24)
+    bias_qv = my_small[:, :, 30, :48].reshape(2, DP, 2, 3, 8).transpose(0, 3, 2, 1, 4).reshape(2, 3, 2, DH)
+    bias_in = my_small[:, :, 31, :96].reshape(2, DP, 6, 16).transpose(0, 2, 1, 3).reshape(2, 768)
+    bias_qkv = jnp.stack([bias_qv[:, :, 0], jnp.zeros((2, 3, DH), F32), bias_qv[:, :, 1]], axis=2)
+    bias_qkv = jnp.pad(bias_qkv.reshape(2, 576), ((0, 0), (0, 192)))
+    row_a = lax.dynamic_index_in_dim(vectors, 6 + x * DP + dp, 0)
+    row_c = lax.dynamic_index_in_dim(vectors, 6 + 2 * DP + dp, 0)
+    factor = jnp.full((4, width), loss_factor, F32)
+    vec = jnp.concatenate([row_a, row_c, vectors[0:6], bias_qkv, bias_in, factor])
+    live = jnp.concatenate([live_a, live_c, live_d])
+    mask = jnp.broadcast_to(jnp.where(live, 0.0, -1e30).astype(F32)[:, None], (1024, 128))
+    grads, yg, sums = step(tok.reshape(T, width), tea, w.reshape(3, 2, width, 768), vec, mask)
+    loss_part = jnp.sum(sums[8])
+    g_qkvb = jnp.stack([sums[9, :576], sums[13, :576]]).reshape(2, 3, 3, DH)
+    g_qvb = jnp.stack([g_qkvb[:, :, 0], g_qkvb[:, :, 2]]).reshape(2, 6, DH)
+
+    by_owner = sums[0:8].reshape(8, DP, 2, 2, 24)
+    by_owner = lax.dynamic_index_in_dim(by_owner, c, 3, keepdims=False)
+    by_owner = by_owner.transpose(2, 1, 0, 3).reshape(16, 8, 24)
     msg = jnp.zeros((16, 16, 128), F32)
-    msg = msg.at[:, :8, :24].set(sums).at[:, 8, 0].set(loss_part)
-    qvb = jnp.stack([g_qb, g_vb]).reshape(2, 2, 3, DP, 8).transpose(1, 3, 0, 2, 4).reshape(16, 48)
-    inb = g_in_bias.reshape(2, 6, DP, 16).transpose(0, 2, 1, 3).reshape(16, 96)
+    msg = msg.at[:, :8, :24].set(by_owner).at[:, 8, 0].set(loss_part)
+    qvb = g_qvb.reshape(2, 2, 3, DP, 8).transpose(1, 3, 0, 2, 4).reshape(16, 48)
+    inb = sums[11:13].reshape(2, 6, DP, 16).transpose(0, 2, 1, 3).reshape(16, 96)
     msg = msg.at[:, 9, :48].set(qvb).at[:, 10, :96].set(inb)
-    grads = jnp.stack(
-        [
-            jnp.concatenate([g_qkv.reshape(width, 2, 576), g_out.reshape(width, 2, 192)], axis=2),
-            g_in.reshape(width, 2, 768),
-            g_back.reshape(width, 2, 768),
-        ]
-    ).transpose(0, 2, 1, 3).reshape(3, 16, ROWS, 768)
-    yg = jnp.stack([out, grad_in]).astype(BF).reshape(2, 12, 64, 4, quarter).transpose(0, 3, 1, 2, 4)
-    gs, msgs, home = reduce_all(grads, msg, yg)
+    gs, msgs, home = reduce_all(grads.reshape(3, 16, ROWS, 768), msg, yg)
 
     place_home = jnp.sum(
         jnp.where(send_index[:, None, :] == ranks[None, :, None], ranks[None, None, :], 0), axis=2

time: 555 us -> 354 us (0.64)
  local copies, waits for them, and re-layouts: 131 us -> 38.1 us
  matrix products: 67.9 us -> 1.06 us
  other arithmetic: 62.2 us -> 11.9 us
  Pallas kernels: 282 us -> 298 us
    dot_general x24 -> x0, matrix products: 66.8 us -> none  [the longest x12 44.9 us: dot(): return lax.dot_general(a, b, (dims, ((), ())), preferred_element_type=F32)]
    pallas_call x6 -> x1, Pallas kernels: 54.1 us -> 72.2 us  [step(): pl.pallas_call(step_kernel, name='step', out_shape=(jax.ShapeDtypeStruct(...]
    reduce_sum x15 -> x1, other arithmetic: 18.9 us -> 1.35 us  [per_device_compact(): loss_part = jnp.sum(sums[8])]
    unnamed x176 -> x20, local copies, waits for them, and re-layouts: 24.6 us -> 7.58 us
    slice x25 -> x10, local copies, waits for them, and re-layouts: 18.2 us -> 2.53 us  [the longest x1 0.81 us: per_device_compact(): g_qkvb = jnp.stack([sums[9, :576], sums[13, :576]]).reshape(2, 3, 3, DH)]
    another operation x23 -> x10, local copies, waits for them, and re-layouts: 17.8 us -> 2.55 us  [the longest x4 11.4 us: per_device_compact(): jnp.stack([out, grad_in]).astype(BF).reshape(2, 12, 64, 4, quarter)]
    transpose x3 -> x1, local copies, waits for them, and re-layouts: 15.1 us -> 0.01 us  [per_device_compact(): my_small[:, :, 30, :48].reshape(2, DP, 2, 3, 8).transpose(0, 3, 2, 1, 4)]
    transpose x3 -> x1, other arithmetic: 14.1 us -> 0.01 us  [per_device_compact(): qvb = g_qvb.reshape(2, 2, 3, DP, 8).transpose(1, 3, 0, 2, 4).reshape(16, 48)]
where the time goes in v2:
time: 354 us; the launch traced here: 353 us
  Pallas kernels  298 us (84%)
  local copies, waits for them, and re-layouts  38.1 us (11%)
  other arithmetic  11.9 us (3%)
  between operations  3.56 us (1%)
    pallas_call x1, Pallas kernels, reduce_all(): pl.pallas_call(reduce_kernel, name='reduce_all', out_shape=(jax.ShapeDtyp...  116 us
    pallas_call x1, Pallas kernels, gather_all(): pl.pallas_call(gather_kernel, name='gather_all', out_shape=(jax.ShapeDtyp...  110 us
    pallas_call x1, Pallas kernels, step(): pl.pallas_call(step_kernel, name='step', out_shape=(jax.ShapeDtypeStruct(...  72.2 us
    unnamed x20, local copies, waits for them, and re-layouts  7.58 us

profile of v2, /device:TPU:24, one launch (start us, length us, event | category | flops | bytes accessed | tf_op | source)
XLA Modules:
  0.0 352.8 jit_solution(9352549677614820395)
XLA Ops:
  0.7 1.3 reduce_sum.60
  2.7 1.3 fusion.36
  4.0 0.8 reshape.398
  4.8 0.7 compare_and_fusion
  5.4 0.7 compare_select_fusion.2
  6.1 0.6 pad.43.clone
  6.7 0.7 copy.125
  7.4 0.6 broadcast_in_dim.50
  8.1 0.8 reshape.395
  9.6 0.7 add_compare_fusion
  10.7 0.7 add_compare_fusion.1
  12.0 0.6 reshape.431
  12.6 0.9 copy.123
  13.5 1.0 maximum_bitcast_fusion
  14.5 1.0 copy.124
  15.5 0.6 gather_fusion.2
  16.2 0.7 fusion.17
  17.2 1.8 pad_maximum_fusion.wsh
  19.0 1.0 broadcast_in_dim.54.mask
  20.0 1.5 copy.122
  21.5 1.6 gather_fusion.1
  23.1 2.2 gather_fusion
  25.3 109.6 %gather_all.1 = (bf16[12,64,768]{2,1,0:T(8,128)(2,1)}, bf16[4,12,64,192]{3,2,1,0:T(8,128)(2,1)}, bf16[3,16,96,768]{3,2,1,0:T(8,128)(2,1)}, bf16[4,8,32,128]{3,2,1,0:T(8,128)(2,1)}) custom-call(bf16[3,8,64,768]{3,2,1,0:T(8,128)(2,1)} %bitcast.72, bf16[3,8,64,192]{3,2,1,0:T(8,128)(2,1)} %bitcast.76, bf16[3,96,768]{2,1,0:T(8,128)(2,1)} %pad_maximum_fusion.wsh, ...), custom_call_target="tpu_custom_call" | custom-call | tf_op jit(solution)/shard_map/gather_all/pallas_call | solution.py:547
  134.9 0.9 constant_dynamic-slice_fusion.5
  136.2 0.7 pad_maximum_fusion.1
  137.1 1.0 convert_bitcast_fusion
  139.2 1.3 concatenate.47.vec
  140.4 72.2 %step.1 = (f32[3,2,768,768]{3,2,1,0:T(8,128)}, bf16[2,4,12,64,192]{4,3,2,1,0:T(8,128)(2,1)}, f32[16,768]{1,0:T(8,128)}) custom-call(bf16[768,768]{1,0:T(8,128)(2,1)} %bitcast.81, bf16[4,12,64,192]{3,2,1,0:T(8,128)(2,1)} %get-tuple-element.107.tea, bf16[3,2,768,768]{3,2,1,0:T(8,128)(2,1)} %bitcast.73, f32[16,768]{1,0:T(8,128)} %concatenate.47.vec, ...), custom_call_target="tpu_custom_call" | custom-call | tf_op jit(solution)/shard_map/step/pallas_call | solution.py:1016
  212.6 1.3 slice_reduce_fusion.1
  214.0 0.8 fusion.33
  214.8 0.7 slice.261
  215.5 0.7 slice.255
  216.4 0.7 broadcast.224
  217.9 0.7 scatter.29
  218.6 1.6 scatter.30
  220.2 1.6 scatter.31
  221.7 1.6 scatter.34.msg
  223.3 116.4 %reduce_all.1 = (f32[3,96,768]{2,1,0:T(8,128)}, f32[16,16,128]{2,1,0:T(8,128)}, bf16[2,3,8,64,192]{4,3,2,1,0:T(8,128)(2,1)}) custom-call(f32[3,16,96,768]{3,2,1,0:T(8,128)} %bitcast.71, f32[16,16,128]{2,1,0:T(8,128)} %scatter.34.msg, bf16[2,4,12,64,192]{4,3,2,1,0:T(8,128)(2,1)} %get-tuple-element.112.yg), custom_call_target="tpu_custom_call" | custom-call | tf_op jit(solution)/shard_map/reduce_all/pallas_call | solution.py:680
  339.7 2.2 gather_fusion.3
  342.3 1.1 copy.141
  343.4 1.1 copy.140
  346.3 0.6 slice.293
  347.0 0.6 copy.142
  347.5 0.7 reshape_squeeze.20
  348.2 1.1 fusion
  349.4 0.7 copy.143
  350.1 0.7 slice_bitcast_fusion.2
  350.8 0.8 slice_bitcast_fusion
  (76 shorter events, 6.4 us)
Async XLA Ops:
  17.2 1.8 copy-start.4
  20.0 3.1 copy-start
  136.1 3.0 copy-start.3
  342.3 2.2 copy-start.2
  342.3 5.9 %copy-start.5 = (s32[24]{0:T(128)S(1)}, s32[24]{0:T(128)}, u32[]{:S(2)}) copy-start(s32[24]{0:T(128)} %param.30) | copy-start | bytes 292
  342.3 7.0 %copy-start.1 = (f32[3,96,768]{2,1,0:T(8,128)S(1)}, f32[3,96,768]{2,1,0:T(8,128)}, u32[]{:S(2)}) copy-start(f32[3,96,768]{2,1,0:T(8,128)} %get-tuple-element.115) | copy-start | bytes 2654212

commit v3 on v2

--- a/solution.py
+++ b/solution.py
@@ -411,160 +411,6 @@
     pl.semaphore_wait(barrier, 2 * DP)
 
 
-def gather_kernel(
-    xs, ts, wsh, small, tok, tea, w, smalls,
-    s_tok, r_tok, s_tea, r_tea, s_small, r_small, s_w, r_w, s_core, r_core,
-):
-    dp, mp, x, c = place()
-    z, y = lax.div(dp, 2), lax.rem(dp, 2)
-    other = 2 * x + 1 - c
-    mine = x * DP + dp
-    half = pl.ds(pl.multiple_of(384 * c, 128), 384)
-    greet_plane(dp, x, c)
-    sent = []
-
-    def go(copy):
-        copy.start()
-        sent.append(copy)
-
-    pltpu.make_async_copy(xs.at[x, dp, :, half], tok.at[dp, :, half], r_tok.at[dp]).start()
-
-    @pl.when(y == x)
-    def _():
-        pltpu.make_async_copy(xs.at[2, dp, :, half], tok.at[8 + z, :, half], r_tok.at[8 + z]).start()
-
-    for k in range(1, DP):
-        d = lax.rem(dp + k, DP)
-        go(remote(xs.at[x, d, :, half], tok.at[dp, :, half], s_tok.at[k], r_tok.at[dp], d, mp))
-
-    @pl.when(y == x)
-    def _():
-        for k in range(1, DP):
-            d = lax.rem(dp + k, DP)
-            remote(xs.at[2, d, :, half], tok.at[8 + z, :, half], s_tok.at[8 + k], r_tok.at[8 + z], d, mp).start()
-
-    pltpu.make_async_copy(small, smalls.at[mp, dp], r_small.at[mine]).start()
-    for k in range(DP):
-        for xr in range(2):
-            if k or xr:
-                d, m = lax.rem(dp + k, DP), 2 * lax.rem(x + xr, 2) + c
-                go(remote(small, smalls.at[mp, dp], s_small.at[2 * k + xr], r_small.at[mine], d, m))
-
-    mx, dy = 2 * (1 - x) + c, 2 * z + 1 - y
-    for p in range(3):
-        pltpu.make_async_copy(wsh.at[p], w.at[p, mine], r_w.at[p, mine]).start()
-        for k in range(1, 4):
-            zz = lax.rem(z + k, 4)
-            go(remote(wsh.at[p], w.at[p, mine], s_w.at[p, k - 1], r_w.at[p, mine], 2 * zz + y, mp))
-        go(remote(wsh.at[p], w.at[p, mine], s_w.at[p, 3], r_w.at[p, mine], dp, mx))
-        go(remote(wsh.at[p], w.at[p, mine], s_w.at[p, 4], r_w.at[p, mine], dy, mp))
-
-    def spread(p):
-        for k in range(1, 4):
-            b = x * DP + 2 * lax.rem(z + k, 4) + y
-            landed(w.at[p, b], r_w.at[p, b], s_w.at[p, 0], dp, mp)
-            go(remote(w.at[p, b], w.at[p, b], s_w.at[p, 3 + 2 * k], r_w.at[p, b], dp, mx))
-            go(remote(w.at[p, b], w.at[p, b], s_w.at[p, 4 + 2 * k], r_w.at[p, b], dy, mp))
-
-    def relay(p):
-        for k in range(4):
-            bx, by = (1 - x) * DP + 2 * k + y, x * DP + 2 * k + 1 - y
-            landed(w.at[p, bx], r_w.at[p, bx], s_w.at[p, 0], dp, mp)
-            landed(w.at[p, by], r_w.at[p, by], s_w.at[p, 0], dp, mp)
-            if k < 2:
-                go(remote(w.at[p, bx], w.at[p, bx], s_w.at[p, 11 + k], r_w.at[p, bx], dy, mp))
-            else:
-                go(remote(w.at[p, by], w.at[p, by], s_w.at[p, 11 + k], r_w.at[p, by], dp, mx))
-
-    spread(0)
-
-    pltpu.make_async_copy(ts.at[x, dp], tea.at[mp, dp], r_tea.at[x, dp]).start()
-    for k in range(DP):
-        d = lax.rem(dp + k, DP)
-        for xr in range(2):
-            if k or xr:
-                xx = lax.rem(x + xr, 2)
-                go(remote(ts.at[xx, d], tea.at[mp, dp], s_tea.at[2 * k + xr], r_tea.at[x, dp], d, 2 * xx + c))
-        if k:
-            go(remote(ts.at[2, d], tea.at[mp, 8 + z], s_tea.at[16 + k], r_tea.at[x, 8 + z], d, 2 * y + c))
-
-    @pl.when(y == x)
-    def _():
-        pltpu.make_async_copy(ts.at[2, dp], tea.at[mp, 8 + z], r_tea.at[x, 8 + z]).start()
-
-    @pl.when(y != x)
-    def _():
-        copy = remote(ts.at[2, dp], tea.at[mp, 8 + z], s_tea.at[16], r_tea.at[x, 8 + z], dp, 2 * y + c)
-        copy.start()
-        copy.wait_send()
-
-    spread(1)
-    relay(0)
-    spread(2)
-
-    for j in range(12):
-        landed(tok.at[j, :, half], r_tok.at[j], s_tok.at[0], dp, mp)
-    go(remote(tok.at[:, :, half], tok.at[:, :, half], s_core.at[0], r_core.at[0], dp, other))
-    for j in range(8):
-        for xx in range(2):
-            m = 2 * xx + c
-            landed(smalls.at[m, j], r_small.at[xx * DP + j], s_small.at[0], dp, mp)
-    go(remote(smalls.at[c], smalls.at[c], s_core.at[1], r_core.at[1], dp, other))
-    go(remote(smalls.at[2 + c], smalls.at[2 + c], s_core.at[2], r_core.at[2], dp, other))
-
-    relay(1)
-    relay(2)
-
-    for xx in range(2):
-        for j in range(12):
-            landed(tea.at[2 * xx + c, j], r_tea.at[xx, j], s_tea.at[0], dp, mp)
-    go(remote(tea.at[c], tea.at[c], s_core.at[3], r_core.at[3], dp, other))
-    go(remote(tea.at[2 + c], tea.at[2 + c], s_core.at[4], r_core.at[4], dp, other))
-
-    for p in range(3):
-        landed(w.at[p, mine], r_w.at[p, mine], s_w.at[p, 0], dp, mp)
-        for k in range(4):
-            b = (1 - x) * DP + 2 * k + 1 - y
-            landed(w.at[p, b], r_w.at[p, b], s_w.at[p, 0], dp, mp)
-    o = 1 - c
-    landed(tok.at[:, :, pl.ds(pl.multiple_of(384 * o, 128), 384)], r_core.at[0], s_core.at[0], dp, mp)
-    landed(smalls.at[o], r_core.at[1], s_core.at[0], dp, mp)
-    landed(smalls.at[2 + o], r_core.at[2], s_core.at[0], dp, mp)
-    landed(tea.at[o], r_core.at[3], s_core.at[0], dp, mp)
-    landed(tea.at[2 + o], r_core.at[4], s_core.at[0], dp, mp)
-    for copy in sent:
-        copy.wait_send()
-
-    @pl.when(y == x)
-    def _():
-        for k in range(1, DP):
-            d = lax.rem(dp + k, DP)
-            remote(xs.at[2, d, :, half], tok.at[8 + z, :, half], s_tok.at[8 + k], r_tok.at[8 + z], d, mp).wait_send()
-
-
-def gather_all(xs, ts, wsh, small):
-    dma = pltpu.SemaphoreType.DMA
-    return pl.pallas_call(
-        gather_kernel,
-        name="gather_all",
-        out_shape=(
-            jax.ShapeDtypeStruct((12, 64, 768), BF),
-            jax.ShapeDtypeStruct((4, 12, 64, 192), BF),
-            jax.ShapeDtypeStruct((3, 16, ROWS, 768), BF),
-            jax.ShapeDtypeStruct((4, DP, 32, 128), BF),
-        ),
-        in_specs=[VM] * 4,
-        out_specs=(VM,) * 4,
-        scratch_shapes=[
-            dma((16,)), dma((12,)), dma((24,)), dma((2, 12)), dma((16,)), dma((16,)),
-            dma((3, 15)), dma((3, 16)), dma((5,)), dma((5,)),
-        ],
-        compiler_params=pltpu.CompilerParams(
-            collective_id=1, has_side_effects=True, vmem_limit_bytes=VMEM_LIMIT
-        ),
-    )(xs, ts, wsh, small)
-
-
 def reduce_kernel(
     g, msg, yg, gs, msgs, back,
     s1, r1, s2, r2, s3, r3,
@@ -744,18 +590,154 @@
 
 
 def step_kernel(
-    tok, tea, w, vec, mask,
+    xs, ts, wsh, small, mask, factor,
     g, yg, sums,
-    nin, q_s, kv, kvt, o_t, att, n2_s, act, gy, gm, gp, x3, recv, tr, ga, dq, dkv, dkx, dkr, lse,
+    tok, tea, w, smalls, vecs, vec, nin, q_s, kv, kvt, o_t, att, n2_s, act, gy, gm, gp, x3, recv, tr, ga, dq, dkv, dkx, dkr, lse,
     s_core, r_core, s_x, r_x,
+    s_tok, r_tok, s_tea, r_tea, s_small, r_small, s_w, r_w, s_pair, r_pair,
 ):
     dp, mp, x, c = place()
     other, across = 2 * x + 1 - c, 2 * (1 - x) + c
-    barrier = pltpu.get_barrier_semaphore()
-    for m in (other, across):
-        pl.semaphore_signal(barrier, inc=1, device_id=(dp, m), device_id_type=MESH)
-    pl.semaphore_wait(barrier, 2)
+    z, y = lax.div(dp, 2), lax.rem(dp, 2)
+    mine = x * DP + dp
+    half = pl.ds(pl.multiple_of(384 * c, 128), 384)
+    beside = 2 * z + 1 - y
+    greet_plane(dp, x, c)
+    sent = []
+
+    def go(copy):
+        copy.start()
+        sent.append(copy)
+
+    def rows64(j):
+        return pl.ds(pl.multiple_of(64 * j, 64), 64)
+
+    def weights_z(p):
+        pltpu.make_async_copy(wsh.at[p], w.at[p, mine], r_w.at[p, mine]).start()
+        for k in range(1, 4):
+            zz = lax.rem(z + k, 4)
+            go(remote(wsh.at[p], w.at[p, mine], s_w.at[p, k - 1], r_w.at[p, mine], 2 * zz + y, mp))
+
+    def weights_xy(p):
+        go(remote(wsh.at[p], w.at[p, mine], s_w.at[p, 3], r_w.at[p, mine], dp, across))
+        go(remote(wsh.at[p], w.at[p, mine], s_w.at[p, 4], r_w.at[p, mine], beside, mp))
+
+    def spread(p):
+        for k in range(1, 4):
+            b = x * DP + 2 * lax.rem(z + k, 4) + y
+            landed(w.at[p, b], r_w.at[p, b], s_w.at[p, 0], dp, mp)
+            go(remote(w.at[p, b], w.at[p, b], s_w.at[p, 3 + 2 * k], r_w.at[p, b], dp, across))
+            go(remote(w.at[p, b], w.at[p, b], s_w.at[p, 4 + 2 * k], r_w.at[p, b], beside, mp))
+
+    def relay(p):
+        for k in range(4):
+            bx, by = (1 - x) * DP + 2 * k + y, x * DP + 2 * k + 1 - y
+            landed(w.at[p, bx], r_w.at[p, bx], s_w.at[p, 0], dp, mp)
+            landed(w.at[p, by], r_w.at[p, by], s_w.at[p, 0], dp, mp)
+            if k < 2:
+                go(remote(w.at[p, bx], w.at[p, bx], s_w.at[p, 11 + k], r_w.at[p, bx], beside, mp))
+            else:
+                go(remote(w.at[p, by], w.at[p, by], s_w.at[p, 11 + k], r_w.at[p, by], dp, across))
+
+    def complete(p):
+        landed(w.at[p, mine], r_w.at[p, mine], s_w.at[p, 0], dp, mp)
+        for k in range(4):
+            b = (1 - x) * DP + 2 * k + 1 - y
+            landed(w.at[p, b], r_w.at[p, b], s_w.at[p, 0], dp, mp)
+
+    pltpu.make_async_copy(small, smalls.at[mp, dp], r_small.at[mine]).start()
+    for k in range(DP):
+        for xr in range(2):
+            if k or xr:
+                d, m = lax.rem(dp + k, DP), 2 * lax.rem(x + xr, 2) + c
+                go(remote(small, smalls.at[mp, dp], s_small.at[2 * k + xr], r_small.at[mine], d, m))
+
+    def token_copy(k, d, m_from, j):
+        return remote(
+            xs.at[m_from, d, :, half], tok.at[rows64(j), half], s_tok.at[k], r_tok.at[j], d, mp
+        )
+
+    weights_xy(0)
+    pltpu.make_async_copy(xs.at[x, dp, :, half], tok.at[rows64(dp), half], r_tok.at[dp]).start()
+    for k in range(1, DP):
+        go(token_copy(k, lax.rem(dp + k, DP), x, dp))
+
+    @pl.when(y == x)
+    def _():
+        pltpu.make_async_copy(
+            xs.at[2, dp, :, half], tok.at[rows64(8 + z), half], r_tok.at[8 + z]
+        ).start()
+        for k in range(1, DP):
+            token_copy(8 + k, lax.rem(dp + k, DP), 2, 8 + z).start()
+
+    weights_z(0)
+    weights_z(1)
+    spread(0)
+
+    for j in range(12):
+        landed(tok.at[rows64(j), half], r_tok.at[j], s_tok.at[0], dp, mp)
+    go(remote(tok.at[:, half], tok.at[:, half], s_pair.at[0], r_pair.at[0], dp, other))
+    for j in range(8):
+        for xx in range(2):
+            m = 2 * xx + c
+            landed(smalls.at[m, j], r_small.at[xx * DP + j], s_small.at[0], dp, mp)
+    go(remote(smalls.at[c], smalls.at[c], s_pair.at[1], r_pair.at[1], dp, other))
+    go(remote(smalls.at[2 + c], smalls.at[2 + c], s_pair.at[2], r_pair.at[2], dp, other))
+    relay(0)
+    weights_xy(1)
+    weights_z(2)
+
+    pltpu.make_async_copy(ts.at[x, dp], tea.at[mp, dp], r_tea.at[x, dp]).start()
+    for k in range(DP):
+        d = lax.rem(dp + k, DP)
+        for xr in range(2):
+            if k or xr:
+                xx = lax.rem(x + xr, 2)
+                go(remote(ts.at[xx, d], tea.at[mp, dp], s_tea.at[2 * k + xr], r_tea.at[x, dp], d, 2 * xx + c))
+        if k:
+            go(remote(ts.at[2, d], tea.at[mp, 8 + z], s_tea.at[16 + k], r_tea.at[x, 8 + z], d, 2 * y + c))
+
+    @pl.when(y == x)
+    def _():
+        pltpu.make_async_copy(ts.at[2, dp], tea.at[mp, 8 + z], r_tea.at[x, 8 + z]).start()
+
+    @pl.when(y != x)
+    def _():
+        remote(ts.at[2, dp], tea.at[mp, 8 + z], s_tea.at[16], r_tea.at[x, 8 + z], dp, 2 * y + c).start()
+
+    o = 1 - c
+    their_half = pl.ds(pl.multiple_of(384 * o, 128), 384)
+    landed(tok.at[:, their_half], r_pair.at[0], s_pair.at[0], dp, mp)
+    landed(smalls.at[o], r_pair.at[1], s_pair.at[0], dp, mp)
+    landed(smalls.at[2 + o], r_pair.at[2], s_pair.at[0], dp, mp)
+
+    low, high = lax.broadcasted_iota(jnp.int32, (512, 128), 0), lax.broadcasted_iota(jnp.int32, (512, 128), 1)
+    lane, quarter = low & 127, lax.shift_right_logical(low, 7)
+    pick = jnp.where((high == 24 * quarter + lane) & (lane < 24), 1.0, 0.0).astype(BF)
+    stacked = jnp.concatenate(
+        [jnp.concatenate([smalls[m, d, 0:32] for m in range(4)], axis=1) for d in range(DP)], axis=0
+    )
+    picked = nn(stacked, pick)
+    vecs[...] = jnp.concatenate([picked[32 * d : 32 * d + 32, 0:96] for d in range(DP)], axis=1)
+    vec[0:1] = vecs[pl.ds(6 + x * DP + dp, 1)]
+    vec[1:2] = vecs[pl.ds(6 + 2 * DP + dp, 1)]
+    vec[2:8] = vecs[0:6]
+    blank = jnp.zeros((1, 64), F32)
+    for xi in range(2):
+        biases = smalls[2 * xi + c, 0, 32:48].astype(F32)
+        for d in range(1, DP):
+            biases = biases + smalls[2 * xi + c, d, 32:48].astype(F32)
+        vec[10 + xi : 11 + xi] = jnp.concatenate([biases[k : k + 1] for k in range(6)], axis=1)
+        pieces = []
+        for j in range(3):
+            pieces += [biases[8 + j : 9 + j, 0:64], blank, biases[11 + j : 12 + j, 0:64]]
+        vec[8 + xi : 9 + xi] = jnp.concatenate(pieces + [blank] * 3, axis=1)
+    complete(0)
     smid = g.at[0, 0]
+
+    def half_of(p, xi, low, high):
+        return w[p, DP * xi : DP * xi + DP, :, low:high].reshape(768, high - low)
+
     sums[...] = jnp.zeros(sums.shape, F32)
 
     def core(k, buffer, i):
@@ -784,7 +766,7 @@
         nb = (normed * vec[2:3] + vec[4:5]).astype(BF)
         nin[rows] = nb
         for xi in range(2):
-            pr = (nn(nb, w[0, xi, :, 0:640]) + vec[8 + xi : 9 + xi, 0:640]).astype(BF)
+            pr = (nn(nb, half_of(0, xi, 0, 640)) + vec[8 + xi : 9 + xi, 0:640]).astype(BF)
             for j in range(3):
                 head, a = 3 * xi + j, 192 * j
                 q_s[head, rows] = jnp.concatenate([pr[:, a : a + 64], jnp.zeros((R, 64), BF)], axis=1)
@@ -795,6 +777,7 @@
     kv_copy = remote(kv.at[:, own], kv.at[:, theirs], s_x.at[0], r_x.at[0], dp, across)
     kv_copy.start()
     each(2, project)
+    spread(1)
 
     def turn(part):
         def body(h):
@@ -824,8 +807,11 @@
 
     each(6, attend_a)
     kv_copy.wait()
+    relay(1)
+    weights_xy(2)
     turn(1)
     each(6, lambda h: attend(h, 2))
+    spread(2)
 
     def out_project(i):
         rows = chunk(i)
@@ -833,12 +819,13 @@
         for xi in range(2):
             a = o_t[xi, :, rows].T
             att[xi, rows] = a
-            piece = nt(a, w[0, xi, :, 512:768])
+            piece = nt(a, half_of(0, xi, 512, 768))
             part = piece if part is None else part + piece
         smid[rows] = part
         core(0, smid, i).start()
 
     each(3, out_project)
+    complete(1)
 
     def forward(i):
         rows = chunk(i)
@@ -848,18 +835,28 @@
         normed, _ = normalize_rows(mid)
         nb = (normed * vec[3:4] + vec[5:6]).astype(BF)
         n2_s[rows] = nb
-        part = None
         for xi in range(2):
-            value, slope = gelu_pair(nn(nb, w[1, xi]) + vec[10 + xi : 11 + xi])
-            a = value.astype(BF)
-            act[xi, rows] = a
+            value, slope = gelu_pair(nn(nb, half_of(1, xi, 0, 768)) + vec[10 + xi : 11 + xi])
+            act[xi, rows] = value.astype(BF)
             g[1, xi, rows] = slope
-            piece = nt(a, w[2, xi])
-            part = piece if part is None else part + piece
-        gy[rows] = part
+
+    each(3, forward)
+    relay(2)
+    for xx in range(2):
+        for j in range(12):
+            landed(tea.at[2 * xx + c, j], r_tea.at[xx, j], s_tea.at[0], dp, mp)
+    go(remote(tea.at[c], tea.at[c], s_pair.at[3], r_pair.at[3], dp, other))
+    go(remote(tea.at[2 + c], tea.at[2 + c], s_pair.at[4], r_pair.at[4], dp, other))
+    complete(2)
+
+    def forward_out(i):
+        rows = chunk(i)
+        gy[rows] = nt(act[0, rows], half_of(2, 0, 0, 768)) + nt(act[1, rows], half_of(2, 1, 0, 768))
         core(1, gy, i).start()
 
-    each(3, forward)
+    each(3, forward_out)
+    landed(tea.at[o], r_pair.at[3], s_pair.at[0], dp, mp)
+    landed(tea.at[2 + o], r_pair.at[4], s_pair.at[0], dp, mp)
 
     def turn_back(i):
         rows, blocks = chunk(i), pl.ds(i * 4, 4)
@@ -871,17 +868,17 @@
         target = jnp.concatenate([tea[m, blocks].reshape(R, 192) for m in range(4)], axis=1)
         residual = jnp.where(wide(mask[rows], T) == 0.0, out - target.astype(F32), 0.0)
         add(8, colsum(residual * residual))
-        grad_y = residual * vec[12:13]
+        grad_y = residual * factor[0:1, 0:1]
         gy[rows] = grad_y
         gb = grad_y.astype(BF)
         gm[rows] = gb
         add(5, colsum(gb.astype(F32)))
         part = None
         for xi in range(2):
-            gpre = (nn(gb, w[2, xi]) * g[1, xi, rows]).astype(BF)
+            gpre = (nn(gb, half_of(2, xi, 0, 768)) * g[1, xi, rows]).astype(BF)
             gp[xi, rows] = gpre
             add(11 + xi, colsum(gpre.astype(F32)))
-            piece = nt(gpre, w[1, xi])
+            piece = nt(gpre, half_of(1, xi, 0, 768))
             part = piece if part is None else part + piece
         x3[rows] = part
         core(2, x3, i).start()
@@ -919,7 +916,7 @@
         gm[rows] = gb
         add(4, colsum(gb.astype(F32)))
         for xi in range(2):
-            gatt = nn(gb, w[0, xi, :, 512:768]).astype(BF)
+            gatt = nn(gb, half_of(0, xi, 512, 768)).astype(BF)
             for j in range(3):
                 piece = gatt[:, 64 + 64 * j : 128 + 64 * j]
                 ga[3 * xi + j, rows] = jnp.concatenate([jnp.zeros((R, 64), BF), piece], axis=1)
@@ -975,7 +972,7 @@
             gr = jnp.concatenate(pieces + [jnp.zeros((R, 64), BF)], axis=1)
             gp[xi, rows, 0:640] = gr
             add(9 + xi if xi == 0 else 13, colsum(gr.astype(F32)))
-            piece = nt(gr, w[0, xi, :, 0:640])
+            piece = nt(gr, half_of(0, xi, 0, 640))
             part = piece if part is None else part + piece
         x3[rows] = part
         core(3, x3, i).start()
@@ -1008,9 +1005,20 @@
             yg[1, m, blocks] = out_b[:, 192 * m : 192 * m + 192].reshape(4, 64, 192)
 
     each(3, in_back)
-
-
-def step(tok, tea, w, vec, mask):
+    for copy in sent:
+        copy.wait_send()
+
+    @pl.when(y == x)
+    def _():
+        for k in range(1, DP):
+            token_copy(8 + k, lax.rem(dp + k, DP), 2, 8 + z).wait_send()
+
+    @pl.when(y != x)
+    def _():
+        remote(ts.at[2, dp], tea.at[mp, 8 + z], s_tea.at[16], r_tea.at[x, 8 + z], dp, 2 * y + c).wait_send()
+
+
+def step(xs, ts, wsh, small, mask, factor):
     dma = pltpu.SemaphoreType.DMA
     vm = pltpu.VMEM
     return pl.pallas_call(
@@ -1021,20 +1029,24 @@
             jax.ShapeDtypeStruct((2, 4, 12, 64, 192), BF),
             jax.ShapeDtypeStruct((16, 768), F32),
         ),
-        in_specs=[VM] * 5,
+        in_specs=[pl.BlockSpec(memory_space=pl.ANY)] * 4 + [VM] * 2,
         out_specs=(VM,) * 3,
         scratch_shapes=[
+            vm((T, 768), BF), vm((4, 12, 64, 192), BF), vm((3, 16, ROWS, 768), BF),
+            vm((4, DP, 48, 128), BF), vm((32, 768), F32), vm((16, 768), F32),
             vm((T, 768), BF), vm((6, T, 128), BF), vm((6, 1024, 128), BF), vm((6, 128, 1024), BF),
             vm((2, R, T), BF), vm((2, T, R), BF), vm((T, 768), BF), vm((2, T, 768), BF),
             vm((T, 768), F32), vm((T, 768), BF), vm((2, T, 768), BF), vm((T, 768), F32),
             vm((2, T, 768), F32), vm((768, T), BF), vm((6, T, 128), BF), vm((6, T, 64), BF),
             vm((6, T, 128), F32), vm((6, R, 128), BF), vm((6, R, 128), BF), vm((6, 1, T), F32),
             dma((4, 3)), dma((4, 3)), dma((2,)), dma((2,)),
+            dma((16,)), dma((12,)), dma((24,)), dma((2, 12)), dma((16,)), dma((16,)),
+            dma((3, 15)), dma((3, 16)), dma((5,)), dma((5,)),
         ],
         compiler_params=pltpu.CompilerParams(
             collective_id=3, has_side_effects=True, vmem_limit_bytes=VMEM_LIMIT
         ),
-    )(tok, tea, w, vec, mask)
+    )(xs, ts, wsh, small, mask, factor)
 
 
 def per_device_compact(
@@ -1069,27 +1081,21 @@
 
     wsh = jnp.stack([jnp.concatenate([w_qkv, w_out.T], axis=1), w_in, w_back.T])
     chosen = jnp.take(table, timestep, axis=0)
-    small = jnp.zeros((32, 128), BF)
-    small = small.at[:30, :24].set(jnp.concatenate([norm_gains, shifts, chosen]))
-    small = small.at[30, :48].set(qv_bias.reshape(48)).at[31, :96].set(in_bias.reshape(96))
-
-    tok, tea, w, smalls = gather_all(x_blocks, t_blocks, wsh, small)
-
-    vectors = smalls[:, :, :30, :24].transpose(2, 1, 0, 3).reshape(30, width).astype(F32)
-    my_small = jnp.stack(
-        [lax.dynamic_index_in_dim(smalls, 2 * k + c, 0, keepdims=False) for k in range(2)]
-    ).astype(F32)
-    bias_qv = my_small[:, :, 30, :48].reshape(2, DP, 2, 3, 8).transpose(0, 3, 2, 1, 4).reshape(2, 3, 2, DH)
-    bias_in = my_small[:, :, 31, :96].reshape(2, DP, 6, 16).transpose(0, 2, 1, 3).reshape(2, 768)
-    bias_qkv = jnp.stack([bias_qv[:, :, 0], jnp.zeros((2, 3, DH), F32), bias_qv[:, :, 1]], axis=2)
-    bias_qkv = jnp.pad(bias_qkv.reshape(2, 576), ((0, 0), (0, 192)))
-    row_a = lax.dynamic_index_in_dim(vectors, 6 + x * DP + dp, 0)
-    row_c = lax.dynamic_index_in_dim(vectors, 6 + 2 * DP + dp, 0)
-    factor = jnp.full((4, width), loss_factor, F32)
-    vec = jnp.concatenate([row_a, row_c, vectors[0:6], bias_qkv, bias_in, factor])
+    rows = jnp.concatenate([norm_gains, shifts, chosen])
+    lanes = jnp.arange(128)
+    spread_in = jnp.where(lanes // 16 == dp, jnp.tile(in_bias, (1, 8)), 0)
+    spread_qv = jnp.where((lanes // 8 == dp)[:64], jnp.tile(qv_bias.reshape(6, 8), (1, 8)), 0)
+    small = jnp.concatenate(
+        [
+            jnp.pad(rows, ((0, 2), (0, 104))),
+            jnp.pad(spread_in, ((0, 2), (0, 0))),
+            jnp.pad(spread_qv, ((0, 2), (0, 64))),
+        ]
+    ).astype(BF)
     live = jnp.concatenate([live_a, live_c, live_d])
     mask = jnp.broadcast_to(jnp.where(live, 0.0, -1e30).astype(F32)[:, None], (1024, 128))
-    grads, yg, sums = step(tok.reshape(T, width), tea, w.reshape(3, 2, width, 768), vec, mask)
+    factor = jnp.full((8, 128), loss_factor, F32)
+    grads, yg, sums = step(x_blocks, t_blocks, wsh, small, mask, factor)
     loss_part = jnp.sum(sums[8])
     g_qkvb = jnp.stack([sums[9, :576], sums[13, :576]]).reshape(2, 3, 3, DH)
     g_qvb = jnp.stack([g_qkvb[:, :, 0], g_qkvb[:, :, 2]]).reshape(2, 6, DH)

time: 354 us -> 331 us (0.935)
  Pallas kernels: 298 us -> 281 us
  local copies, waits for them, and re-layouts: 38.1 us -> 33.5 us
    pallas_call x1 -> x0, Pallas kernels: 110 us -> none  [gather_all(): pl.pallas_call(gather_kernel, name='gather_all', out_shape=(jax.ShapeDtyp...]
    pallas_call x1, Pallas kernels: 72.2 us -> 168 us  [step(): pl.pallas_call(step_kernel, name='step', out_shape=(jax.ShapeDtypeStruct(...]
    unnamed x20 -> x16, local copies, waits for them, and re-layouts: 7.58 us -> 7.58 us
where the time goes in v3:
time: 331 us; the launch traced here: 330 us
  Pallas kernels  281 us (85%)
  local copies, waits for them, and re-layouts  33.5 us (10%)
  other arithmetic  10.8 us (3%)
  between operations  3.41 us (1%)
    pallas_call x1, Pallas kernels, step(): pl.pallas_call(step_kernel, name='step', out_shape=(jax.ShapeDtypeStruct(...  168 us
    pallas_call x1, Pallas kernels, reduce_all(): pl.pallas_call(reduce_kernel, name='reduce_all', out_shape=(jax.ShapeDtyp...  114 us
    unnamed x16, local copies, waits for them, and re-layouts  7.58 us

profile of v3, /device:TPU:24, one launch (start us, length us, event | category | flops | bytes accessed | tf_op | source)
XLA Modules:
  0.0 330.0 jit_solution(13312695885538421044)
XLA Ops:
  0.7 1.3 reduce_sum.61
  2.7 1.3 fusion.35
  4.0 0.7 compare_and_fusion
  4.6 0.7 compare_select_fusion.2
  5.3 0.7 copy.90
  6.0 0.6 broadcast_in_dim.108.factor
  6.7 0.8 reshape.296
  7.5 0.2 fusion.7
  8.0 0.2 multiply_reduce_fusion
  8.2 0.7 add_compare_fusion
  9.4 0.7 add_compare_fusion.1
  10.7 0.6 reshape.325
  11.3 0.7 tile.19
  12.0 0.9 copy.88
  12.9 1.0 maximum_bitcast_fusion
  13.9 1.2 copy.89
  15.1 0.6 gather_fusion.2
  15.8 0.7 fusion.22
  16.5 0.6 fusion.14.small
  17.1 1.8 pad_maximum_fusion.wsh
  18.9 1.0 broadcast_in_dim.107.mask
  19.9 1.3 copy.87
  21.2 1.6 gather_fusion.1
  22.8 2.2 gather_fusion
  25.0 167.5 %step.1 = (f32[3,2,768,768]{3,2,1,0:T(8,128)}, bf16[2,4,12,64,192]{4,3,2,1,0:T(8,128)(2,1)}, f32[16,768]{1,0:T(8,128)}) custom-call(bf16[3,8,64,768]{3,2,1,0:T(8,128)(2,1)} %bitcast.62, bf16[3,8,64,192]{3,2,1,0:T(8,128)(2,1)} %bitcast.68, bf16[3,96,768]{2,1,0:T(8,128)(2,1)} %pad_maximum_fusion.wsh, bf16[48,128]{1,0:T(8,128)(2,1)} %fusion.14.small, ...), custom_call_target="tpu_custom_call" | custom-call | tf_op jit(solution)/shard_map/step/pallas_call | solution.py:1024
  192.5 1.3 slice_reduce_fusion.1
  193.8 0.8 fusion.33
  194.6 0.7 slice.179
  195.4 0.7 slice.173
  196.2 0.7 broadcast.214
  197.4 0.2 reshape.299
  197.8 0.7 scatter.14
  198.4 1.6 scatter.15
  200.0 1.6 scatter.16
  201.6 1.6 scatter.19.msg
  203.1 113.8 %reduce_all.1 = (f32[3,96,768]{2,1,0:T(8,128)}, f32[16,16,128]{2,1,0:T(8,128)}, bf16[2,3,8,64,192]{4,3,2,1,0:T(8,128)(2,1)}) custom-call(f32[3,16,96,768]{3,2,1,0:T(8,128)} %bitcast.61, f32[16,16,128]{2,1,0:T(8,128)} %scatter.19.msg, bf16[2,4,12,64,192]{4,3,2,1,0:T(8,128)(2,1)} %get-tuple-element.68.yg), custom_call_target="tpu_custom_call" | custom-call | tf_op jit(solution)/shard_map/reduce_all/pallas_call | solution.py:526
  316.9 2.2 gather_fusion.3
  319.5 1.1 copy.102
  320.6 1.1 copy.101
  321.7 0.5 slice.205
  322.9 0.6 slice.207
  323.5 0.6 slice.208
  324.2 0.6 copy.103
  324.8 0.7 reshape_squeeze.12
  325.4 1.1 fusion
  326.6 0.7 copy.104
  327.3 0.7 slice_bitcast_fusion.2
  328.0 0.8 slice_bitcast_fusion
  (54 shorter events, 2.8 us)
Async XLA Ops:
  13.9 8.9 %copy-start = (bf16[3,512,768]{2,1,0:T(8,128)(2,1)S(1)}, bf16[3,512,768]{2,1,0:T(8,128)(2,1)}, u32[]{:S(2)}) copy-start(bf16[3,512,768]{2,1,0:T(8,128)(2,1)} %param.22) | copy-start | bytes 7077892
  319.3 2.4 copy-start.2
  319.3 6.1 %copy-start.3 = (s32[24]{0:T(128)S(1)}, s32[24]{0:T(128)}, u32[]{:S(2)}) copy-start(s32[24]{0:T(128)} %param.24) | copy-start | bytes 292
  319.3 7.2 %copy-start.1 = (f32[3,96,768]{2,1,0:T(8,128)S(1)}, f32[3,96,768]{2,1,0:T(8,128)}, u32[]{:S(2)}) copy-start(f32[3,96,768]{2,1,0:T(8,128)} %get-tuple-element.71) | copy-start | bytes 2654212

commit v4 on v3

--- a/solution.py
+++ b/solution.py
@@ -411,141 +411,6 @@
     pl.semaphore_wait(barrier, 2 * DP)
 
 
-def reduce_kernel(
-    g, msg, yg, gs, msgs, back,
-    s1, r1, s2, r2, s3, r3,
-    s_msg, r_msg, s_yg, r_yg, s_a, r_a, s_b, r_b, s_c, r_c,
-):
-    dp, mp, x, c = place()
-    z, y = lax.div(dp, 2), lax.rem(dp, 2)
-    mine = x * DP + dp
-    greet_plane(dp, x, c)
-    sent = []
-
-    def go(copy):
-        copy.start()
-        sent.append(copy)
-
-    mx, dy = 2 * (1 - x) + c, 2 * z + 1 - y
-
-    def first(p):
-        for k in range(4):
-            b = (1 - x) * DP + 2 * k + 1 - y
-            s1[p, k] = g[p, b].astype(BF)
-            there = (dp, mx) if k < 2 else (dy, mp)
-            go(remote(s1.at[p, k], r1.at[p, k], s_a.at[p, k], r_a.at[p, k], *there))
-
-    def second(p):
-        for k in range(4):
-            bx, by = (1 - x) * DP + 2 * k + y, x * DP + 2 * k + 1 - y
-            landed(r1.at[p, k], r_a.at[p, k], s_a.at[p, k], dp, mp)
-            extra = r1[p, k].astype(F32)
-            gx, gy = g[p, bx], g[p, by]
-            if k < 2:
-                gy = gy + extra
-            else:
-                gx = gx + extra
-            s2[p, 0, k] = gx.astype(BF)
-            s2[p, 1, k] = gy.astype(BF)
-            go(remote(s2.at[p, 0, k], r2.at[p, 0, k], s_b.at[p, 0, k], r_b.at[p, 0, k], dp, mx))
-            go(remote(s2.at[p, 1, k], r2.at[p, 1, k], s_b.at[p, 1, k], r_b.at[p, 1, k], dy, mp))
-
-    def third(p):
-        for k in range(1, 5):
-            zz = lax.rem(z + k, 4)
-            b = x * DP + 2 * zz + y
-            for side in range(2):
-                landed(r2.at[p, side, zz], r_b.at[p, side, zz], s_b.at[p, side, 0], dp, mp)
-            total = g[p, b] + r2[p, 0, zz].astype(F32) + r2[p, 1, zz].astype(F32)
-            if k < 4:
-                s3[p, k - 1] = total.astype(BF)
-                go(remote(s3.at[p, k - 1], r3.at[p, k - 1], s_c.at[p, k - 1], r_c.at[p, k - 1], 2 * zz + y, mp))
-            else:
-                gs[p] = total
-
-    def last(p):
-        for k in range(3):
-            landed(r3.at[p, k], r_c.at[p, k], s_c.at[p, k], dp, mp)
-        gs[p] = gs[p] + (r3[p, 0].astype(F32) + r3[p, 1].astype(F32) + r3[p, 2].astype(F32))
-
-    first(2)
-    first(1)
-    pltpu.make_async_copy(msg.at[mine], msgs.at[mine], r_msg.at[mine]).start()
-    for k in range(DP):
-        for xr in range(2):
-            if k or xr:
-                d, xx = lax.rem(dp + k, DP), lax.rem(x + xr, 2)
-                go(remote(msg.at[xx * DP + d], msgs.at[mine], s_msg.at[2 * k + xr], r_msg.at[mine], d, 2 * xx + c))
-    second(2)
-    first(0)
-    second(1)
-    third(2)
-
-    pltpu.make_async_copy(yg.at[:, mp, dp], back.at[:, x, dp], r_yg.at[x, dp]).start()
-    for k in range(DP):
-        s = lax.rem(dp + k, DP)
-        for xr in range(2):
-            if k or xr:
-                m = 2 * lax.rem(x + xr, 2) + c
-                go(remote(yg.at[:, m, s], back.at[:, x, dp], s_yg.at[2 * k + xr], r_yg.at[x, dp], s, m))
-    for k in range(4):
-        j = lax.rem(z + k, 4)
-        for xr in range(2):
-            m = 2 * lax.rem(x + xr, 2) + c
-            if k or xr:
-                go(remote(yg.at[:, m, 8 + j], back.at[:, 2, dp], s_yg.at[16 + 2 * k + xr], r_yg.at[2, dp], 2 * j + x, m))
-
-    @pl.when(y == x)
-    def _():
-        pltpu.make_async_copy(yg.at[:, mp, 8 + z], back.at[:, 2, dp], r_yg.at[2, dp]).start()
-
-    @pl.when(y != x)
-    def _():
-        copy = remote(yg.at[:, mp, 8 + z], back.at[:, 2, dp], s_yg.at[16], r_yg.at[2, dp], 2 * z + x, mp)
-        copy.start()
-        copy.wait_send()
-
-    second(0)
-    third(1)
-    third(0)
-    last(2)
-    last(1)
-    last(0)
-    for j in range(16):
-        landed(msgs.at[j], r_msg.at[j], s_msg.at[0], dp, mp)
-    for m in range(3):
-        for j in range(DP):
-            landed(back.at[:, m, j], r_yg.at[m, j], s_yg.at[0], dp, mp)
-    for copy in sent:
-        copy.wait_send()
-
-
-def reduce_all(g, msg, yg):
-    dma = pltpu.SemaphoreType.DMA
-    block = (ROWS, 768)
-    return pl.pallas_call(
-        reduce_kernel,
-        name="reduce_all",
-        out_shape=(
-            jax.ShapeDtypeStruct((3, ROWS, 768), F32),
-            jax.ShapeDtypeStruct((16, 16, 128), F32),
-            jax.ShapeDtypeStruct((2, 3, DP, 64, 192), BF),
-        ),
-        in_specs=[VM] * 3,
-        out_specs=(VM,) * 3,
-        scratch_shapes=[
-            pltpu.VMEM((3, 4) + block, BF), pltpu.VMEM((3, 4) + block, BF),
-            pltpu.VMEM((3, 2, 4) + block, BF), pltpu.VMEM((3, 2, 4) + block, BF),
-            pltpu.VMEM((3, 3) + block, BF), pltpu.VMEM((3, 3) + block, BF),
-            dma((16,)), dma((16,)), dma((24,)), dma((3, DP)), dma((3, 4)), dma((3, 4)),
-            dma((3, 2, 4)), dma((3, 2, 4)), dma((3, 3)), dma((3, 3)),
-        ],
-        compiler_params=pltpu.CompilerParams(
-            collective_id=2, has_side_effects=True, vmem_limit_bytes=VMEM_LIMIT
-        ),
-    )(g, msg, yg)
-
-
 def dot(a, b, dims):
     return lax.dot_general(a, b, (dims, ((), ())), preferred_element_type=F32)
 
@@ -591,10 +456,12 @@
 
 def step_kernel(
     xs, ts, wsh, small, mask, factor,
-    g, yg, sums,
-    tok, tea, w, smalls, vecs, vec, nin, q_s, kv, kvt, o_t, att, n2_s, act, gy, gm, gp, x3, recv, tr, ga, dq, dkv, dkx, dkr, lse,
+    gs, msgs, back,
+    g, yg, sums, msg, r1, r2, r3,
+    tok, tea, w, smalls, vecs, vec, nin, q_s, kv, kvt, o_t, att, n2_s, act, gy, gm, gp, x3, recv, tr, dkx, dkr, lse,
     s_core, r_core, s_x, r_x,
     s_tok, r_tok, s_tea, r_tea, s_small, r_small, s_w, r_w, s_pair, r_pair,
+    s_msg, r_msg, s_yg, r_yg, s_a, r_a, s_b, r_b, s_c, r_c,
 ):
     dp, mp, x, c = place()
     other, across = 2 * x + 1 - c, 2 * (1 - x) + c
@@ -645,6 +512,9 @@
             b = (1 - x) * DP + 2 * k + 1 - y
             landed(w.at[p, b], r_w.at[p, b], s_w.at[p, 0], dp, mp)
 
+    weights_z(0)
+    weights_xy(0)
+
     pltpu.make_async_copy(small, smalls.at[mp, dp], r_small.at[mine]).start()
     for k in range(DP):
         for xr in range(2):
@@ -657,7 +527,8 @@
             xs.at[m_from, d, :, half], tok.at[rows64(j), half], s_tok.at[k], r_tok.at[j], d, mp
         )
 
-    weights_xy(0)
+    weights_xy(1)
+    weights_xy(2)
     pltpu.make_async_copy(xs.at[x, dp, :, half], tok.at[rows64(dp), half], r_tok.at[dp]).start()
     for k in range(1, DP):
         go(token_copy(k, lax.rem(dp + k, DP), x, dp))
@@ -670,8 +541,8 @@
         for k in range(1, DP):
             token_copy(8 + k, lax.rem(dp + k, DP), 2, 8 + z).start()
 
-    weights_z(0)
     weights_z(1)
+    weights_z(2)
     spread(0)
 
     for j in range(12):
@@ -684,8 +555,6 @@
     go(remote(smalls.at[c], smalls.at[c], s_pair.at[1], r_pair.at[1], dp, other))
     go(remote(smalls.at[2 + c], smalls.at[2 + c], s_pair.at[2], r_pair.at[2], dp, other))
     relay(0)
-    weights_xy(1)
-    weights_z(2)
 
     pltpu.make_async_copy(ts.at[x, dp], tea.at[mp, dp], r_tea.at[x, dp]).start()
     for k in range(DP):
@@ -753,12 +622,83 @@
 
         lax.fori_loop(0, count, run, 0)
 
+    def lanes(h):
+        return pl.ds(pl.multiple_of(128 * h, 128), 128)
+
     def add(row, value):
         width = value.shape[1]
         sums[row : row + 1, 0:width] = sums[row : row + 1, 0:width] + value
 
     def stream(i):
         return tok[chunk(i)].astype(F32) + jnp.where(i < 2, vec[0:1], vec[1:2])
+
+    def block(p, xi, d):
+        return g.at[p, xi, pl.ds(pl.multiple_of(ROWS * d, ROWS), ROWS)]
+
+    def first(p):
+        for k in range(4):
+            w[p, k] = block(p, 1 - x, 2 * k + 1 - y)[...].astype(BF)
+            there = (dp, across) if k < 2 else (beside, mp)
+            go(remote(w.at[p, k], r1.at[p, k], s_a.at[p, k], r_a.at[p, k], *there))
+
+    def second(p):
+        for k in range(4):
+            landed(r1.at[p, k], r_a.at[p, k], s_a.at[p, k], dp, mp)
+            extra = r1[p, k].astype(F32)
+            gx, gy_ = block(p, 1 - x, 2 * k + y)[...], block(p, x, 2 * k + 1 - y)[...]
+            if k < 2:
+                gy_ = gy_ + extra
+            else:
+                gx = gx + extra
+            w[p, 4 + k] = gx.astype(BF)
+            w[p, 8 + k] = gy_.astype(BF)
+            go(remote(w.at[p, 4 + k], r2.at[p, 0, k], s_b.at[p, 0, k], r_b.at[p, 0, k], dp, across))
+            go(remote(w.at[p, 8 + k], r2.at[p, 1, k], s_b.at[p, 1, k], r_b.at[p, 1, k], beside, mp))
+
+    def third(p):
+        for k in range(1, 5):
+            zz = lax.rem(z + k, 4)
+            for side in range(2):
+                landed(r2.at[p, side, zz], r_b.at[p, side, zz], s_b.at[p, side, 0], dp, mp)
+            total = block(p, x, 2 * zz + y)[...] + r2[p, 0, zz].astype(F32) + r2[p, 1, zz].astype(F32)
+            if k < 4:
+                w[p, 11 + k] = total.astype(BF)
+                go(remote(w.at[p, 11 + k], r3.at[p, k - 1], s_c.at[p, k - 1], r_c.at[p, k - 1], 2 * zz + y, mp))
+            else:
+                gs[p] = total
+
+    def last(p):
+        for k in range(3):
+            landed(r3.at[p, k], r_c.at[p, k], s_c.at[p, k], dp, mp)
+        gs[p] = gs[p] + (r3[p, 0].astype(F32) + r3[p, 1].astype(F32) + r3[p, 2].astype(F32))
+
+    def home_copy(n):
+        return remote(
+            yg.at[n, mp, 8 + z], back.at[n, 2, dp], s_yg.at[n, 16], r_yg.at[n, 2, dp], 2 * z + x, mp
+        )
+
+    def go_home(n):
+        pltpu.make_async_copy(yg.at[n, mp, dp], back.at[n, x, dp], r_yg.at[n, x, dp]).start()
+        for k in range(DP):
+            s = lax.rem(dp + k, DP)
+            for xr in range(2):
+                if k or xr:
+                    m = 2 * lax.rem(x + xr, 2) + c
+                    go(remote(yg.at[n, m, s], back.at[n, x, dp], s_yg.at[n, 2 * k + xr], r_yg.at[n, x, dp], s, m))
+        for k in range(4):
+            j = lax.rem(z + k, 4)
+            for xr in range(2):
+                m = 2 * lax.rem(x + xr, 2) + c
+                if k or xr:
+                    go(remote(yg.at[n, m, 8 + j], back.at[n, 2, dp], s_yg.at[n, 16 + 2 * k + xr], r_yg.at[n, 2, dp], 2 * j + x, m))
+
+        @pl.when(y == x)
+        def _():
+            pltpu.make_async_copy(yg.at[n, mp, 8 + z], back.at[n, 2, dp], r_yg.at[n, 2, dp]).start()
+
+        @pl.when(y != x)
+        def _():
+            home_copy(n).start()
 
     def project(i):
         rows = chunk(i)
@@ -808,7 +748,6 @@
     each(6, attend_a)
     kv_copy.wait()
     relay(1)
-    weights_xy(2)
     turn(1)
     each(6, lambda h: attend(h, 2))
     spread(2)
@@ -900,8 +839,14 @@
 
     turn_rows(gm)
     weight_grad(2, act)
+    for copy in sent:
+        copy.wait_send()
+    sent.clear()
+    first(2)
     turn_rows(n2_s)
     weight_grad(1, gp)
+    first(1)
+    second(2)
 
     def mid_back(i):
         rows = chunk(i)
@@ -919,34 +864,37 @@
             gatt = nn(gb, half_of(0, xi, 512, 768)).astype(BF)
             for j in range(3):
                 piece = gatt[:, 64 + 64 * j : 128 + 64 * j]
-                ga[3 * xi + j, rows] = jnp.concatenate([jnp.zeros((R, 64), BF), piece], axis=1)
+                n2_s[rows, 384 * xi + 128 * j : 384 * xi + 128 * j + 128] = jnp.concatenate([jnp.zeros((R, 64), BF), piece], axis=1)
 
     each(3, mid_back)
+    go_home(0)
 
     def attend_grad(h, block):
         part = block // 2
         keys, rows = slice(part * 512, part * 512 + 512), slice(block * R, block * R + R)
-        kvs, q, go = kv[h, keys], q_s[h, rows], ga[h, rows]
+        kvs, q, go = kv[h, keys], q_s[h, rows], n2_s[rows, lanes(h)]
         st = nt(kvs, q) * LOG_SCALE + wide(mask[keys], R)
         pt = jnp.exp(st - lse[h, :, rows])
         dpt = nt(kvs, go)
         delta = colsum(pt * dpt)
         dst = (pt * (dpt - delta)).astype(BF)
         dqt = nn(kvt[h, 0:64, keys], dst) * LOG_SCALE
-        dq[h, rows] = dqt.T.astype(BF)
+        q_s[h, rows, 0:64] = dqt.T.astype(BF)
         return nn(dst, q) * LOG_SCALE + nn(pt.astype(BF), go)
 
     def grad_c(h):
         both = attend_grad(h, 2)
-        dkv[h, 512:768] = both[0:256]
+        recv[0, 512:768, lanes(h)] = both[0:256]
         dkx[h] = both[256:512].astype(BF)
 
     def grad_a(h):
-        dkv[h, 0:512] = attend_grad(h, 0) + attend_grad(h, 1)
+        recv[0, 0:512, lanes(h)] = attend_grad(h, 0) + attend_grad(h, 1)
 
     each(6, grad_c)
     dk_copy = remote(dkx, dkr, s_x.at[1], r_x.at[1], dp, across)
     dk_copy.start()
+    second(1)
+    third(2)
     each(6, grad_a)
     turn_rows(gm)
 
@@ -955,10 +903,11 @@
             g[0, xi, chunk(i), 512:768] = nn(tr[chunk(i)], att[xi])
 
     each(3, out_grad)
+    third(1)
     dk_copy.wait()
 
     def join(h):
-        dkv[h, 512:768] = dkv[h, 512:768] + dkr[h].astype(F32)
+        recv[0, 512:768, lanes(h)] = recv[0, 512:768, lanes(h)] + dkr[h].astype(F32)
 
     each(6, join)
 
@@ -968,7 +917,8 @@
         for xi in range(2):
             pieces = []
             for j in range(3):
-                pieces += [dq[3 * xi + j, rows], dkv[3 * xi + j, rows].astype(BF)]
+                at = 384 * xi + 128 * j
+                pieces += [q_s[3 * xi + j, rows, 0:64], recv[0, rows, at : at + 128].astype(BF)]
             gr = jnp.concatenate(pieces + [jnp.zeros((R, 64), BF)], axis=1)
             gp[xi, rows, 0:640] = gr
             add(9 + xi if xi == 0 else 13, colsum(gr.astype(F32)))
@@ -988,6 +938,7 @@
             g[0, xi, rows, 512:640] = g[0, xi, rows, 512:640] + h[:, 512:640]
 
     each(3, qkv_grad)
+    first(0)
 
     def in_back(i):
         rows, blocks = chunk(i), pl.ds(i * 4, 4)
@@ -1005,6 +956,42 @@
             yg[1, m, blocks] = out_b[:, 192 * m : 192 * m + 192].reshape(4, 64, 192)
 
     each(3, in_back)
+    second(0)
+
+    msg[...] = jnp.zeros(msg.shape, F32)
+    loss_row = sums[8:9, 0:128]
+    for k in range(1, 6):
+        loss_row = loss_row + sums[8:9, 128 * k : 128 * k + 128]
+    for xi in range(2):
+        bias_sums = sums[9:10] if xi == 0 else sums[13:14]
+        hidden = sums[11 + xi : 12 + xi]
+        for d in range(DP):
+            at, owner = 96 * d + 48 * xi, 8 * xi + d
+            msg[owner, 0:8, 0:24] = jnp.where(c == 0, sums[0:8, at : at + 24], sums[0:8, at + 24 : at + 48])
+            msg[owner, 8:9] = loss_row
+            for j in range(3):
+                for kind in range(2):
+                    low = 192 * j + 128 * kind
+                    msg[owner, 9 + 3 * kind + j : 10 + 3 * kind + j, 0:64] = bias_sums[:, low : low + 64]
+            for k in range(6):
+                msg[owner, 16 + k : 17 + k] = hidden[:, 128 * k : 128 * k + 128]
+    pltpu.make_async_copy(msg.at[mine], msgs.at[mine], r_msg.at[mine]).start()
+    for k in range(DP):
+        for xr in range(2):
+            if k or xr:
+                d, xx = lax.rem(dp + k, DP), lax.rem(x + xr, 2)
+                go(remote(msg.at[xx * DP + d], msgs.at[mine], s_msg.at[2 * k + xr], r_msg.at[mine], d, 2 * xx + c))
+    go_home(1)
+    third(0)
+    last(2)
+    last(1)
+    last(0)
+    for j in range(16):
+        landed(msgs.at[j], r_msg.at[j], s_msg.at[0], dp, mp)
+    for n in range(2):
+        for m in range(3):
+            for j in range(DP):
+                landed(back.at[n, m, j], r_yg.at[n, m, j], s_yg.at[n, 0], dp, mp)
     for copy in sent:
         copy.wait_send()
 
@@ -1016,32 +1003,39 @@
     @pl.when(y != x)
     def _():
         remote(ts.at[2, dp], tea.at[mp, 8 + z], s_tea.at[16], r_tea.at[x, 8 + z], dp, 2 * y + c).wait_send()
+        home_copy(0).wait_send()
+        home_copy(1).wait_send()
 
 
 def step(xs, ts, wsh, small, mask, factor):
     dma = pltpu.SemaphoreType.DMA
     vm = pltpu.VMEM
+    block = (ROWS, 768)
     return pl.pallas_call(
         step_kernel,
         name="step",
         out_shape=(
-            jax.ShapeDtypeStruct((3, 2, T, 768), F32),
-            jax.ShapeDtypeStruct((2, 4, 12, 64, 192), BF),
-            jax.ShapeDtypeStruct((16, 768), F32),
+            jax.ShapeDtypeStruct((3, ROWS, 768), F32),
+            jax.ShapeDtypeStruct((16, 24, 128), F32),
+            jax.ShapeDtypeStruct((2, 3, DP, 64, 192), BF),
         ),
         in_specs=[pl.BlockSpec(memory_space=pl.ANY)] * 4 + [VM] * 2,
-        out_specs=(VM,) * 3,
+        out_specs=(VM, VM, pl.BlockSpec(memory_space=pl.ANY)),
         scratch_shapes=[
-            vm((T, 768), BF), vm((4, 12, 64, 192), BF), vm((3, 16, ROWS, 768), BF),
+            vm((3, 2, T, 768), F32), vm((2, 4, 12, 64, 192), BF), vm((16, 768), F32), vm((16, 24, 128), F32),
+            vm((3, 4) + block, BF), vm((3, 2, 4) + block, BF), vm((3, 3) + block, BF),
+            vm((T, 768), BF), vm((4, 12, 64, 192), BF), vm((3, 16) + block, BF),
             vm((4, DP, 48, 128), BF), vm((32, 768), F32), vm((16, 768), F32),
             vm((T, 768), BF), vm((6, T, 128), BF), vm((6, 1024, 128), BF), vm((6, 128, 1024), BF),
             vm((2, R, T), BF), vm((2, T, R), BF), vm((T, 768), BF), vm((2, T, 768), BF),
             vm((T, 768), F32), vm((T, 768), BF), vm((2, T, 768), BF), vm((T, 768), F32),
-            vm((2, T, 768), F32), vm((768, T), BF), vm((6, T, 128), BF), vm((6, T, 64), BF),
-            vm((6, T, 128), F32), vm((6, R, 128), BF), vm((6, R, 128), BF), vm((6, 1, T), F32),
+            vm((2, T, 768), F32), vm((768, T), BF), vm((6, R, 128), BF), vm((6, R, 128), BF),
+            vm((6, 1, T), F32),
             dma((4, 3)), dma((4, 3)), dma((2,)), dma((2,)),
             dma((16,)), dma((12,)), dma((24,)), dma((2, 12)), dma((16,)), dma((16,)),
             dma((3, 15)), dma((3, 16)), dma((5,)), dma((5,)),
+            dma((16,)), dma((16,)), dma((2, 24)), dma((2, 3, DP)), dma((3, 4)), dma((3, 4)),
+            dma((3, 2, 4)), dma((3, 2, 4)), dma((3, 3)), dma((3, 3)),
         ],
         compiler_params=pltpu.CompilerParams(
             collective_id=3, has_side_effects=True, vmem_limit_bytes=VMEM_LIMIT
@@ -1095,27 +1089,14 @@
     live = jnp.concatenate([live_a, live_c, live_d])
     mask = jnp.broadcast_to(jnp.where(live, 0.0, -1e30).astype(F32)[:, None], (1024, 128))
     factor = jnp.full((8, 128), loss_factor, F32)
-    grads, yg, sums = step(x_blocks, t_blocks, wsh, small, mask, factor)
-    loss_part = jnp.sum(sums[8])
-    g_qkvb = jnp.stack([sums[9, :576], sums[13, :576]]).reshape(2, 3, 3, DH)
-    g_qvb = jnp.stack([g_qkvb[:, :, 0], g_qkvb[:, :, 2]]).reshape(2, 6, DH)
-
-    by_owner = sums[0:8].reshape(8, DP, 2, 2, 24)
-    by_owner = lax.dynamic_index_in_dim(by_owner, c, 3, keepdims=False)
-    by_owner = by_owner.transpose(2, 1, 0, 3).reshape(16, 8, 24)
-    msg = jnp.zeros((16, 16, 128), F32)
-    msg = msg.at[:, :8, :24].set(by_owner).at[:, 8, 0].set(loss_part)
-    qvb = g_qvb.reshape(2, 2, 3, DP, 8).transpose(1, 3, 0, 2, 4).reshape(16, 48)
-    inb = sums[11:13].reshape(2, 6, DP, 16).transpose(0, 2, 1, 3).reshape(16, 96)
-    msg = msg.at[:, 9, :48].set(qvb).at[:, 10, :96].set(inb)
-    gs, msgs, home = reduce_all(grads.reshape(3, 16, ROWS, 768), msg, yg)
+    gs, msgs, home = step(x_blocks, t_blocks, wsh, small, mask, factor)
 
     place_home = jnp.sum(
         jnp.where(send_index[:, None, :] == ranks[None, :, None], ranks[None, None, :], 0), axis=2
     )
     home = home[:, micro, place_home].reshape(2, 3, seq_len, quarter)
     total = jnp.sum(msgs, axis=0)
-    loss = total[8, 0] / (valid_count * width)
+    loss = jnp.sum(total[8]) / (valid_count * width)
     rows_a = msgs[:, 6, :24].reshape(16, 24)
     rows_c = msgs[:DP, 7, :24] + msgs[DP:, 7, :24]
     seq_rows = jnp.concatenate([rows_a, rows_c])
@@ -1129,10 +1110,10 @@
         total[0:2, :24],
         total[2:6, :24],
         gs[0, :, :576],
-        total[9, :48].reshape(2, 3, 8),
+        lax.dynamic_slice(total, (9, 8 * dp), (6, 8)).reshape(2, 3, 8),
         gs[0, :, 576:].T,
         gs[1],
-        total[10, :96].reshape(6, 16),
+        lax.dynamic_slice(total, (16, 16 * dp), (6, 16)),
         gs[2].T,
     )
 

time: 331 us -> 275 us (0.83)
  Pallas kernels: 281 us -> 237 us
  local copies, waits for them, and re-layouts: 33.5 us -> 23.8 us
    pallas_call x1 -> x0, Pallas kernels: 114 us -> none  [reduce_all(): pl.pallas_call(reduce_kernel, name='reduce_all', out_shape=(jax.ShapeDtyp...]
    pallas_call x1, Pallas kernels: 168 us -> 237 us  [step(): pl.pallas_call(step_kernel, name='step', out_shape=(jax.ShapeDtypeStruct(...]
    scatter x4 -> x0, local copies, waits for them, and re-layouts: 5.37 us -> none  [the longest x2 3.14 us: per_device_compact(): msg = msg.at[:, 9, :48].set(qvb).at[:, 10, :96].set(inb)]
where the time goes in v4:
time: 275 us
  Pallas kernels  237 us (86%)
  local copies, waits for them, and re-layouts  23.8 us (9%)
  other arithmetic  10 us (4%)
  between operations  3.3 us (1%)
    pallas_call x1, Pallas kernels, step(): pl.pallas_call(step_kernel, name='step', out_shape=(jax.ShapeDtypeStruct(...  237 us
    unnamed x16, local copies, waits for them, and re-layouts  7.57 us

profile of v4, /device:TPU:24, one launch (start us, length us, event | category | flops | bytes accessed | tf_op | source)
XLA Modules:
  0.0 274.7 jit_solution(17023739846965624775)
XLA Ops:
  0.7 1.3 reduce_sum.61
  2.7 1.3 fusion.33
  4.0 0.7 compare_and_fusion
  4.6 0.7 compare_select_fusion.2
  5.3 0.7 copy.74
  6.0 0.6 broadcast_in_dim.106.factor
  6.6 0.1 tile.23
  6.7 0.8 reshape.142
  7.5 0.2 fusion.7
  7.8 0.2 select_reduce_fusion.1
  8.0 0.2 multiply_reduce_fusion
  8.2 0.7 add_compare_fusion
  9.0 0.1 lt.102
  9.1 0.2 multiply_reduce_fusion.2
  9.3 0.7 add_compare_fusion.1
  10.1 0.1 lt.109
  10.2 0.1 lt.106
  10.3 0.1 reshape.145
  10.3 0.2 select_reduce_fusion
  10.6 0.6 reshape.165
  11.3 0.7 tile.19
  12.0 0.1 tile.20
  12.1 0.9 copy.72
  12.9 1.0 maximum_bitcast_fusion
  13.9 1.0 copy.73
  15.0 0.6 gather_fusion.2
  15.6 0.7 fusion.22
  16.3 0.6 fusion.14.small
  16.9 1.8 pad_maximum_fusion.wsh
  18.7 1.0 broadcast_in_dim.105.mask
  19.7 1.5 copy.71
  21.2 1.6 gather_fusion.1
  22.8 2.2 gather_fusion
  25.0 236.6 %step.1 = (f32[3,96,768]{2,1,0:T(8,128)}, f32[16,24,128]{2,1,0:T(8,128)}, bf16[2,3,8,64,192]{4,3,2,1,0:T(8,128)(2,1)}) custom-call(bf16[3,8,64,768]{3,2,1,0:T(8,128)(2,1)} %bitcast.44, bf16[3,8,64,192]{3,2,1,0:T(8,128)(2,1)} %bitcast.50, bf16[3,96,768]{2,1,0:T(8,128)(2,1)} %pad_maximum_fusion.wsh, bf16[48,128]{1,0:T(8,128)(2,1)} %fusion.14.small, ...), custom_call_target="tpu_custom_call" | custom-call | tf_op jit(solution)/shard_map/step/pallas_call | solution.py:1014
  261.6 2.2 gather_fusion.3
  263.8 0.2 copy.105
  263.9 0.2 fusion.32
  264.2 1.1 copy.79
  265.2 1.1 copy.78
  266.4 0.6 slice_reduce_fusion.1
  267.6 0.6 slice.70
  268.2 0.6 slice.71
  268.8 0.7 constant_dynamic-slice_fusion.1
  269.5 0.6 copy.80
  270.1 1.1 fusion
  271.3 0.7 copy.81
  272.0 0.7 slice_bitcast_fusion.2
  272.7 0.8 slice_bitcast_fusion
  (28 shorter events, 0.6 us)
Async XLA Ops:
  19.7 3.1 %copy-start = (bf16[3,512,768]{2,1,0:T(8,128)(2,1)S(1)}, bf16[3,512,768]{2,1,0:T(8,128)(2,1)}, u32[]{:S(2)}) copy-start(bf16[3,512,768]{2,1,0:T(8,128)(2,1)} %param.14) | copy-start | bytes 7077892
  264.1 2.2 copy-start.2
  264.1 6.0 %copy-start.3 = (s32[24]{0:T(128)S(1)}, s32[24]{0:T(128)}, u32[]{:S(2)}) copy-start(s32[24]{0:T(128)} %param.16) | copy-start | bytes 292
  264.1 7.0 %copy-start.1 = (f32[3,96,768]{2,1,0:T(8,128)S(1)}, f32[3,96,768]{2,1,0:T(8,128)}, u32[]{:S(2)}) copy-start(f32[3,96,768]{2,1,0:T(8,128)} %get-tuple-element.17) | copy-start | bytes 2654212

commit v5 on v4

--- a/solution.py
+++ b/solution.py
@@ -490,21 +490,21 @@
         go(remote(wsh.at[p], w.at[p, mine], s_w.at[p, 4], r_w.at[p, mine], beside, mp))
 
     def spread(p):
-        for k in range(1, 4):
+        for k in (3, 2, 1):
             b = x * DP + 2 * lax.rem(z + k, 4) + y
             landed(w.at[p, b], r_w.at[p, b], s_w.at[p, 0], dp, mp)
             go(remote(w.at[p, b], w.at[p, b], s_w.at[p, 3 + 2 * k], r_w.at[p, b], dp, across))
             go(remote(w.at[p, b], w.at[p, b], s_w.at[p, 4 + 2 * k], r_w.at[p, b], beside, mp))
 
     def relay(p):
-        for k in range(4):
+        for n in (0, 3, 2, 1):
+            k = lax.rem(z + n, 4)
             bx, by = (1 - x) * DP + 2 * k + y, x * DP + 2 * k + 1 - y
             landed(w.at[p, bx], r_w.at[p, bx], s_w.at[p, 0], dp, mp)
             landed(w.at[p, by], r_w.at[p, by], s_w.at[p, 0], dp, mp)
-            if k < 2:
-                go(remote(w.at[p, bx], w.at[p, bx], s_w.at[p, 11 + k], r_w.at[p, bx], beside, mp))
-            else:
-                go(remote(w.at[p, by], w.at[p, by], s_w.at[p, 11 + k], r_w.at[p, by], dp, across))
+            b = jnp.where(k < 2, bx, by)
+            there = jnp.where(k < 2, beside, dp), jnp.where(k < 2, mp, across)
+            go(remote(w.at[p, b], w.at[p, b], s_w.at[p, 11 + n], r_w.at[p, b], *there))
 
     def complete(p):
         landed(w.at[p, mine], r_w.at[p, mine], s_w.at[p, 0], dp, mp)
@@ -636,22 +636,20 @@
         return g.at[p, xi, pl.ds(pl.multiple_of(ROWS * d, ROWS), ROWS)]
 
     def first(p):
-        for k in range(4):
+        for n in range(1, 5):
+            k = lax.rem(z + n, 4)
             w[p, k] = block(p, 1 - x, 2 * k + 1 - y)[...].astype(BF)
-            there = (dp, across) if k < 2 else (beside, mp)
+            there = jnp.where(k < 2, dp, beside), jnp.where(k < 2, across, mp)
             go(remote(w.at[p, k], r1.at[p, k], s_a.at[p, k], r_a.at[p, k], *there))
 
     def second(p):
-        for k in range(4):
+        for n in range(1, 5):
+            k = lax.rem(z + n, 4)
             landed(r1.at[p, k], r_a.at[p, k], s_a.at[p, k], dp, mp)
             extra = r1[p, k].astype(F32)
             gx, gy_ = block(p, 1 - x, 2 * k + y)[...], block(p, x, 2 * k + 1 - y)[...]
-            if k < 2:
-                gy_ = gy_ + extra
-            else:
-                gx = gx + extra
-            w[p, 4 + k] = gx.astype(BF)
-            w[p, 8 + k] = gy_.astype(BF)
+            w[p, 4 + k] = (gx + jnp.where(k < 2, 0.0, extra)).astype(BF)
+            w[p, 8 + k] = (gy_ + jnp.where(k < 2, extra, 0.0)).astype(BF)
             go(remote(w.at[p, 4 + k], r2.at[p, 0, k], s_b.at[p, 0, k], r_b.at[p, 0, k], dp, across))
             go(remote(w.at[p, 8 + k], r2.at[p, 1, k], s_b.at[p, 1, k], r_b.at[p, 1, k], beside, mp))
 
@@ -797,14 +795,30 @@
     landed(tea.at[o], r_pair.at[3], s_pair.at[0], dp, mp)
     landed(tea.at[2 + o], r_pair.at[4], s_pair.at[0], dp, mp)
 
+    def teacher_rows(j):
+        pieces = []
+        for m in range(4):
+            low = tea[m, j, 64:96]
+            pieces += [tea[m, j, 0:64], jnp.concatenate([low[:, 0:64], low[:, 64:128]], axis=0)]
+        return jnp.concatenate(pieces, axis=1)
+
+    def pack_out(n, i, value):
+        for q in range(4):
+            a = 64 * q
+            for m in range(4):
+                b = 192 * m
+                yg[n, m, 4 * i + q, 0:64] = value[a : a + 64, b : b + 128]
+                yg[n, m, 4 * i + q, 64:96] = jnp.concatenate(
+                    [value[a : a + 32, b + 128 : b + 192], value[a + 32 : a + 64, b + 128 : b + 192]], axis=1
+                )
+
     def turn_back(i):
-        rows, blocks = chunk(i), pl.ds(i * 4, 4)
+        rows = chunk(i)
         core(1, gy, i).wait()
         out = smid[rows] + (gy[rows] + recv[1, rows] + vec[7:8])
         out_b = out.astype(BF)
-        for m in range(4):
-            yg[0, m, blocks] = out_b[:, 192 * m : 192 * m + 192].reshape(4, 64, 192)
-        target = jnp.concatenate([tea[m, blocks].reshape(R, 192) for m in range(4)], axis=1)
+        pack_out(0, i, out_b)
+        target = jnp.concatenate([teacher_rows(4 * i + q) for q in range(4)], axis=0)
         residual = jnp.where(wide(mask[rows], T) == 0.0, out - target.astype(F32), 0.0)
         add(8, colsum(residual * residual))
         grad_y = residual * factor[0:1, 0:1]
@@ -941,7 +955,7 @@
     first(0)
 
     def in_back(i):
-        rows, blocks = chunk(i), pl.ds(i * 4, 4)
+        rows = chunk(i)
         core(3, x3, i).wait()
         grad_h = x3[rows] + recv[1, rows]
         normed, inverse = normalize_rows(stream(i))
@@ -952,8 +966,7 @@
         add(6, jnp.where(i < 2, total, 0.0))
         add(7, jnp.where(i < 2, 0.0, total))
         out_b = grad_in.astype(BF)
-        for m in range(4):
-            yg[1, m, blocks] = out_b[:, 192 * m : 192 * m + 192].reshape(4, 64, 192)
+        pack_out(1, i, out_b)
 
     each(3, in_back)
     second(0)
@@ -1017,14 +1030,14 @@
         out_shape=(
             jax.ShapeDtypeStruct((3, ROWS, 768), F32),
             jax.ShapeDtypeStruct((16, 24, 128), F32),
-            jax.ShapeDtypeStruct((2, 3, DP, 64, 192), BF),
+            jax.ShapeDtypeStruct((2, 3, DP, 96, 128), BF),
         ),
         in_specs=[pl.BlockSpec(memory_space=pl.ANY)] * 4 + [VM] * 2,
         out_specs=(VM, VM, pl.BlockSpec(memory_space=pl.ANY)),
         scratch_shapes=[
-            vm((3, 2, T, 768), F32), vm((2, 4, 12, 64, 192), BF), vm((16, 768), F32), vm((16, 24, 128), F32),
+            vm((3, 2, T, 768), F32), vm((2, 4, 12, 96, 128), BF), vm((16, 768), F32), vm((16, 24, 128), F32),
             vm((3, 4) + block, BF), vm((3, 2, 4) + block, BF), vm((3, 3) + block, BF),
-            vm((T, 768), BF), vm((4, 12, 64, 192), BF), vm((3, 16) + block, BF),
+            vm((T, 768), BF), vm((4, 12, 96, 128), BF), vm((3, 16) + block, BF),
             vm((4, DP, 48, 128), BF), vm((32, 768), F32), vm((16, 768), F32),
             vm((T, 768), BF), vm((6, T, 128), BF), vm((6, 1024, 128), BF), vm((6, 128, 1024), BF),
             vm((2, R, T), BF), vm((2, T, R), BF), vm((T, 768), BF), vm((2, T, 768), BF),
@@ -1062,7 +1075,11 @@
     )
     micro = jnp.arange(3)[:, None]
     x_blocks = input_stream.reshape(3, DP, 64, width)[micro, send_index]
-    t_blocks = teacher.reshape(3, DP, 64, quarter)[micro, send_index]
+    low = teacher.reshape(3, DP, 64, quarter)
+    low = jnp.concatenate(
+        [low[..., :128], jnp.concatenate([low[:, :, :32, 128:], low[:, :, 32:, 128:]], axis=3)], axis=2
+    )
+    t_blocks = low[micro, send_index]
     half_block = lax.dynamic_index_in_dim(where_block[2].reshape(4, 2), x, 1, keepdims=False)
     their_block = lax.dynamic_index_in_dim(where_block[2].reshape(4, 2), 1 - x, 1, keepdims=False)
     first_block = lax.dynamic_index_in_dim(where_block, x, 0, keepdims=False)
@@ -1094,7 +1111,13 @@
     place_home = jnp.sum(
         jnp.where(send_index[:, None, :] == ranks[None, :, None], ranks[None, None, :], 0), axis=2
     )
-    home = home[:, micro, place_home].reshape(2, 3, seq_len, quarter)
+    home = [home[n][micro, place_home] for n in range(2)]
+    home = [
+        jnp.concatenate(
+            [h[:, :, :64], jnp.concatenate([h[:, :, 64:, :64], h[:, :, 64:, 64:]], axis=2)], axis=3
+        ).reshape(3, seq_len, quarter)
+        for h in home
+    ]
     total = jnp.sum(msgs, axis=0)
     loss = jnp.sum(total[8]) / (valid_count * width)
     rows_a = msgs[:, 6, :24].reshape(16, 24)

time: 275 us -> 265 us (0.964)
  Pallas kernels: 237 us -> 226 us
    pallas_call x1, Pallas kernels: 237 us -> 226 us  [step(): pl.pallas_call(step_kernel, name='step', out_shape=(jax.ShapeDtypeStruct(...]
    unnamed x16 -> x20, local copies, waits for them, and re-layouts: 7.57 us -> 6.37 us
where the time goes in v5:
time: 265 us
  Pallas kernels  226 us (85%)
  local copies, waits for them, and re-layouts  23.2 us (9%)
  other arithmetic  10.6 us (4%)
  between operations  3.4 us (1%)
    pallas_call x1, Pallas kernels, step(): pl.pallas_call(step_kernel, name='step', out_shape=(jax.ShapeDtypeStruct(...  226 us
    unnamed x20, local copies, waits for them, and re-layouts  6.37 us

profile of v5, /device:TPU:24, one launch (start us, length us, event | category | flops | bytes accessed | tf_op | source)
XLA Modules:
  0.0 264.7 jit_solution(17089011956084724790)
XLA Ops:
  0.7 1.4 reduce_sum.61
  2.7 1.3 fusion.35
  4.0 0.7 compare_and_fusion
  4.7 0.7 compare_select_fusion.2
  5.4 0.7 copy.72
  6.1 0.6 broadcast_in_dim.110.factor
  6.7 0.1 tile.23
  6.8 0.8 reshape.143
  7.5 0.2 fusion.7
  7.9 0.2 select_reduce_fusion.1
  8.1 0.2 multiply_reduce_fusion
  8.3 0.7 add_compare_fusion
  9.2 0.2 multiply_reduce_fusion.2
  9.4 0.7 add_compare_fusion.1
  10.4 0.2 select_reduce_fusion
  10.7 0.6 reshape.168
  11.3 0.7 tile.19
  12.1 0.9 copy.70
  13.0 1.0 maximum_bitcast_fusion
  14.0 1.0 copy.71
  15.0 0.6 gather_fusion.2
  15.7 0.7 fusion.22
  16.4 0.6 fusion.14.small
  17.0 1.8 pad_maximum_fusion.wsh
  18.8 1.0 broadcast_in_dim.109.mask
  19.8 0.3 copy.69
  20.3 0.1 maximum_maximum_fusion.2
  20.4 1.6 gather_fusion.1
  21.9 2.2 gather_fusion
  24.1 226.5 %step.1 = (f32[3,96,768]{2,1,0:T(8,128)}, f32[16,24,128]{2,1,0:T(8,128)}, bf16[2,3,8,96,128]{4,3,2,1,0:T(8,128)(2,1)}) custom-call(bf16[3,8,64,768]{3,2,1,0:T(8,128)(2,1)} %bitcast.46, bf16[3,8,96,128]{3,2,1,0:T(8,128)(2,1)} %bitcast.56, bf16[3,96,768]{2,1,0:T(8,128)(2,1)} %pad_maximum_fusion.wsh, bf16[48,128]{1,0:T(8,128)(2,1)} %fusion.14.small, ...), custom_call_target="tpu_custom_call" | custom-call | tf_op jit(solution)/shard_map/step/pallas_call | solution.py:1027
  250.6 1.3 slice_bitcast_fusion
  252.0 0.7 gather_fusion.4
  252.7 0.7 gather_fusion.3
  253.5 0.6 slice_reduce_fusion.1
  254.8 0.6 slice.113
  255.4 0.6 slice.114
  255.9 0.7 constant_dynamic-slice_fusion.1
  256.7 0.6 copy.77
  257.3 1.1 fusion
  258.4 0.7 copy.78
  259.2 0.7 slice_bitcast_fusion.4
  259.9 0.8 slice_bitcast_fusion.2
  260.8 0.1 fusion.33
  260.9 0.2 maximum_maximum_fusion.1
  261.1 1.1 copy.76
  262.2 0.1 fusion.34
  262.3 0.2 maximum_maximum_fusion
  262.5 1.1 copy.75
  (41 shorter events, 1.3 us)
Async XLA Ops:
  0.6 19.2 %copy-start.3 = (bf16[3,512,192]{1,2,0:T(8,128)(2,1)S(1)}, bf16[3,512,192]{1,2,0:T(8,128)(2,1)}, u32[]{:S(2)}) copy-start(bf16[3,512,192]{1,2,0:T(8,128)(2,1)} %param.15) | copy-start | bytes 1769476
  20.2 1.8 copy-start
  250.6 1.4 copy-start.1
  251.9 1.5 copy-start.4
  251.9 5.3 %copy-start.5 = (s32[24]{0:T(128)S(1)}, s32[24]{0:T(128)}, u32[]{:S(2)}) copy-start(s32[24]{0:T(128)} %param.16) | copy-start | bytes 292
  252.0 6.4 %copy-start.2 = (f32[3,96,768]{2,1,0:T(8,128)S(1)}, f32[3,96,768]{2,1,0:T(8,128)}, u32[]{:S(2)}) copy-start(f32[3,96,768]{2,1,0:T(8,128)} %get-tuple-element.17) | copy-start | bytes 2654212

commit v6 on v5

--- a/solution.py
+++ b/solution.py
@@ -1056,89 +1056,179 @@
     )(xs, ts, wsh, small, mask, factor)
 
 
+def send_slot(perm, m, d, dp):
+    index = 0
+    for k in range(DP):
+        v = perm[m, DP * d + k]
+        index = index + jnp.where(lax.shift_right_logical(v, 3) == dp, v & 7, 0)
+    return index
+
+
+def one_hot(timestep):
+    steps = lax.broadcasted_iota(jnp.int32, (1, 1000), 1)
+    return jnp.concatenate(
+        [jnp.where(steps == timestep[n], 1.0, 0.0).astype(F32) for n in range(24)], axis=0
+    )
+
+
+def valid_count(lengths):
+    count = lengths[0]
+    for n in range(1, 24):
+        count = count + lengths[n]
+    return count
+
+
+def pack_kernel(
+    perm, lengths, timestep, xin, tin, table, gains, shifts, qvb, inb, w_qkv, w_out, w_in, w_back,
+    xs, ts, wsh, small, mask, factor,
+    rows, lines, sem,
+):
+    dp, mp, x, c = place()
+    slots = [[send_slot(perm, m, d, dp) for d in range(DP)] for m in range(3)]
+    copies = []
+    for m in range(3):
+        for d in range(DP):
+            source = xin.at[m, pl.ds(pl.multiple_of(64 * slots[m][d], 64), 64)]
+            copies.append(pltpu.make_async_copy(source, xs.at[m, d], sem.at[m, d]))
+            copies[-1].start()
+    for m in range(3):
+        rows[m] = tin[m].T
+    for m in range(3):
+        for d in range(DP):
+            v = rows[m, pl.ds(pl.multiple_of(64 * slots[m][d], 64), 64)]
+            ts[m, d, 0:64] = v[:, 0:128]
+            ts[m, d, 64:96] = jnp.concatenate([v[0:32, 128:192], v[32:64, 128:192]], axis=1)
+    wsh[0, :, 0:576] = w_qkv[...]
+    wsh[0, :, 576:768] = w_out[...].T
+    wsh[1] = w_in[...]
+    wsh[2] = w_back[...]
+
+    lane = lax.broadcasted_iota(jnp.int32, (8, 128), 1)
+    lines[...] = jnp.zeros(lines.shape, F32)
+    lines[0:2, 0:24] = gains[...].astype(F32)
+    lines[2:6, 0:24] = shifts[...].astype(F32)
+    lines[6:30, 0:24] = nt(one_hot(timestep).astype(BF), table[...])
+    spread = jnp.concatenate([inb[...].astype(F32)] * 8, axis=1)
+    lines[32:38] = jnp.where(lax.shift_right_logical(lane[0:6], 4) == dp, spread, 0.0)
+    for j in range(3):
+        both = jnp.concatenate([qvb[j].astype(F32)] * 8, axis=1)
+        both = jnp.where(lax.shift_right_logical(lane[0:2, 0:64], 3) == dp, both, 0.0)
+        lines[40 + j : 41 + j, 0:64] = both[0:1]
+        lines[43 + j : 44 + j, 0:64] = both[1:2]
+    small[...] = lines[...].astype(BF)
+
+    inside = lax.broadcasted_iota(jnp.int32, (64, 128), 0)
+    micro_lengths = lengths[x * DP + dp], lengths[2 * DP + dp]
+    for j in range(16):
+        own = j < 8
+        m = x if own else 2
+        wanted = j if own else 2 * (j % 4) + (x if j < 12 else 1 - x)
+        at = 0
+        for p in range(DP):
+            v = perm[m, DP * dp + p]
+            at = at + jnp.where(lax.shift_right_logical(v, 3) == wanted, p, 0)
+        live = inside + 64 * at < micro_lengths[0 if own else 1]
+        mask[64 * j : 64 * j + 64] = jnp.where(live, 0.0, -1e30).astype(F32)
+    count = jnp.full((8, 128), valid_count(lengths), jnp.int32).astype(F32)
+    factor[...] = (3.0 * DP * 512) / count
+    for copy in copies:
+        copy.wait()
+
+
+def pack(*arguments):
+    vm = pltpu.VMEM
+    smem = pl.BlockSpec(memory_space=pltpu.SMEM)
+    return pl.pallas_call(
+        pack_kernel,
+        name="pack",
+        out_shape=(
+            jax.ShapeDtypeStruct((3, DP, 64, 768), BF),
+            jax.ShapeDtypeStruct((3, DP, 96, 128), BF),
+            jax.ShapeDtypeStruct((3, ROWS, 768), BF),
+            jax.ShapeDtypeStruct((48, 128), BF),
+            jax.ShapeDtypeStruct((1024, 128), F32),
+            jax.ShapeDtypeStruct((8, 128), F32),
+        ),
+        in_specs=[smem] * 3 + [pl.BlockSpec(memory_space=pl.ANY)] + [VM] * 10,
+        out_specs=(VM,) * 6,
+        scratch_shapes=[vm((3, 512, 192), BF), vm((48, 128), F32), pltpu.SemaphoreType.DMA((3, DP))],
+        compiler_params=pltpu.CompilerParams(vmem_limit_bytes=32 * 1024 * 1024),
+    )(*arguments)
+
+
+def unpack_kernel(
+    perm, lengths, timestep, gs, msgs, home,
+    y_out, loss, grad_x, table, gains, shifts, g_qkv, g_qvb, g_out, g_in, g_inb, g_back,
+    rows,
+):
+    dp, mp, x, c = place()
+    for m in range(3):
+        slots = [send_slot(perm, m, d, dp) for d in range(DP)]
+        for n, target in ((0, y_out), (1, grad_x)):
+            for d in range(DP):
+                low = home[n, m, d, 64:96]
+                value = jnp.concatenate(
+                    [home[n, m, d, 0:64], jnp.concatenate([low[:, 0:64], low[:, 64:128]], axis=0)], axis=1
+                )
+                rows[n, pl.ds(pl.multiple_of(64 * slots[d], 64), 64)] = value
+            target[m] = rows[n].T
+    total = msgs[0]
+    for j in range(1, 16):
+        total = total + msgs[j]
+    count = jnp.full((1, 1), valid_count(lengths), jnp.int32).astype(F32)
+    loss[...] = jnp.sum(total[8:9], axis=1, keepdims=True) / (count * 768.0)
+    gains[...] = total[0:2, 0:24]
+    shifts[...] = total[2:6, 0:24]
+    turned = pltpu.roll(total, lax.rem(128 - 8 * dp, 128), 1)
+    for j in range(3):
+        for kind in range(2):
+            at = 9 + 3 * kind + j
+            g_qvb[j, kind : kind + 1] = turned[at : at + 1, 0:8]
+    g_inb[...] = pltpu.roll(total, lax.rem(128 - 16 * dp, 128), 1)[16:22, 0:16]
+    lines = [msgs[j, 6:7] for j in range(16)] + [msgs[d, 7:8] + msgs[DP + d, 7:8] for d in range(DP)]
+    columns = jnp.concatenate(lines, axis=0).T[0:24]
+    chosen = one_hot(timestep)
+    result = columns[:, 0:1] * chosen[0:1]
+    for n in range(1, 24):
+        result = result + columns[:, n : n + 1] * chosen[n : n + 1]
+    table[...] = result
+    g_qkv[...] = gs[0, :, 0:576]
+    g_out[...] = gs[0, :, 576:768].T
+    g_in[...] = gs[1]
+    g_back[...] = gs[2]
+
+
+def unpack(*arguments):
+    smem = pl.BlockSpec(memory_space=pltpu.SMEM)
+    shapes = [
+        ((3, 192, 512), BF), ((1, 1), F32), ((3, 192, 512), BF), ((24, 1000), F32), ((2, 24), F32),
+        ((4, 24), F32), ((96, 576), F32), ((3, 2, 8), F32), ((192, 96), F32), ((96, 768), F32),
+        ((6, 16), F32), ((96, 768), F32),
+    ]
+    return pl.pallas_call(
+        unpack_kernel,
+        name="unpack",
+        out_shape=tuple(jax.ShapeDtypeStruct(*shape) for shape in shapes),
+        in_specs=[smem] * 3 + [VM] * 3,
+        out_specs=(VM,) * 12,
+        scratch_shapes=[pltpu.VMEM((2, 512, 192), BF)],
+        compiler_params=pltpu.CompilerParams(vmem_limit_bytes=32 * 1024 * 1024),
+    )(*arguments)
+
+
 def per_device_compact(
     input_stream, teacher, timestep, lengths, block_perm, table, norm_gains, shifts,
     w_qkv, qv_bias, w_out, w_in, in_bias, w_back,
 ):
-    dp, mp, x, c = place()
-    seq_len, width, quarter = input_stream.shape[1], input_stream.shape[2], teacher.shape[2]
-    valid_count = jnp.sum(lengths).astype(F32)
-    loss_factor = 3 * DP * seq_len / valid_count
-
-    order = block_perm.reshape(3, DP, DP)
-    source, local = order // DP, order % DP
-    send_index = jnp.sum(jnp.where(source == dp, local, 0), axis=2)
-    my_source = lax.dynamic_index_in_dim(source, dp, 1, keepdims=False)
-    ranks = jnp.arange(DP, dtype=jnp.int32)
-    where_block = jnp.sum(
-        jnp.where(my_source[:, None, :] == ranks[None, :, None], ranks[None, None, :], 0), axis=2
-    )
-    micro = jnp.arange(3)[:, None]
-    x_blocks = input_stream.reshape(3, DP, 64, width)[micro, send_index]
-    low = teacher.reshape(3, DP, 64, quarter)
-    low = jnp.concatenate(
-        [low[..., :128], jnp.concatenate([low[:, :, :32, 128:], low[:, :, 32:, 128:]], axis=3)], axis=2
-    )
-    t_blocks = low[micro, send_index]
-    half_block = lax.dynamic_index_in_dim(where_block[2].reshape(4, 2), x, 1, keepdims=False)
-    their_block = lax.dynamic_index_in_dim(where_block[2].reshape(4, 2), 1 - x, 1, keepdims=False)
-    first_block = lax.dynamic_index_in_dim(where_block, x, 0, keepdims=False)
-    length_a = lax.dynamic_index_in_dim(lengths, x * DP + dp, 0, keepdims=False)
-    length_c = lax.dynamic_index_in_dim(lengths, 2 * DP + dp, 0, keepdims=False)
-    inside = jnp.arange(64, dtype=jnp.int32)
-    live_a = ((first_block[:, None] * 64 + inside[None]) < length_a).reshape(512)
-    live_c = ((half_block[:, None] * 64 + inside[None]) < length_c).reshape(256)
-    live_d = ((their_block[:, None] * 64 + inside[None]) < length_c).reshape(256)
-
-    wsh = jnp.stack([jnp.concatenate([w_qkv, w_out.T], axis=1), w_in, w_back.T])
-    chosen = jnp.take(table, timestep, axis=0)
-    rows = jnp.concatenate([norm_gains, shifts, chosen])
-    lanes = jnp.arange(128)
-    spread_in = jnp.where(lanes // 16 == dp, jnp.tile(in_bias, (1, 8)), 0)
-    spread_qv = jnp.where((lanes // 8 == dp)[:64], jnp.tile(qv_bias.reshape(6, 8), (1, 8)), 0)
-    small = jnp.concatenate(
-        [
-            jnp.pad(rows, ((0, 2), (0, 104))),
-            jnp.pad(spread_in, ((0, 2), (0, 0))),
-            jnp.pad(spread_qv, ((0, 2), (0, 64))),
-        ]
-    ).astype(BF)
-    live = jnp.concatenate([live_a, live_c, live_d])
-    mask = jnp.broadcast_to(jnp.where(live, 0.0, -1e30).astype(F32)[:, None], (1024, 128))
-    factor = jnp.full((8, 128), loss_factor, F32)
-    gs, msgs, home = step(x_blocks, t_blocks, wsh, small, mask, factor)
-
-    place_home = jnp.sum(
-        jnp.where(send_index[:, None, :] == ranks[None, :, None], ranks[None, None, :], 0), axis=2
-    )
-    home = [home[n][micro, place_home] for n in range(2)]
-    home = [
-        jnp.concatenate(
-            [h[:, :, :64], jnp.concatenate([h[:, :, 64:, :64], h[:, :, 64:, 64:]], axis=2)], axis=3
-        ).reshape(3, seq_len, quarter)
-        for h in home
-    ]
-    total = jnp.sum(msgs, axis=0)
-    loss = jnp.sum(total[8]) / (valid_count * width)
-    rows_a = msgs[:, 6, :24].reshape(16, 24)
-    rows_c = msgs[:DP, 7, :24] + msgs[DP:, 7, :24]
-    seq_rows = jnp.concatenate([rows_a, rows_c])
-    onehot = (jnp.arange(table.shape[0], dtype=jnp.int32)[:, None] == timestep[None, :]).astype(F32)
-    grad_table = jnp.dot(onehot, seq_rows, precision=lax.Precision.HIGHEST, preferred_element_type=F32)
-    return (
-        home[0],
-        loss,
-        home[1],
-        grad_table,
-        total[0:2, :24],
-        total[2:6, :24],
-        gs[0, :, :576],
-        lax.dynamic_slice(total, (9, 8 * dp), (6, 8)).reshape(2, 3, 8),
-        gs[0, :, 576:].T,
-        gs[1],
-        lax.dynamic_slice(total, (16, 16 * dp), (6, 16)),
-        gs[2].T,
-    )
+    packed = pack(
+        block_perm, lengths, timestep, input_stream, teacher.transpose(0, 2, 1), table.T, norm_gains, shifts,
+        qv_bias.transpose(1, 0, 2), in_bias, w_qkv, w_out, w_in, w_back.T,
+    )
+    outs = list(unpack(block_perm, lengths, timestep, *step(*packed)))
+    outs[0], outs[2] = outs[0].transpose(0, 2, 1), outs[2].transpose(0, 2, 1)
+    outs[1], outs[3] = outs[1].reshape(()), outs[3].T
+    outs[7], outs[11] = outs[7].transpose(1, 0, 2), outs[11].T
+    return tuple(outs)
 
 
 def solution(mesh):

time: 265 us -> 258 us (0.974)
  other arithmetic: 10.6 us -> 0 us
  Pallas kernels: 226 us -> 235 us
  between operations: 3.4 us -> 0.71 us
    unnamed x20 -> x52, local copies, waits for them, and re-layouts: 6.37 us -> 22.1 us
    pallas_call x0 -> x2, Pallas kernels: none -> 8.25 us  [the longest x1 4.94 us: pack(): pl.pallas_call(pack_kernel, name='pack', out_shape=(jax.ShapeDtypeStruct(...]
    gather x5 -> x0, local copies, waits for them, and re-layouts: 5.78 us -> none  [the longest x1 2.17 us: per_device_compact(): x_blocks = input_stream.reshape(3, DP, 64, width)[micro, send_index]]
    another operation x2 -> x0, other arithmetic: 2.8 us -> none  [per_device_compact(): wsh = jnp.stack([jnp.concatenate([w_qkv, w_out.T], axis=1), w_in, w_back.T])]
where the time goes in v6:
time: 258 us; the launch traced here: 257 us
  Pallas kernels  235 us (91%)
  local copies, waits for them, and re-layouts  22.1 us (9%)
    pallas_call x1, Pallas kernels, step(): pl.pallas_call(step_kernel, name='step', out_shape=(jax.ShapeDtypeStruct(...  226 us
    unnamed x52, local copies, waits for them, and re-layouts  22.1 us

profile of v6, /device:TPU:24, one launch (start us, length us, event | category | flops | bytes accessed | tf_op | source)
XLA Modules:
  0.0 257.3 jit_solution(3951753017716672661)
XLA Ops:
  0.6 0.0 copy-start
  0.7 1.7 copy-done
  2.3 0.0 copy-start.4
  2.3 1.1 copy-done.4
  3.4 0.0 copy-start.9
  3.4 0.9 copy-done.9
  4.3 0.0 copy-start.10
  4.3 0.9 copy-done.10
  5.2 0.0 copy-start.11
  5.2 0.9 copy-done.11
  6.1 0.0 copy-start.12
  6.1 0.8 copy-done.12
  6.9 0.0 copy-start.13
  6.9 0.8 copy-done.13
  7.7 0.0 copy-start.15
  7.7 0.7 copy-done.15
  8.4 0.0 copy-start.18
  8.4 0.7 copy-done.18
  9.1 0.0 copy-start.19
  9.1 0.7 copy-done.19
  9.7 0.0 copy-start.21
  9.7 0.7 copy-done.21
  10.4 0.7 copy-done.23
  11.1 0.0 copy-start.24
  11.1 0.7 copy-done.24
  11.7 0.0 copy-start.25
  11.7 0.7 copy-done.25
  12.4 4.9 %pack.1 = (bf16[3,8,64,768]{3,2,1,0:T(8,128)(2,1)S(1)}, bf16[3,8,96,128]{3,2,1,0:T(8,128)(2,1)S(1)}, bf16[3,96,768]{2,1,0:T(8,128)(2,1)S(1)}, bf16[48,128]{1,0:T...) custom-call(s32[3,64]{1,0:T(4,128)S(1)} %copy-done.15, s32[24]{0:T(128)S(1)} %copy-done.19, ...), custom_call_target="tpu_custom_call" | custom-call | tf_op jit(solution)/shard_map/pack/pallas_call | solution.py:1141
  17.3 0.0 copy-start.1
  17.4 1.4 copy-done.1
  18.8 0.0 copy-start.5
  18.8 0.8 copy-done.5
  19.6 0.0 copy-start.6
  19.6 0.8 copy-done.6
  20.4 0.0 copy-start.7
  20.4 0.8 copy-done.7
  21.2 0.0 copy-start.14
  21.2 0.6 copy-done.14
  21.8 0.6 copy-done.17
  22.4 226.3 %step.1 = (f32[3,96,768]{2,1,0:T(8,128)}, f32[16,24,128]{2,1,0:T(8,128)}, bf16[2,3,8,96,128]{4,3,2,1,0:T(8,128)(2,1)}) custom-call(bf16[3,8,64,768]{3,2,1,0:T(8,128)(2,1)} %copy-done.1, bf16[3,8,96,128]{3,2,1,0:T(8,128)(2,1)} %copy-done.5, bf16[3,96,768]{2,1,0:T(8,128)(2,1)} %copy-done.7, bf16[48,128]{1,0:T(8,128)(2,1)} %copy-done.14, ...), custom_call_target="tpu_custom_call" | custom-call | tf_op jit(solution)/shard_map/step/pallas_call | solution.py:1027
  248.6 0.0 copy-start.2
  248.6 1.3 copy-done.2
  249.9 1.2 copy-done.3
  251.1 0.9 copy-done.8
  252.0 0.7 copy-done.16
  252.7 0.7 copy-done.20
  253.3 0.7 copy-done.22
  254.0 3.3 %unpack.1 = (bf16[3,192,512]{2,1,0:T(8,128)(2,1)}, f32[1,1]{1,0:T(1,128)}, bf16[3,192,512]{2,1,0:T(8,128)(2,1)}, f32[24,1000]{1,0:T(8,128)}, f32[2,24]{1,0:T(2,1...) custom-call(s32[3,64]{1,0:T(4,128)S(1)} %copy-done.16, ...), custom_call_target="tpu_custom_call" | custom-call | tf_op jit(solution)/shard_map/unpack/pallas_call | solution.py:1208
  (7 shorter events, 0.0 us)
Async XLA Ops:
  0.6 1.7 copy-start
  2.3 1.1 copy-start.4
  3.4 0.9 copy-start.9
  4.3 0.9 copy-start.10
  5.2 0.9 copy-start.11
  6.1 0.8 copy-start.12
  6.9 0.8 copy-start.13
  7.7 0.7 copy-start.15
  8.4 0.7 copy-start.18
  9.1 0.7 copy-start.19
  9.7 0.7 copy-start.21
  10.4 0.7 copy-start.23
  11.1 0.7 copy-start.24
  11.7 0.7 copy-start.25
  17.3 1.4 copy-start.1
  18.8 0.8 copy-start.5
  19.6 0.8 copy-start.6
  20.4 0.8 copy-start.7
  21.2 0.6 copy-start.14
  21.8 0.6 copy-start.17
  248.6 1.3 copy-start.2
  249.9 1.2 copy-start.3
  251.1 0.9 copy-start.8
  252.0 0.7 copy-start.16
  252.7 0.7 copy-start.20
  253.3 0.7 copy-start.22

commit v7 on v6

--- a/solution.py
+++ b/solution.py
@@ -457,7 +457,7 @@
 def step_kernel(
     xs, ts, wsh, small, mask, factor,
     gs, msgs, back,
-    g, yg, sums, msg, r1, r2, r3,
+    g, yg, sums, msg, s1, r1, r2, r3,
     tok, tea, w, smalls, vecs, vec, nin, q_s, kv, kvt, o_t, att, n2_s, act, gy, gm, gp, x3, recv, tr, dkx, dkr, lse,
     s_core, r_core, s_x, r_x,
     s_tok, r_tok, s_tea, r_tea, s_small, r_small, s_w, r_w, s_pair, r_pair,
@@ -496,8 +496,8 @@
             go(remote(w.at[p, b], w.at[p, b], s_w.at[p, 3 + 2 * k], r_w.at[p, b], dp, across))
             go(remote(w.at[p, b], w.at[p, b], s_w.at[p, 4 + 2 * k], r_w.at[p, b], beside, mp))
 
-    def relay(p):
-        for n in (0, 3, 2, 1):
+    def relay(p, steps=(3, 2, 1)):
+        for n in steps:
             k = lax.rem(z + n, 4)
             bx, by = (1 - x) * DP + 2 * k + y, x * DP + 2 * k + 1 - y
             landed(w.at[p, bx], r_w.at[p, bx], s_w.at[p, 0], dp, mp)
@@ -543,11 +543,15 @@
 
     weights_z(1)
     weights_z(2)
+    for p in range(3):
+        relay(p, (0,))
     spread(0)
 
     for j in range(12):
         landed(tok.at[rows64(j), half], r_tok.at[j], s_tok.at[0], dp, mp)
-    go(remote(tok.at[:, half], tok.at[:, half], s_pair.at[0], r_pair.at[0], dp, other))
+    ours, theirs, whole = pl.ds(512, 256), pl.ds(768, 256), pl.ds(0, T)
+    go(remote(tok.at[ours, half], tok.at[theirs, half], s_x.at[0], r_x.at[0], dp, across))
+    go(remote(tok.at[whole, half], tok.at[whole, half], s_pair.at[0], r_pair.at[0], dp, other))
     for j in range(8):
         for xx in range(2):
             m = 2 * xx + c
@@ -576,7 +580,9 @@
 
     o = 1 - c
     their_half = pl.ds(pl.multiple_of(384 * o, 128), 384)
-    landed(tok.at[:, their_half], r_pair.at[0], s_pair.at[0], dp, mp)
+    landed(tok.at[theirs, half], r_x.at[0], s_x.at[0], dp, mp)
+    go(remote(tok.at[theirs, half], tok.at[theirs, half], s_pair.at[5], r_pair.at[5], dp, other))
+    landed(tok.at[whole, their_half], r_pair.at[0], s_pair.at[0], dp, mp)
     landed(smalls.at[o], r_pair.at[1], s_pair.at[0], dp, mp)
     landed(smalls.at[2 + o], r_pair.at[2], s_pair.at[0], dp, mp)
 
@@ -601,6 +607,7 @@
         for j in range(3):
             pieces += [biases[8 + j : 9 + j, 0:64], blank, biases[11 + j : 12 + j, 0:64]]
         vec[8 + xi : 9 + xi] = jnp.concatenate(pieces + [blank] * 3, axis=1)
+    landed(tok.at[theirs, their_half], r_pair.at[5], s_pair.at[0], dp, mp)
     complete(0)
     smid = g.at[0, 0]
 
@@ -638,9 +645,10 @@
     def first(p):
         for n in range(1, 5):
             k = lax.rem(z + n, 4)
-            w[p, k] = block(p, 1 - x, 2 * k + 1 - y)[...].astype(BF)
-            there = jnp.where(k < 2, dp, beside), jnp.where(k < 2, across, mp)
-            go(remote(w.at[p, k], r1.at[p, k], s_a.at[p, k], r_a.at[p, k], *there))
+            staged = s1 if p == 2 else w.at[p]
+            staged[k] = block(p, 1 - x, 2 * k + 1 - y)[...].astype(BF)
+            there = jnp.where(k < (1 if p == 1 else 2), dp, beside), jnp.where(k < (1 if p == 1 else 2), across, mp)
+            go(remote(staged.at[k], r1.at[p, k], s_a.at[p, k], r_a.at[p, k], *there))
 
     def second(p):
         for n in range(1, 5):
@@ -648,8 +656,8 @@
             landed(r1.at[p, k], r_a.at[p, k], s_a.at[p, k], dp, mp)
             extra = r1[p, k].astype(F32)
             gx, gy_ = block(p, 1 - x, 2 * k + y)[...], block(p, x, 2 * k + 1 - y)[...]
-            w[p, 4 + k] = (gx + jnp.where(k < 2, 0.0, extra)).astype(BF)
-            w[p, 8 + k] = (gy_ + jnp.where(k < 2, extra, 0.0)).astype(BF)
+            w[p, 4 + k] = (gx + jnp.where(k < (1 if p == 1 else 2), 0.0, extra)).astype(BF)
+            w[p, 8 + k] = (gy_ + jnp.where(k < (1 if p == 1 else 2), extra, 0.0)).astype(BF)
             go(remote(w.at[p, 4 + k], r2.at[p, 0, k], s_b.at[p, 0, k], r_b.at[p, 0, k], dp, across))
             go(remote(w.at[p, 8 + k], r2.at[p, 1, k], s_b.at[p, 1, k], r_b.at[p, 1, k], beside, mp))
 
@@ -710,11 +718,15 @@
                 q_s[head, rows] = jnp.concatenate([pr[:, a : a + 64], jnp.zeros((R, 64), BF)], axis=1)
                 kv[head, rows] = pr[:, a + 64 : a + 192]
 
-    project(2)
-    own, theirs = pl.ds(512, 256), pl.ds(768, 256)
-    kv_copy = remote(kv.at[:, own], kv.at[:, theirs], s_x.at[0], r_x.at[0], dp, across)
-    kv_copy.start()
-    each(2, project)
+    each(3, project)
+
+    normed, _ = normalize_rows(stream(3))
+    nb = (normed * vec[2:3] + vec[4:5]).astype(BF)
+    for xi in range(2):
+        pr = (nn(nb, half_of(0, xi, 0, 640)) + vec[8 + xi : 9 + xi, 0:640]).astype(BF)
+        for j in range(3):
+            kv[3 * xi + j, theirs] = pr[:, 192 * j + 64 : 192 * j + 192]
+
     spread(1)
 
     def turn(part):
@@ -744,7 +756,6 @@
         attend(h, 1)
 
     each(6, attend_a)
-    kv_copy.wait()
     relay(1)
     turn(1)
     each(6, lambda h: attend(h, 2))
@@ -812,7 +823,7 @@
                     [value[a : a + 32, b + 128 : b + 192], value[a + 32 : a + 64, b + 128 : b + 192]], axis=1
                 )
 
-    def turn_back(i):
+    def take_loss(i):
         rows = chunk(i)
         core(1, gy, i).wait()
         out = smid[rows] + (gy[rows] + recv[1, rows] + vec[7:8])
@@ -826,6 +837,33 @@
         gb = grad_y.astype(BF)
         gm[rows] = gb
         add(5, colsum(gb.astype(F32)))
+
+    each(3, take_loss)
+
+    def turn_rows(source):
+        def body(i):
+            tr[:, chunk(i)] = source[chunk(i)].T
+
+        each(3, body)
+
+    def weight_grad(p, values):
+        def body(i):
+            for xi in range(2):
+                g[p, xi, chunk(i)] = nn(tr[chunk(i)], values[xi])
+
+        each(3, body)
+
+    turn_rows(gm)
+    weight_grad(2, act)
+    for copy in sent:
+        copy.wait_send()
+    sent.clear()
+    first(2)
+    go_home(0)
+
+    def turn_back(i):
+        rows = chunk(i)
+        gb = gm[rows]
         part = None
         for xi in range(2):
             gpre = (nn(gb, half_of(2, xi, 0, 768)) * g[1, xi, rows]).astype(BF)
@@ -838,25 +876,6 @@
 
     each(3, turn_back)
 
-    def turn_rows(source):
-        def body(i):
-            tr[:, chunk(i)] = source[chunk(i)].T
-
-        each(3, body)
-
-    def weight_grad(p, values):
-        def body(i):
-            for xi in range(2):
-                g[p, xi, chunk(i)] = nn(tr[chunk(i)], values[xi])
-
-        each(3, body)
-
-    turn_rows(gm)
-    weight_grad(2, act)
-    for copy in sent:
-        copy.wait_send()
-    sent.clear()
-    first(2)
     turn_rows(n2_s)
     weight_grad(1, gp)
     first(1)
@@ -881,7 +900,6 @@
                 n2_s[rows, 384 * xi + 128 * j : 384 * xi + 128 * j + 128] = jnp.concatenate([jnp.zeros((R, 64), BF), piece], axis=1)
 
     each(3, mid_back)
-    go_home(0)
 
     def attend_grad(h, block):
         part = block // 2
@@ -1036,8 +1054,8 @@
         out_specs=(VM, VM, pl.BlockSpec(memory_space=pl.ANY)),
         scratch_shapes=[
             vm((3, 2, T, 768), F32), vm((2, 4, 12, 96, 128), BF), vm((16, 768), F32), vm((16, 24, 128), F32),
-            vm((3, 4) + block, BF), vm((3, 2, 4) + block, BF), vm((3, 3) + block, BF),
-            vm((T, 768), BF), vm((4, 12, 96, 128), BF), vm((3, 16) + block, BF),
+            vm((4,) + block, BF), vm((3, 4) + block, BF), vm((3, 2, 4) + block, BF), vm((3, 3) + block, BF),
+            vm((1024, 768), BF), vm((4, 12, 96, 128), BF), vm((3, 16) + block, BF),
             vm((4, DP, 48, 128), BF), vm((32, 768), F32), vm((16, 768), F32),
             vm((T, 768), BF), vm((6, T, 128), BF), vm((6, 1024, 128), BF), vm((6, 128, 1024), BF),
             vm((2, R, T), BF), vm((2, T, R), BF), vm((T, 768), BF), vm((2, T, 768), BF),
@@ -1046,7 +1064,7 @@
             vm((6, 1, T), F32),
             dma((4, 3)), dma((4, 3)), dma((2,)), dma((2,)),
             dma((16,)), dma((12,)), dma((24,)), dma((2, 12)), dma((16,)), dma((16,)),
-            dma((3, 15)), dma((3, 16)), dma((5,)), dma((5,)),
+            dma((3, 15)), dma((3, 16)), dma((6,)), dma((6,)),
             dma((16,)), dma((16,)), dma((2, 24)), dma((2, 3, DP)), dma((3, 4)), dma((3, 4)),
             dma((3, 2, 4)), dma((3, 2, 4)), dma((3, 3)), dma((3, 3)),
         ],
@@ -1152,7 +1170,7 @@
         in_specs=[smem] * 3 + [pl.BlockSpec(memory_space=pl.ANY)] + [VM] * 10,
         out_specs=(VM,) * 6,
         scratch_shapes=[vm((3, 512, 192), BF), vm((48, 128), F32), pltpu.SemaphoreType.DMA((3, DP))],
-        compiler_params=pltpu.CompilerParams(vmem_limit_bytes=32 * 1024 * 1024),
+        compiler_params=pltpu.CompilerParams(vmem_limit_bytes=VMEM_LIMIT),
     )(*arguments)
 
 
@@ -1212,7 +1230,7 @@
         in_specs=[smem] * 3 + [VM] * 3,
         out_specs=(VM,) * 12,
         scratch_shapes=[pltpu.VMEM((2, 512, 192), BF)],
-        compiler_params=pltpu.CompilerParams(vmem_limit_bytes=32 * 1024 * 1024),
+        compiler_params=pltpu.CompilerParams(vmem_limit_bytes=VMEM_LIMIT),
     )(*arguments)
 
 

time: 258 us -> 230 us (0.89)
  local copies, waits for them, and re-layouts: 22.1 us -> 0 us
  Pallas kernels: 235 us -> 229 us
    unnamed x52 -> x0, local copies, waits for them, and re-layouts: 22.1 us -> none
    pallas_call x1, Pallas kernels: 226 us -> 218 us  [step(): pl.pallas_call(step_kernel, name='step', out_shape=(jax.ShapeDtypeStruct(...]
where the time goes in v7:
time: 230 us; the launch traced here: 229 us
  Pallas kernels  229 us (100%)
    pallas_call x1, Pallas kernels, step(): pl.pallas_call(step_kernel, name='step', out_shape=(jax.ShapeDtypeStruct(...  218 us
    pallas_call x1, Pallas kernels, pack(): pl.pallas_call(pack_kernel, name='pack', out_shape=(jax.ShapeDtypeStruct(...  5.91 us

profile of v7, /device:TPU:24, one launch (start us, length us, event | category | flops | bytes accessed | tf_op | source)
XLA Modules:
  0.0 229.4 jit_solution(10334367661050556664)
XLA Ops:
  0.6 5.9 %pack.1 = (bf16[3,8,64,768]{3,2,1,0:T(8,128)(2,1)}, bf16[3,8,96,128]{3,2,1,0:T(8,128)(2,1)}, bf16[3,96,768]{2,1,0:T(8,128)(2,1)}, bf16[48,128]{1,0:T(8,128)(2,1)...) custom-call(s32[3,64]{1,0:T(4,128)} %perm.3, s32[24]{0:T(128)} %lengths.3, s32[24]{0:T(128)} %timestep.3, ...), custom_call_target="tpu_custom_call" | custom-call | tf_op jit(solution)/shard_map/pack/pallas_call | solution.py:1159
  6.6 218.5 %step.1 = (f32[3,96,768]{2,1,0:T(8,128)}, f32[16,24,128]{2,1,0:T(8,128)}, bf16[2,3,8,96,128]{4,3,2,1,0:T(8,128)(2,1)}) custom-call(bf16[3,8,64,768]{3,2,1,0:T(8,128)(2,1)} %get-tuple-element.33.xs, bf16[3,8,96,128]{3,2,1,0:T(8,128)(2,1)} %get-tuple-element.34.ts, bf16[3,96,768]{2,1,0:T(8,128)(2,1)} %get-tuple-element.35.wsh, ...), custom_call_target="tpu_custom_call" | custom-call | tf_op jit(solution)/shard_map/step/pallas_call | solution.py:1045
  225.1 4.2 %unpack.1 = (bf16[3,192,512]{2,1,0:T(8,128)(2,1)}, f32[1,1]{1,0:T(1,128)}, bf16[3,192,512]{2,1,0:T(8,128)(2,1)}, f32[24,1000]{1,0:T(8,128)}, f32[2,24]{1,0:T(2,1...) custom-call(s32[3,64]{1,0:T(4,128)} %perm.3, ...), custom_call_target="tpu_custom_call" | custom-call | tf_op jit(solution)/shard_map/unpack/pallas_call | solution.py:1226

commit v8 on v7

--- a/solution.py
+++ b/solution.py
@@ -987,6 +987,7 @@
         pack_out(1, i, out_b)
 
     each(3, in_back)
+    go_home(1)
     second(0)
 
     msg[...] = jnp.zeros(msg.shape, F32)
@@ -1012,7 +1013,6 @@
             if k or xr:
                 d, xx = lax.rem(dp + k, DP), lax.rem(x + xr, 2)
                 go(remote(msg.at[xx * DP + d], msgs.at[mine], s_msg.at[2 * k + xr], r_msg.at[mine], d, 2 * xx + c))
-    go_home(1)
     third(0)
     last(2)
     last(1)

time: 230 us -> 222 us (0.965)
  Pallas kernels: 229 us -> 221 us
    pallas_call x1, Pallas kernels: 218 us -> 210 us  [step(): pl.pallas_call(step_kernel, name='step', out_shape=(jax.ShapeDtypeStruct(...]
where the time goes in v8:
time: 222 us; the launch traced here: 221 us
  Pallas kernels  221 us (100%)
    pallas_call x1, Pallas kernels, step(): pl.pallas_call(step_kernel, name='step', out_shape=(jax.ShapeDtypeStruct(...  210 us
    pallas_call x1, Pallas kernels, pack(): pl.pallas_call(pack_kernel, name='pack', out_shape=(jax.ShapeDtypeStruct(...  5.91 us

profile of v8, /device:TPU:24, one launch (start us, length us, event | category | flops | bytes accessed | tf_op | source)
XLA Modules:
  0.0 221.3 jit_solution(5466373127096832979)
XLA Ops:
  0.6 5.9 %pack.1 = (bf16[3,8,64,768]{3,2,1,0:T(8,128)(2,1)}, bf16[3,8,96,128]{3,2,1,0:T(8,128)(2,1)}, bf16[3,96,768]{2,1,0:T(8,128)(2,1)}, bf16[48,128]{1,0:T(8,128)(2,1)...) custom-call(s32[3,64]{1,0:T(4,128)} %perm.3, s32[24]{0:T(128)} %lengths.3, s32[24]{0:T(128)} %timestep.3, ...), custom_call_target="tpu_custom_call" | custom-call | tf_op jit(solution)/shard_map/pack/pallas_call | solution.py:1159
  6.6 210.5 %step.1 = (f32[3,96,768]{2,1,0:T(8,128)}, f32[16,24,128]{2,1,0:T(8,128)}, bf16[2,3,8,96,128]{4,3,2,1,0:T(8,128)(2,1)}) custom-call(bf16[3,8,64,768]{3,2,1,0:T(8,128)(2,1)} %get-tuple-element.33.xs, bf16[3,8,96,128]{3,2,1,0:T(8,128)(2,1)} %get-tuple-element.34.ts, bf16[3,96,768]{2,1,0:T(8,128)(2,1)} %get-tuple-element.35.wsh, ...), custom_call_target="tpu_custom_call" | custom-call | tf_op jit(solution)/shard_map/step/pallas_call | solution.py:1045
  217.0 4.2 %unpack.1 = (bf16[3,192,512]{2,1,0:T(8,128)(2,1)}, f32[1,1]{1,0:T(1,128)}, bf16[3,192,512]{2,1,0:T(8,128)(2,1)}, f32[24,1000]{1,0:T(8,128)}, f32[2,24]{1,0:T(2,1...) custom-call(s32[3,64]{1,0:T(4,128)} %perm.3, ...), custom_call_target="tpu_custom_call" | custom-call | tf_op jit(solution)/shard_map/unpack/pallas_call | solution.py:1226

commit v9 on v8

--- a/solution.py
+++ b/solution.py
@@ -900,6 +900,7 @@
                 n2_s[rows, 384 * xi + 128 * j : 384 * xi + 128 * j + 128] = jnp.concatenate([jnp.zeros((R, 64), BF), piece], axis=1)
 
     each(3, mid_back)
+    second(1)
 
     def attend_grad(h, block):
         part = block // 2
@@ -925,7 +926,6 @@
     each(6, grad_c)
     dk_copy = remote(dkx, dkr, s_x.at[1], r_x.at[1], dp, across)
     dk_copy.start()
-    second(1)
     third(2)
     each(6, grad_a)
     turn_rows(gm)

time: 222 us -> 222 us (level)
  no operation moved by 1% of the time
where the time goes in v9:
time: 222 us; the launch traced here: 221 us
  Pallas kernels  221 us (100%)
    pallas_call x1, Pallas kernels, step(): pl.pallas_call(step_kernel, name='step', out_shape=(jax.ShapeDtypeStruct(...  210 us
    pallas_call x1, Pallas kernels, pack(): pl.pallas_call(pack_kernel, name='pack', out_shape=(jax.ShapeDtypeStruct(...  5.91 us

profile of v9, /device:TPU:24, one launch (start us, length us, event | category | flops | bytes accessed | tf_op | source)
XLA Modules:
  0.0 221.3 jit_solution(11308633038694606775)
XLA Ops:
  0.6 5.9 %pack.1 = (bf16[3,8,64,768]{3,2,1,0:T(8,128)(2,1)}, bf16[3,8,96,128]{3,2,1,0:T(8,128)(2,1)}, bf16[3,96,768]{2,1,0:T(8,128)(2,1)}, bf16[48,128]{1,0:T(8,128)(2,1)...) custom-call(s32[3,64]{1,0:T(4,128)} %perm.3, s32[24]{0:T(128)} %lengths.3, s32[24]{0:T(128)} %timestep.3, ...), custom_call_target="tpu_custom_call" | custom-call | tf_op jit(solution)/shard_map/pack/pallas_call | solution.py:1159
  6.6 210.5 %step.1 = (f32[3,96,768]{2,1,0:T(8,128)}, f32[16,24,128]{2,1,0:T(8,128)}, bf16[2,3,8,96,128]{4,3,2,1,0:T(8,128)(2,1)}) custom-call(bf16[3,8,64,768]{3,2,1,0:T(8,128)(2,1)} %get-tuple-element.33.xs, bf16[3,8,96,128]{3,2,1,0:T(8,128)(2,1)} %get-tuple-element.34.ts, bf16[3,96,768]{2,1,0:T(8,128)(2,1)} %get-tuple-element.35.wsh, ...), custom_call_target="tpu_custom_call" | custom-call | tf_op jit(solution)/shard_map/step/pallas_call | solution.py:1045
  217.0 4.2 %unpack.1 = (bf16[3,192,512]{2,1,0:T(8,128)(2,1)}, f32[1,1]{1,0:T(1,128)}, bf16[3,192,512]{2,1,0:T(8,128)(2,1)}, f32[24,1000]{1,0:T(8,128)}, f32[2,24]{1,0:T(2,1...) custom-call(s32[3,64]{1,0:T(4,128)} %perm.3, ...), custom_call_target="tpu_custom_call" | custom-call | tf_op jit(solution)/shard_map/unpack/pallas_call | solution.py:1226
